TPU v7x, 32 devices: a whole 2x2x4 slice. The times are simulated.
32 devices in a mesh: layer: 2 (over x), tile: 16 (over z, y, core).
Axes of the slice: x: 2, y: 2, z: 4, core: 2. Of those that a mesh axis runs over, the one named last changes fastest.
Arguments:
- incident: bfloat16 [2, 32768, 128], P(None, 'tile'), may hold values from -6 to 6
- sources: bfloat16 [2, 2, 32768, 128], P('layer', None, 'tile'), may hold values from -6 to 6
- green_tiles: bfloat16 [2, 192, 2, 256, 256], P('layer', 'tile'), may hold values from -0.1875 to 0.1875
- tile_rows: int32 [2, 192], P('layer', 'tile'), may hold values from 0 to 127, as said below
- tile_cols: int32 [2, 192], P('layer', 'tile'), may hold values from 0 to 7, as said below
- tile_count: int32 [2, 16], P('layer', 'tile'), may hold values from 1 to 12, 144 in all within a row
Outputs:
- traces: bfloat16 [2, 2, 32768, 128], P('layer', None, 'tile')
Inputs may be any that keep to these rules, and one draw needn't show every extreme that they name: `tile_rows`: slot i of a layer belongs to tile device d = i // 12; its row block lies among the row blocks held by devices d - 1, d and d + 1, where row block r is held by device r // 8; in every layer some live slot writes to the first row block of the device on its left and some to the last of the device on its right. `tile_cols`: the column block is counted among the 8 row blocks held by the slot's own device. `tile_count`: A device's live slots are its first ones; each layer group has 9 * 16 live slots in all.
All inputs are finite; a program needn't handle non-finite values.
Results may differ from a plain program's by a relative error of at most 0.0095.
Values may be sent and summed in bfloat16 or wider, within the bound.
No kernel may reach another device: no remote copies, remote signals or barrier semaphores. Data moves between devices by JAX's collectives and lax.ppermute only.
A program may use at most 64 MiB of HBM per device.

v0:
```python
import functools

import jax
import jax.numpy as jnp
from jax import lax
from jax.experimental import pallas as pl
from jax.experimental.pallas import tpu as pltpu
from jax.sharding import PartitionSpec as P


MIB = 1 << 20
VMEM = pl.BlockSpec(memory_space=pltpu.VMEM)
HBM = pl.BlockSpec(memory_space=pltpu.HBM)
SMEM = pl.BlockSpec(memory_space=pltpu.SMEM)
PARTS = 2


def inner_route(devices):
    return [(i, i ^ 1) for i in range(devices)]


def outer_route(wave, devices):
    pairs = [(wave * devices + i, wave * devices + i + 1) for i in range(1, devices - 1, 2)]
    return pairs + [(b, a) for a, b in pairs]


def down_route(depth):
    return [(i, (i + 1) % depth) for i in range(depth)]


def in_hbm(array):
    return pltpu.with_memory_space_constraint(array, pltpu.HBM)


def quarters(shape):
    return lax.rem(lax.broadcasted_iota(jnp.int32, shape, 1), shape[1] // 2) < shape[1] // 4


def pack(block, part):
    rows, width = block.shape
    upper, lower = block[: rows // 2], block[rows // 2 :]
    if part == 0:
        lower = pltpu.roll(lower, width // 4, 1)
    else:
        upper = pltpu.roll(upper, width - width // 4, 1)
    return jnp.where(quarters(upper.shape), upper, lower)


def turn(value):
    half = value.shape[1] // 2
    moved = pltpu.roll(value, half, 1)
    lane = lax.broadcasted_iota(jnp.int32, value.shape, 1)
    return jnp.where(lane < half, -moved, moved)


def accumulate(index_refs, rows_s, cols_s, tiles, pair, sums, blocks, ready):
    tile_size = tiles.shape[-1]
    first = (lax.axis_index("tile") - 1) * blocks
    count = index_refs[2][0, 0]
    for i in range(tiles.shape[0]):
        ready(i)
        live = i < count
        row = jnp.where(live, rows_s[0, i] - first, 3 * blocks)
        column = jnp.where(live, cols_s[0, i], 0)
        rows = pl.ds(pl.multiple_of(column * tile_size, tile_size), tile_size)
        target = pl.ds(pl.multiple_of(row * tile_size, tile_size), tile_size)
        term = jnp.dot(tiles[i, 0], pair[0, rows, :], preferred_element_type=jnp.float32)
        term += jnp.dot(tiles[i, 1], pair[1, rows, :], preferred_element_type=jnp.float32)
        sums[target, :] += term


def side_starts(rows_dev):
    odd = lax.rem(lax.axis_index("tile"), 2)
    return (1 - odd) * 2 * rows_dev, odd * 2 * rows_dev


def read_block(sums, start, r, tile_size):
    return sums[pl.ds(pl.multiple_of(start + r * tile_size, tile_size), tile_size), :]


def front_kernel(front, blocks, *refs):
    index_refs, incident, sources = refs[:3], refs[3], refs[4]
    if front == 0:
        stored, outer_refs, inner_ref, own_refs, tiles = refs[5], refs[6:8], refs[8], refs[9:11], refs[11]
        rest = refs[12:]
    else:
        tiles, outer_refs, inner_ref, own_refs = refs[5], refs[7:9], refs[9], refs[10:12]
        rest = refs[13:]
    rows_s, cols_s, source_v, pair, sums, sems, tile_sems = rest
    slots, tile_size = tiles.shape[0], tiles.shape[-1]
    rows_dev = pair.shape[1]
    packed = rows_dev // 2

    def tile_copy(i):
        return pltpu.make_async_copy(stored.at[0, i], tiles.at[i], tile_sems.at[i])

    active = lax.axis_index("layer") == 0
    copies = [
        pltpu.make_async_copy(index_refs[0], rows_s, sems.at[0]),
        pltpu.make_async_copy(index_refs[1], cols_s, sems.at[1]),
        pltpu.make_async_copy(incident.at[front], pair.at[0], sems.at[2]),
        pltpu.make_async_copy(sources.at[0, front], source_v, sems.at[3]),
    ]

    @pl.when(active)
    def _():
        for copy in copies[:3]:
            copy.start()

    if front == 0:
        for i in range(slots):
            tile_copy(i).start()

    @pl.when(active)
    def _():
        copies[3].start()
        sums[...] = jnp.zeros(sums.shape, jnp.float32)
        for copy in copies[:3]:
            copy.wait()
        for r in range(blocks):
            rows = pl.ds(r * tile_size, tile_size)
            pair[1, rows, :] = turn(pair[0, rows, :].astype(jnp.float32)).astype(jnp.bfloat16)
        ready = (lambda i: tile_copy(i).wait()) if front == 0 else (lambda i: None)
        accumulate(index_refs, rows_s, cols_s, tiles, pair, sums, blocks, ready)
        inner_start, outer_start = side_starts(rows_dev)
        copies[3].wait()
        half = tile_size // 2
        for r in range(blocks):
            own = sums[pl.ds(rows_dev + r * tile_size, tile_size), :]
            own = own + source_v[pl.ds(r * tile_size, tile_size), :].astype(jnp.float32)
            inner = read_block(sums, inner_start, r, tile_size)
            outer = read_block(sums, outer_start, r, tile_size)
            for part in range(PARTS):
                rows = pl.ds(r * half, half)
                own_refs[part][rows, :] = pack(own, part)
                outer_refs[part][rows, :] = pack(outer, part).astype(jnp.bfloat16)
                inner_ref[pl.ds(part * packed + r * half, half), :] = pack(inner, part).astype(jnp.bfloat16)

    if front == 0:

        @pl.when(jnp.logical_not(active))
        def _():
            for i in range(slots):
                tile_copy(i).wait()


def scratch(slots, rows_dev, width, tile_size):
    return [
        pltpu.SMEM((1, slots), jnp.int32),
        pltpu.SMEM((1, slots), jnp.int32),
        pltpu.VMEM((rows_dev, width), jnp.bfloat16),
        pltpu.VMEM((2, rows_dev, width), jnp.bfloat16),
        pltpu.VMEM((3 * rows_dev + tile_size, width), jnp.float32),
        pltpu.SemaphoreType.DMA((4,)),
        pltpu.SemaphoreType.DMA((slots,)),
    ]


def kernel_options(name, flops, moved, limit=20):
    return dict(
        compiler_params=pltpu.CompilerParams(vmem_limit_bytes=limit * MIB),
        cost_estimate=pl.CostEstimate(flops=flops, bytes_accessed=moved, transcendentals=0),
        name=name,
    )


def front_products(front, incident, sources, tiles, index, blocks, through=None):
    rows_dev, width = incident.shape[-2:]
    slots, _, tile_size, _ = tiles.shape[-4:]
    packed = rows_dev // 2
    outer = pltpu.VMEM((packed, width), jnp.bfloat16)
    own = pltpu.VMEM((packed, width), jnp.float32)
    outs = [outer, outer, pltpu.VMEM((rows_dev, width), jnp.bfloat16), own, own]
    args, specs, aliases = [*index, incident, sources, tiles], [HBM, HBM, SMEM, HBM, HBM], {}
    if front == 0:
        specs.append(HBM)
        outs.append(pltpu.VMEM((slots, 2, tile_size, tile_size), jnp.bfloat16))
    else:
        specs += [VMEM, VMEM]
        aliases = {len(args): len(outs)}
        args.append(through)
        outs.append(outer)
    return pl.pallas_call(
        functools.partial(front_kernel, front, blocks),
        out_shape=outs,
        in_specs=specs,
        out_specs=[VMEM] * len(outs),
        scratch_shapes=scratch(slots, rows_dev, width, tile_size),
        input_output_aliases=aliases,
        **kernel_options(f"front_{front}", 10**9, 5 * 10**6),
    )(*args)


def chunk_kernel(wave, front, part, blocks, *refs):
    index_refs, (inbound, sources, tiles, outer_ref, inner_ref, own_ref) = refs[:3], refs[3:9]
    rows_s, cols_s, source_v, pair, sums, sems, _ = refs[9:]
    tile_size = tiles.shape[-1]
    rows_dev, width = pair.shape[1:]
    half = tile_size // 2

    @pl.when(lax.axis_index("layer") == wave)
    def _():
        copies = [
            pltpu.make_async_copy(index_refs[0], rows_s, sems.at[0]),
            pltpu.make_async_copy(index_refs[1], cols_s, sems.at[1]),
            pltpu.make_async_copy(sources.at[0, front], source_v, sems.at[3]),
        ]
        for copy in copies:
            copy.start()
        sums[...] = jnp.zeros(sums.shape, jnp.float32)
        for r in range(blocks):
            upper = inbound[pl.ds(r * half, half), :].astype(jnp.float32)
            lower = pltpu.roll(upper, width - width // 4, 1)
            for j, value in enumerate((upper, lower)):
                rows = pl.ds(r * tile_size + j * half, half)
                pair[0, rows, :] = value.astype(jnp.bfloat16)
                pair[1, rows, :] = turn(value).astype(jnp.bfloat16)
        for copy in copies[:2]:
            copy.wait()
        accumulate(index_refs, rows_s, cols_s, tiles, pair, sums, blocks, lambda i: None)
        inner_start, outer_start = side_starts(rows_dev)
        copies[2].wait()
        for r in range(blocks):
            rows = pl.ds(r * half, half)
            outer_ref[rows, :] = pack(read_block(sums, outer_start, r, tile_size), 0).astype(jnp.bfloat16)
            inner_ref[rows, :] = pack(read_block(sums, inner_start, r, tile_size), 0).astype(jnp.bfloat16)
            source = source_v[pl.ds(r * tile_size, tile_size), :].astype(jnp.float32)
            own = sums[pl.ds(rows_dev + r * tile_size, tile_size), :]
            own_ref[rows, :] = pack(own, 0) + pack(source, part)


def chunk_products(wave, front, part, inbound, sources, tiles, index, blocks):
    rows_dev, width = sources.shape[-2:]
    slots, _, tile_size, _ = tiles.shape
    payload = pltpu.VMEM((rows_dev // 2, width), jnp.bfloat16)
    return pl.pallas_call(
        functools.partial(chunk_kernel, wave, front, part, blocks),
        out_shape=[payload, payload, pltpu.VMEM((rows_dev // 2, width), jnp.float32)],
        in_specs=[HBM, HBM, SMEM, VMEM, HBM, VMEM],
        out_specs=[VMEM] * 3,
        scratch_shapes=scratch(slots, rows_dev, width, tile_size),
        **kernel_options(f"chunk_{wave}_{front}_{part}", 10**9, 5 * 10**6),
    )(*index, inbound, sources, tiles)


def combine_kernel(wave, part, has_through, final, *refs):
    own_ref, inner_ref, outer_ref = refs[:3]
    packed, width = own_ref.shape
    out_ref = refs[-1] if not has_through else refs[-2]
    rows = pl.ds(part * packed if inner_ref.shape[0] > packed else 0, packed)
    total = own_ref[...] + inner_ref[rows, :].astype(jnp.float32) + outer_ref[...].astype(jnp.float32)
    if wave > 0:
        active = lax.axis_index("layer") == wave
        total = jnp.where(active, total, refs[3][...].astype(jnp.float32))
    if not (final and part == PARTS - 1):
        out_ref[...] = total.astype(jnp.bfloat16)
        return
    blocks, half = final
    low, high = refs[4][...].astype(jnp.float32), total
    first = quarters((half, width))
    for r in range(blocks):
        a, b = low[r * half : (r + 1) * half], high[r * half : (r + 1) * half]
        upper = jnp.where(first, a, pltpu.roll(b, width // 4, 1))
        lower = jnp.where(first, pltpu.roll(a, width - width // 4, 1), b)
        out_ref[0, 0, pl.ds(2 * r * half, half), :] = upper.astype(jnp.bfloat16)
        out_ref[0, 0, pl.ds((2 * r + 1) * half, half), :] = lower.astype(jnp.bfloat16)


def combine(wave, front, part, own, inner, outer, earlier=None, through=None, final=None, partner=None, result=None, fronts=0):
    packed, width = own.shape
    args, specs, aliases = [own, inner, outer], [VMEM] * 3, {}
    grid = {}
    if wave > 0:
        args.append(earlier)
        specs.append(VMEM)
    outs, out_specs = [pltpu.VMEM((packed, width), jnp.bfloat16)], [VMEM]
    if through is not None:
        aliases = {len(args): 1}
        args.append(through)
        specs.append(VMEM)
        outs.append(pltpu.VMEM(through.shape, through.dtype))
        out_specs.append(VMEM)
    if final and part == PARTS - 1:
        grid = {"grid": (1,)}
        args.append(partner)
        specs.append(VMEM)
        outs = [jax.ShapeDtypeStruct((1, fronts, 2 * packed, width), jnp.bfloat16)]
        out_specs = [pl.BlockSpec((1, 1, 2 * packed, width), lambda i: (0, front, 0, 0))]
        if result is not None:
            aliases = {len(args): 0}
            args.append(result)
            specs.append(pl.BlockSpec(memory_space=pl.ANY))
    return pl.pallas_call(
        functools.partial(combine_kernel, wave, part, through is not None, final),
        out_shape=outs,
        in_specs=specs,
        out_specs=out_specs,
        input_output_aliases=aliases,
        **grid,
        **kernel_options(f"combine_{wave}_{front}_{part}", 10**6, 10**6, 12),
    )(*args)


def shards(incident, sources, green_tiles, tile_rows, tile_cols, tile_count):
    depth, devices = lax.axis_size("layer"), lax.axis_size("tile")
    layer_route = down_route(depth)
    fronts, rows_dev, _ = incident.shape
    tile_size = green_tiles.shape[-1]
    blocks = rows_dev // tile_size
    index = (in_hbm(tile_rows), in_hbm(tile_cols), tile_count)
    incident, sources, green_tiles = map(in_hbm, (incident, sources, green_tiles))

    def across(payload, wave):
        return lax.ppermute(payload, ("layer", "tile"), outer_route(wave, devices))

    def beside(payload):
        return lax.ppermute(payload, "tile", inner_route(devices))

    def down(payload):
        return lax.ppermute(payload, "layer", layer_route)

    def total(wave, chunk, *args, **kwargs):
        return combine(wave, chunk // PARTS, chunk % PARTS, *args, **kwargs)

    chunks, payloads, held, waiting = [], [], green_tiles, None
    for front in range(fronts):
        made = front_products(front, incident, sources, held, index, blocks, waiting)
        if front == 0:
            held, waiting = made[5], made[1]
            payloads = [None] * PARTS
            outers = [across(made[0], 0), None]
        else:
            if front == 1:
                chunks[1][2] = across(made[5], 0)
            payloads += made[:2]
            outers = [None, None]
            waiting = made[1]
        inner = beside(made[2])
        chunks += [[made[3 + part], inner, outers[part]] for part in range(PARTS)]
    if fronts == 1:
        chunks[1][2] = across(waiting, 0)
    passed, leaving = [], []
    for c in range(len(chunks)):
        behind = c + PARTS
        through = payloads[behind] if behind < len(chunks) else None
        made = total(0, c, *chunks[c], through=through)
        if through is not None:
            chunks[behind][2] = across(made[1], 0)
        leaving.append(made[0])
        if depth > 1:
            passed.append(down(made[0]))
    for wave in range(1, depth):
        final = wave == depth - 1
        chunks = []
        for c, inbound in enumerate(passed):
            outer, inner, own = chunk_products(
                wave, c // PARTS, c % PARTS, inbound, sources, held, index, blocks
            )
            chunks.append((own, beside(inner), across(outer, wave)))
        if final:
            break
        leaving = [total(wave, c, *chunk, leaving[c])[0] for c, chunk in enumerate(chunks)]
        passed = [down(chunk) for chunk in leaving]
    result = partner = None
    for c, chunk in enumerate(chunks):
        (out,) = total(
            depth - 1, c, *chunk, leaving[c],
            final=(blocks, tile_size // 2), partner=partner, result=result, fronts=fronts,
        )
        partner = out
        if c % PARTS == PARTS - 1:
            result = out
    return result


def solution(mesh):
    return jax.shard_map(
        shards,
        mesh=mesh,
        in_specs=(
            P(None, "tile", None),
            P("layer", None, "tile", None),
            P("layer", "tile", None, None, None),
            P("layer", "tile"),
            P("layer", "tile"),
            P("layer", "tile"),
        ),
        out_specs=P("layer", None, "tile", None),
        check_vma=False,
    )
```

profile of v0, /device:TPU:19, one launch (start us, length us, event | category | flops | bytes accessed | tf_op | source)
XLA Modules:
  0.0 72.3 jit_solution(4114137006411069060)
XLA Ops:
  0.7 2.0 %front_0.1 = (bf16[1024,128]{1,0:T(8,128)(2,1)S(1)}, bf16[1024,128]{1,0:T(8,128)(2,1)S(1)}, bf16[2048,128]{1,0:T(8,128)(2,1)S(1)}, f32[1024,128]{1,0:T(8,128)S(1...) custom-call(s32[1,12]{1,0:T(1,128)} %refs_0_.11, s32[1,12]{1,0:T(1,128)} %refs_1_.11, ...), custom_call_target="tpu_custom_call" | custom-call | flops 1000000000 | bytes 5000000 | tf_op jit(solution)/shard_map/front_0/pallas_call | solution.py:183
  2.6 0.7 %collective-permute-start.1 = (bf16[2048,128]{1,0:T(8,128)(2,1)S(1)}, bf16[2048,128]{1,0:T(8,128)(2,1)S(1)}, u32[]{:S(2)}, u32[]{:S(2)}) collective-permute-start(bf16[2048,128]{1,0:T(8,128)(2,1)S(1)} %get-tuple-element.38), channel_id=1, source_target_pairs={{0,1},{1,0},{2,3},{3,2},{4,5},{5,4},{6,7},{7,6},{8,9},{9,8},{10,11... | collective-permute-start | bytes 1572872 | tf_op jit(solution)/shard_map/ppermute | solution.py:317
  3.4 0.7 collective-permute-start.7
  4.0 0.2 front_1.1
  4.2 0.7 collective-permute-start.2
  4.9 0.1 collective-permute-start
  5.0 0.1 combine_0_0_0.1
  5.1 0.7 collective-permute-start.8
  5.8 0.1 combine_0_0_1.1
  5.9 0.7 collective-permute-start.3
  6.6 22.1 %collective-permute-start.15 = (bf16[1024,128]{1,0:T(8,128)(2,1)S(1)}, bf16[1024,128]{1,0:T(8,128)(2,1)S(1)}, u32[]{:S(2)}, u32[]{:S(2)}) collective-permute-start(bf16[1024,128]{1,0:T(8,128)(2,1)S(1)} %get-tuple-element.57.refs_3_), channel_id=1, source_target_pairs={{0,16},{16,0},{1,17},{17,1},{2,18},{18,2},{3,19},{19,3},{4,20},{20... | collective-permute-start | bytes 786440 | tf_op jit(solution)/shard_map/ppermute | solution.py:320
  28.7 0.1 combine_0_1_0.1.refs_3_
  28.8 3.8 %collective-permute-start.9 = (bf16[1024,128]{1,0:T(8,128)(2,1)S(1)}, bf16[1024,128]{1,0:T(8,128)(2,1)S(1)}, u32[]{:S(2)}, u32[]{:S(2)}) collective-permute-start(bf16[1024,128]{1,0:T(8,128)(2,1)S(1)} %combine_0_1_0.1.refs_3_), channel_id=1, source_target_pairs={{0,16},{16,0},{1,17},{17,1},{2,18},{18,2},{3,19},{19,3},{4,20},{20... | collective-permute-start | bytes 786440 | tf_op jit(solution)/shard_map/ppermute | solution.py:320
  32.6 0.1 combine_0_1_1.1.refs_3_
  32.7 2.7 %collective-permute-start.4 = (bf16[1024,128]{1,0:T(8,128)(2,1)S(1)}, bf16[1024,128]{1,0:T(8,128)(2,1)S(1)}, u32[]{:S(2)}, u32[]{:S(2)}) collective-permute-start(bf16[1024,128]{1,0:T(8,128)(2,1)S(1)} %combine_0_1_1.1.refs_3_), channel_id=1, source_target_pairs={{0,16},{16,0},{1,17},{17,1},{2,18},{18,2},{3,19},{19,3},{4,20},{20... | collective-permute-start | bytes 786440 | tf_op jit(solution)/shard_map/ppermute | solution.py:320
  35.5 2.5 %chunk_1_0_0.1 = (bf16[1024,128]{1,0:T(8,128)(2,1)S(1)}, bf16[1024,128]{1,0:T(8,128)(2,1)S(1)}, f32[1024,128]{1,0:T(8,128)S(1)}) custom-call(s32[1,12]{1,0:T(1,128)} %refs_0_.11, s32[1,12]{1,0:T(1,128)} %refs_1_.11, s32[1,1]{1,0:T(1,128)S(6)} %copy.15.refs_2_, bf16[1024,128]{1,0:T(8,128)(2,1)S(1)} %collective-permute-done.15.refs_3_, ...), custom_call_target="tpu_custom_call" | custom-call | flops 1000000000 | bytes 5000000 | tf_op jit(solution)/shard_map/chunk_1_0_0/pallas_call | solution.py:236
  38.0 4.2 %collective-permute-start.17 = (bf16[1024,128]{1,0:T(8,128)(2,1)S(1)}, bf16[1024,128]{1,0:T(8,128)(2,1)S(1)}, u32[]{:S(2)}, u32[]{:S(2)}) collective-permute-start(bf16[1024,128]{1,0:T(8,128)(2,1)S(1)} %get-tuple-element.60), channel_id=1, source_target_pairs={{17,18},{19,20},{21,22},{23,24},{25,26},{27,28},{29,30},{18,17},{2... | collective-permute-start | bytes 786440 | tf_op jit(solution)/shard_map/ppermute | solution.py:314
  42.3 2.5 %chunk_1_0_1.1 = (bf16[1024,128]{1,0:T(8,128)(2,1)S(1)}, bf16[1024,128]{1,0:T(8,128)(2,1)S(1)}, f32[1024,128]{1,0:T(8,128)S(1)}) custom-call(s32[1,12]{1,0:T(1,128)} %refs_0_.11, s32[1,12]{1,0:T(1,128)} %refs_1_.11, s32[1,1]{1,0:T(1,128)S(6)} %copy.15.refs_2_, bf16[1024,128]{1,0:T(8,128)(2,1)S(1)} %collective-permute-done.12.refs_3_, ...), custom_call_target="tpu_custom_call" | custom-call | flops 1000000000 | bytes 5000000 | tf_op jit(solution)/shard_map/chunk_1_0_1/pallas_call | solution.py:236
  44.8 0.4 collective-permute-start.13
  45.2 1.4 %collective-permute-done.9.refs_3_ = bf16[1024,128]{1,0:T(8,128)(2,1)S(1)} collective-permute-done((bf16[1024,128]{1,0:T(8,128)(2,1)S(1)}, bf16[1024,128]{1,0:T(8,128)(2,1)S(1)}, u32[]{:S(2)}, u32[]{:S(2)}) %collective-permute-start.9) | collective-permute-done | bytes 262176 | tf_op jit(solution)/shard_map/ppermute | solution.py:320
  46.6 3.2 %collective-permute-start.14 = (bf16[1024,128]{1,0:T(8,128)(2,1)S(1)}, bf16[1024,128]{1,0:T(8,128)(2,1)S(1)}, u32[]{:S(2)}, u32[]{:S(2)}) collective-permute-start(bf16[1024,128]{1,0:T(8,128)(2,1)S(1)} %get-tuple-element.56), channel_id=1, source_target_pairs={{17,18},{19,20},{21,22},{23,24},{25,26},{27,28},{29,30},{18,17},{2... | collective-permute-start | bytes 786440 | tf_op jit(solution)/shard_map/ppermute | solution.py:314
  49.8 2.5 %chunk_1_1_0.1 = (bf16[1024,128]{1,0:T(8,128)(2,1)S(1)}, bf16[1024,128]{1,0:T(8,128)(2,1)S(1)}, f32[1024,128]{1,0:T(8,128)S(1)}) custom-call(s32[1,12]{1,0:T(1,128)} %refs_0_.11, s32[1,12]{1,0:T(1,128)} %refs_1_.11, s32[1,1]{1,0:T(1,128)S(6)} %copy.15.refs_2_, bf16[1024,128]{1,0:T(8,128)(2,1)S(1)} %collective-permute-done.9.refs_3_, ...), custom_call_target="tpu_custom_call" | custom-call | flops 1000000000 | bytes 5000000 | tf_op jit(solution)/shard_map/chunk_1_1_0/pallas_call | solution.py:236
  52.4 2.7 %chunk_1_1_1.1 = (bf16[1024,128]{1,0:T(8,128)(2,1)S(1)}, bf16[1024,128]{1,0:T(8,128)(2,1)S(1)}, f32[1024,128]{1,0:T(8,128)S(1)}) custom-call(s32[1,12]{1,0:T(1,128)} %refs_0_.11, s32[1,12]{1,0:T(1,128)} %refs_1_.11, s32[1,1]{1,0:T(1,128)S(6)} %copy.15.refs_2_, bf16[1024,128]{1,0:T(8,128)(2,1)S(1)} %collective-permute-done.4.refs_3_, ...), custom_call_target="tpu_custom_call" | custom-call | flops 1000000000 | bytes 5000000 | tf_op jit(solution)/shard_map/chunk_1_1_1/pallas_call | solution.py:236
  55.1 2.4 %collective-permute-start.11 = (bf16[1024,128]{1,0:T(8,128)(2,1)S(1)}, bf16[1024,128]{1,0:T(8,128)(2,1)S(1)}, u32[]{:S(2)}, u32[]{:S(2)}) collective-permute-start(bf16[1024,128]{1,0:T(8,128)(2,1)S(1)} %get-tuple-element.52), channel_id=1, source_target_pairs={{17,18},{19,20},{21,22},{23,24},{25,26},{27,28},{29,30},{18,17},{2... | collective-permute-start | bytes 786440 | tf_op jit(solution)/shard_map/ppermute | solution.py:314
  57.5 0.2 collective-permute-start.5
  57.7 3.0 %collective-permute-start.6 = (bf16[1024,128]{1,0:T(8,128)(2,1)S(1)}, bf16[1024,128]{1,0:T(8,128)(2,1)S(1)}, u32[]{:S(2)}, u32[]{:S(2)}) collective-permute-start(bf16[1024,128]{1,0:T(8,128)(2,1)S(1)} %get-tuple-element.44), channel_id=1, source_target_pairs={{17,18},{19,20},{21,22},{23,24},{25,26},{27,28},{29,30},{18,17},{2... | collective-permute-start | bytes 786440 | tf_op jit(solution)/shard_map/ppermute | solution.py:314
  60.8 0.1 combine_1_0_0.1.refs_4_
  60.9 1.1 %combine_1_0_1.1.refs_5_ = bf16[1,2,2048,128]{3,2,1,0:T(8,128)(2,1)} custom-call(f32[1024,128]{1,0:T(8,128)S(1)} %get-tuple-element.54.refs_0_, bf16[1024,128]{1,0:T(8,128)(2,1)S(1)} %collective-permute-done.13.refs_1_, bf16[1024,128]{1,0:T(8,128)(2,1)S(1)} %collective-permute-done.14.refs_2_, bf16[1024,128]{1,0:T(8,128)(2,1)S(1)} %get-tuple-element.53.refs_3_, ...), custom_call_target="tpu_custom_call" | custom-call | flops 1000000 | bytes 1000000 | tf_op jit(solution)/shard_map/combine_1_0_1/pallas_call | solution.py:293
  62.0 6.4 %collective-permute-done.11.refs_2_ = bf16[1024,128]{1,0:T(8,128)(2,1)S(1)} collective-permute-done((bf16[1024,128]{1,0:T(8,128)(2,1)S(1)}, bf16[1024,128]{1,0:T(8,128)(2,1)S(1)}, u32[]{:S(2)}, u32[]{:S(2)}) %collective-permute-start.11) | collective-permute-done | bytes 262176 | tf_op jit(solution)/shard_map/ppermute | solution.py:314
  68.4 0.1 combine_1_1_0.1.refs_4_
  68.5 2.7 %collective-permute-done.6.refs_2_ = bf16[1024,128]{1,0:T(8,128)(2,1)S(1)} collective-permute-done((bf16[1024,128]{1,0:T(8,128)(2,1)S(1)}, bf16[1024,128]{1,0:T(8,128)(2,1)S(1)}, u32[]{:S(2)}, u32[]{:S(2)}) %collective-permute-start.6) | collective-permute-done | bytes 262176 | tf_op jit(solution)/shard_map/ppermute | solution.py:314
  71.2 1.1 %combine_1_1_1.1 = bf16[1,2,2048,128]{3,2,1,0:T(8,128)(2,1)} custom-call(f32[1024,128]{1,0:T(8,128)S(1)} %get-tuple-element.42.refs_0_, bf16[1024,128]{1,0:T(8,128)(2,1)S(1)} %collective-permute-done.5.refs_1_, bf16[1024,128]{1,0:T(8,128)(2,1)S(1)} %collective-permute-done.6.refs_2_, ...), custom_call_target="tpu_custom_call", output_to_operand_aliasing={{}: (5, {})} | custom-call | flops 1000000 | bytes 1000000 | tf_op jit(solution)/shard_map/combine_1_1_1/pallas_call | solution.py:293
  (18 shorter events, 0.3 us)
Async XLA Ops:
  2.6 2.4 %collective-permute-start.1 = (bf16[2048,128]{1,0:T(8,128)(2,1)S(1)}, bf16[2048,128]{1,0:T(8,128)(2,1)S(1)}, u32[]{:S(2)}, u32[]{:S(2)}) collective-permute-start(bf16[2048,128]{1,0:T(8,128)(2,1)S(1)} %get-tuple-element.38), channel_id=1, source_target_pairs={{0,1},{1,0},{2,3},{3,2},{4,5},{5,4},{6,7},{7,6},{8,9},{9,8},{10,11... | collective-permute-start | bytes 1572872 | tf_op jit(solution)/shard_map/ppermute | solution.py:317
  3.4 1.6 %collective-permute-start.7 = (bf16[1024,128]{1,0:T(8,128)(2,1)S(1)}, bf16[1024,128]{1,0:T(8,128)(2,1)S(1)}, u32[]{:S(2)}, u32[]{:S(2)}) collective-permute-start(bf16[1024,128]{1,0:T(8,128)(2,1)S(1)} %get-tuple-element.47), channel_id=1, source_target_pairs={{1,2},{3,4},{5,6},{7,8},{9,10},{11,12},{13,14},{2,1},{4,3},{6,5},{... | collective-permute-start | bytes 786440 | tf_op jit(solution)/shard_map/ppermute | solution.py:314
  4.2 1.6 %collective-permute-start.2 = (bf16[1024,128]{1,0:T(8,128)(2,1)S(1)}, bf16[1024,128]{1,0:T(8,128)(2,1)S(1)}, u32[]{:S(2)}, u32[]{:S(2)}) collective-permute-start(bf16[1024,128]{1,0:T(8,128)(2,1)S(1)} %get-tuple-element.39), channel_id=1, source_target_pairs={{1,2},{3,4},{5,6},{7,8},{9,10},{11,12},{13,14},{2,1},{4,3},{6,5},{... | collective-permute-start | bytes 786440 | tf_op jit(solution)/shard_map/ppermute | solution.py:314
  4.9 23.8 %collective-permute-start = (bf16[2048,128]{1,0:T(8,128)(2,1)S(1)}, bf16[2048,128]{1,0:T(8,128)(2,1)S(1)}, u32[]{:S(2)}, u32[]{:S(2)}) collective-permute-start(bf16[2048,128]{1,0:T(8,128)(2,1)S(1)} %get-tuple-element.36), channel_id=1, source_target_pairs={{0,1},{1,0},{2,3},{3,2},{4,5},{5,4},{6,7},{7,6},{8,9},{9,8},{10,11... | collective-permute-start | bytes 1572872 | tf_op jit(solution)/shard_map/ppermute | solution.py:317
  5.1 23.6 %collective-permute-start.8 = (bf16[1024,128]{1,0:T(8,128)(2,1)S(1)}, bf16[1024,128]{1,0:T(8,128)(2,1)S(1)}, u32[]{:S(2)}, u32[]{:S(2)}) collective-permute-start(bf16[1024,128]{1,0:T(8,128)(2,1)S(1)} %get-tuple-element.49), channel_id=1, source_target_pairs={{1,2},{3,4},{5,6},{7,8},{9,10},{11,12},{13,14},{2,1},{4,3},{6,5},{... | collective-permute-start | bytes 786440 | tf_op jit(solution)/shard_map/ppermute | solution.py:314
  5.9 26.7 %collective-permute-start.3 = (bf16[1024,128]{1,0:T(8,128)(2,1)S(1)}, bf16[1024,128]{1,0:T(8,128)(2,1)S(1)}, u32[]{:S(2)}, u32[]{:S(2)}) collective-permute-start(bf16[1024,128]{1,0:T(8,128)(2,1)S(1)} %get-tuple-element.41), channel_id=1, source_target_pairs={{1,2},{3,4},{5,6},{7,8},{9,10},{11,12},{13,14},{2,1},{4,3},{6,5},{... | collective-permute-start | bytes 786440 | tf_op jit(solution)/shard_map/ppermute | solution.py:314
  6.6 28.9 %collective-permute-start.15 = (bf16[1024,128]{1,0:T(8,128)(2,1)S(1)}, bf16[1024,128]{1,0:T(8,128)(2,1)S(1)}, u32[]{:S(2)}, u32[]{:S(2)}) collective-permute-start(bf16[1024,128]{1,0:T(8,128)(2,1)S(1)} %get-tuple-element.57.refs_3_), channel_id=1, source_target_pairs={{0,16},{16,0},{1,17},{17,1},{2,18},{18,2},{3,19},{19,3},{4,20},{20... | collective-permute-start | bytes 786440 | tf_op jit(solution)/shard_map/ppermute | solution.py:320
  28.6 13.7 %collective-permute-start.12 = (bf16[1024,128]{1,0:T(8,128)(2,1)S(1)}, bf16[1024,128]{1,0:T(8,128)(2,1)S(1)}, u32[]{:S(2)}, u32[]{:S(2)}) collective-permute-start(bf16[1024,128]{1,0:T(8,128)(2,1)S(1)} %get-tuple-element.53.refs_3_), channel_id=1, source_target_pairs={{0,16},{16,0},{1,17},{17,1},{2,18},{18,2},{3,19},{19,3},{4,20},{20... | collective-permute-start | bytes 786440 | tf_op jit(solution)/shard_map/ppermute | solution.py:320
  28.8 17.8 %collective-permute-start.9 = (bf16[1024,128]{1,0:T(8,128)(2,1)S(1)}, bf16[1024,128]{1,0:T(8,128)(2,1)S(1)}, u32[]{:S(2)}, u32[]{:S(2)}) collective-permute-start(bf16[1024,128]{1,0:T(8,128)(2,1)S(1)} %combine_0_1_0.1.refs_3_), channel_id=1, source_target_pairs={{0,16},{16,0},{1,17},{17,1},{2,18},{18,2},{3,19},{19,3},{4,20},{20... | collective-permute-start | bytes 786440 | tf_op jit(solution)/shard_map/ppermute | solution.py:320
  32.7 19.6 %collective-permute-start.4 = (bf16[1024,128]{1,0:T(8,128)(2,1)S(1)}, bf16[1024,128]{1,0:T(8,128)(2,1)S(1)}, u32[]{:S(2)}, u32[]{:S(2)}) collective-permute-start(bf16[1024,128]{1,0:T(8,128)(2,1)S(1)} %combine_0_1_1.1.refs_3_), channel_id=1, source_target_pairs={{0,16},{16,0},{1,17},{17,1},{2,18},{18,2},{3,19},{19,3},{4,20},{20... | collective-permute-start | bytes 786440 | tf_op jit(solution)/shard_map/ppermute | solution.py:320
  38.0 17.1 %collective-permute-start.16 = (bf16[1024,128]{1,0:T(8,128)(2,1)S(1)}, bf16[1024,128]{1,0:T(8,128)(2,1)S(1)}, u32[]{:S(2)}, u32[]{:S(2)}) collective-permute-start(bf16[1024,128]{1,0:T(8,128)(2,1)S(1)} %get-tuple-element.59), channel_id=1, source_target_pairs={{0,1},{1,0},{2,3},{3,2},{4,5},{5,4},{6,7},{7,6},{8,9},{9,8},{10,11... | collective-permute-start | bytes 786440 | tf_op jit(solution)/shard_map/ppermute | solution.py:317
  38.0 19.4 %collective-permute-start.17 = (bf16[1024,128]{1,0:T(8,128)(2,1)S(1)}, bf16[1024,128]{1,0:T(8,128)(2,1)S(1)}, u32[]{:S(2)}, u32[]{:S(2)}) collective-permute-start(bf16[1024,128]{1,0:T(8,128)(2,1)S(1)} %get-tuple-element.60), channel_id=1, source_target_pairs={{17,18},{19,20},{21,22},{23,24},{25,26},{27,28},{29,30},{18,17},{2... | collective-permute-start | bytes 786440 | tf_op jit(solution)/shard_map/ppermute | solution.py:314
  44.8 12.9 %collective-permute-start.13 = (bf16[1024,128]{1,0:T(8,128)(2,1)S(1)}, bf16[1024,128]{1,0:T(8,128)(2,1)S(1)}, u32[]{:S(2)}, u32[]{:S(2)}) collective-permute-start(bf16[1024,128]{1,0:T(8,128)(2,1)S(1)} %get-tuple-element.55), channel_id=1, source_target_pairs={{0,1},{1,0},{2,3},{3,2},{4,5},{5,4},{6,7},{7,6},{8,9},{9,8},{10,11... | collective-permute-start | bytes 786440 | tf_op jit(solution)/shard_map/ppermute | solution.py:317
  46.6 14.3 %collective-permute-start.14 = (bf16[1024,128]{1,0:T(8,128)(2,1)S(1)}, bf16[1024,128]{1,0:T(8,128)(2,1)S(1)}, u32[]{:S(2)}, u32[]{:S(2)}) collective-permute-start(bf16[1024,128]{1,0:T(8,128)(2,1)S(1)} %get-tuple-element.56), channel_id=1, source_target_pairs={{17,18},{19,20},{21,22},{23,24},{25,26},{27,28},{29,30},{18,17},{2... | collective-permute-start | bytes 786440 | tf_op jit(solution)/shard_map/ppermute | solution.py:314
  52.3 9.6 %collective-permute-start.10 = (bf16[1024,128]{1,0:T(8,128)(2,1)S(1)}, bf16[1024,128]{1,0:T(8,128)(2,1)S(1)}, u32[]{:S(2)}, u32[]{:S(2)}) collective-permute-start(bf16[1024,128]{1,0:T(8,128)(2,1)S(1)} %get-tuple-element.51), channel_id=1, source_target_pairs={{0,1},{1,0},{2,3},{3,2},{4,5},{5,4},{6,7},{7,6},{8,9},{9,8},{10,11... | collective-permute-start | bytes 786440 | tf_op jit(solution)/shard_map/ppermute | solution.py:317
  55.1 13.3 %collective-permute-start.11 = (bf16[1024,128]{1,0:T(8,128)(2,1)S(1)}, bf16[1024,128]{1,0:T(8,128)(2,1)S(1)}, u32[]{:S(2)}, u32[]{:S(2)}) collective-permute-start(bf16[1024,128]{1,0:T(8,128)(2,1)S(1)} %get-tuple-element.52), channel_id=1, source_target_pairs={{17,18},{19,20},{21,22},{23,24},{25,26},{27,28},{29,30},{18,17},{2... | collective-permute-start | bytes 786440 | tf_op jit(solution)/shard_map/ppermute | solution.py:314
  57.5 11.1 %collective-permute-start.5 = (bf16[1024,128]{1,0:T(8,128)(2,1)S(1)}, bf16[1024,128]{1,0:T(8,128)(2,1)S(1)}, u32[]{:S(2)}, u32[]{:S(2)}) collective-permute-start(bf16[1024,128]{1,0:T(8,128)(2,1)S(1)} %get-tuple-element.43), channel_id=1, source_target_pairs={{0,1},{1,0},{2,3},{3,2},{4,5},{5,4},{6,7},{7,6},{8,9},{9,8},{10,11... | collective-permute-start | bytes 786440 | tf_op jit(solution)/shard_map/ppermute | solution.py:317
  57.7 13.5 %collective-permute-start.6 = (bf16[1024,128]{1,0:T(8,128)(2,1)S(1)}, bf16[1024,128]{1,0:T(8,128)(2,1)S(1)}, u32[]{:S(2)}, u32[]{:S(2)}) collective-permute-start(bf16[1024,128]{1,0:T(8,128)(2,1)S(1)} %get-tuple-element.44), channel_id=1, source_target_pairs={{17,18},{19,20},{21,22},{23,24},{25,26},{27,28},{29,30},{18,17},{2... | collective-permute-start | bytes 786440 | tf_op jit(solution)/shard_map/ppermute | solution.py:314
where the time goes:
time: 72.6 us; the launch traced here: 72.3 us
  starting transfers between devices  45.9 us (63%)
  Pallas kernels  14.9 us (21%)
  waiting for transfers between devices  10.6 us (15%)
  between operations  0.88 us (1%)
    ppermute x4, starting transfers between devices, down(): return lax.ppermute(payload, 'layer', layer_route)  28.7 us
    ppermute x8, starting transfers between devices, across(): return lax.ppermute(payload, ('layer', 'tile'), outer_route(wave, devices))  15.5 us
    pallas_call x4, Pallas kernels, chunk_products(): pl.pallas_call(functools.partial(chunk_kernel, wave, front, part, blocks)...  10.1 us
    ppermute x8, waiting for transfers between devices, across(): return lax.ppermute(payload, ('layer', 'tile'), outer_route(wave, devices))  9.13 us
    pallas_call x8, Pallas kernels, combine(): pl.pallas_call(functools.partial(combine_kernel, wave, part, through is n...  2.67 us
    pallas_call x2, Pallas kernels, front_products(): pl.pallas_call(functools.partial(front_kernel, front, blocks), out_shape=...  2.13 us
    ppermute x6, starting transfers between devices, beside(): return lax.ppermute(payload, 'tile', inner_route(devices))  1.66 us
    ppermute x4, waiting for transfers between devices, down(): return lax.ppermute(payload, 'layer', layer_route)  1.47 us
  transfers between devices with their start and end apart: 18, of which 4 were waited for; matrix products, arithmetic and copies ran while one was open for 0% of the time, Pallas kernels for 16%

commit v1 on v0

--- a/solution.py
+++ b/solution.py
@@ -107,19 +107,22 @@
         for copy in copies[:3]:
             copy.start()
 
-    if front == 0:
-        for i in range(slots):
-            tile_copy(i).start()
+    early = slots // 4 if front == 0 else 0
+    for i in range(early):
+        tile_copy(i).start()
 
     @pl.when(active)
     def _():
-        copies[3].start()
         sums[...] = jnp.zeros(sums.shape, jnp.float32)
         for copy in copies[:3]:
             copy.wait()
+        if front == 0:
+            for i in range(early, slots):
+                tile_copy(i).start()
         for r in range(blocks):
             rows = pl.ds(r * tile_size, tile_size)
             pair[1, rows, :] = turn(pair[0, rows, :].astype(jnp.float32)).astype(jnp.bfloat16)
+        copies[3].start()
         ready = (lambda i: tile_copy(i).wait()) if front == 0 else (lambda i: None)
         accumulate(index_refs, rows_s, cols_s, tiles, pair, sums, blocks, ready)
         inner_start, outer_start = side_starts(rows_dev)
@@ -140,6 +143,8 @@
 
         @pl.when(jnp.logical_not(active))
         def _():
+            for i in range(early, slots):
+                tile_copy(i).start()
             for i in range(slots):
                 tile_copy(i).wait()
 
@@ -191,9 +196,40 @@
     )(*args)
 
 
-def chunk_kernel(wave, front, part, blocks, *refs):
-    index_refs, (inbound, sources, tiles, outer_ref, inner_ref, own_ref) = refs[:3], refs[3:9]
-    rows_s, cols_s, source_v, pair, sums, sems, _ = refs[9:]
+def prepare_kernel(wave, front, part, sources, sums, source_v, sem):
+    rows_dev, width = source_v.shape
+
+    @pl.when(lax.axis_index("layer") == wave)
+    def _():
+        copy = pltpu.make_async_copy(sources.at[0, front], source_v, sem)
+        copy.start()
+        side = jnp.zeros((rows_dev, width), jnp.float32)
+        sums[pl.ds(0, rows_dev), :] = side
+        sums[pl.ds(2 * rows_dev, sums.shape[0] - 2 * rows_dev), :] = jnp.zeros(
+            (sums.shape[0] - 2 * rows_dev, width), jnp.float32
+        )
+        copy.wait()
+        source = source_v[...].astype(jnp.float32)
+        if part > 0:
+            source = pltpu.roll(source, width - width // 4, 1)
+        sums[pl.ds(rows_dev, rows_dev), :] = source
+
+
+def prepare(wave, front, part, sources, tile_size):
+    rows_dev, width = sources.shape[-2:]
+    return pl.pallas_call(
+        functools.partial(prepare_kernel, wave, front, part),
+        out_shape=pltpu.VMEM((3 * rows_dev + tile_size, width), jnp.float32),
+        in_specs=[HBM],
+        out_specs=VMEM,
+        scratch_shapes=[pltpu.VMEM((rows_dev, width), jnp.bfloat16), pltpu.SemaphoreType.DMA(())],
+        **kernel_options(f"prepare_{wave}_{front}_{part}", 10**6, 10**6, 4),
+    )(sources)
+
+
+def chunk_kernel(wave, blocks, *refs):
+    index_refs, (inbound, tiles, _, outer_ref, inner_ref, own_ref, sums) = refs[:3], refs[3:10]
+    rows_s, cols_s, pair, sems = refs[10:]
     tile_size = tiles.shape[-1]
     rows_dev, width = pair.shape[1:]
     half = tile_size // 2
@@ -203,11 +239,9 @@
         copies = [
             pltpu.make_async_copy(index_refs[0], rows_s, sems.at[0]),
             pltpu.make_async_copy(index_refs[1], cols_s, sems.at[1]),
-            pltpu.make_async_copy(sources.at[0, front], source_v, sems.at[3]),
         ]
         for copy in copies:
             copy.start()
-        sums[...] = jnp.zeros(sums.shape, jnp.float32)
         for r in range(blocks):
             upper = inbound[pl.ds(r * half, half), :].astype(jnp.float32)
             lower = pltpu.roll(upper, width - width // 4, 1)
@@ -215,32 +249,35 @@
                 rows = pl.ds(r * tile_size + j * half, half)
                 pair[0, rows, :] = value.astype(jnp.bfloat16)
                 pair[1, rows, :] = turn(value).astype(jnp.bfloat16)
-        for copy in copies[:2]:
+        for copy in copies:
             copy.wait()
         accumulate(index_refs, rows_s, cols_s, tiles, pair, sums, blocks, lambda i: None)
         inner_start, outer_start = side_starts(rows_dev)
-        copies[2].wait()
         for r in range(blocks):
             rows = pl.ds(r * half, half)
             outer_ref[rows, :] = pack(read_block(sums, outer_start, r, tile_size), 0).astype(jnp.bfloat16)
             inner_ref[rows, :] = pack(read_block(sums, inner_start, r, tile_size), 0).astype(jnp.bfloat16)
-            source = source_v[pl.ds(r * tile_size, tile_size), :].astype(jnp.float32)
-            own = sums[pl.ds(rows_dev + r * tile_size, tile_size), :]
-            own_ref[rows, :] = pack(own, 0) + pack(source, part)
-
-
-def chunk_products(wave, front, part, inbound, sources, tiles, index, blocks):
-    rows_dev, width = sources.shape[-2:]
+            own_ref[rows, :] = pack(read_block(sums, rows_dev, r, tile_size), 0)
+
+
+def chunk_products(wave, front, part, inbound, tiles, sums, index, blocks):
     slots, _, tile_size, _ = tiles.shape
+    rows_dev, width = blocks * tile_size, sums.shape[-1]
     payload = pltpu.VMEM((rows_dev // 2, width), jnp.bfloat16)
     return pl.pallas_call(
-        functools.partial(chunk_kernel, wave, front, part, blocks),
-        out_shape=[payload, payload, pltpu.VMEM((rows_dev // 2, width), jnp.float32)],
-        in_specs=[HBM, HBM, SMEM, VMEM, HBM, VMEM],
-        out_specs=[VMEM] * 3,
-        scratch_shapes=scratch(slots, rows_dev, width, tile_size),
-        **kernel_options(f"chunk_{wave}_{front}_{part}", 10**9, 5 * 10**6),
-    )(*index, inbound, sources, tiles)
+        functools.partial(chunk_kernel, wave, blocks),
+        out_shape=[payload, payload, pltpu.VMEM((rows_dev // 2, width), jnp.float32), pltpu.VMEM(sums.shape, sums.dtype)],
+        in_specs=[HBM, HBM, SMEM, VMEM, VMEM, VMEM],
+        out_specs=[VMEM] * 4,
+        scratch_shapes=[
+            pltpu.SMEM((1, slots), jnp.int32),
+            pltpu.SMEM((1, slots), jnp.int32),
+            pltpu.VMEM((2, rows_dev, width), jnp.bfloat16),
+            pltpu.SemaphoreType.DMA((2,)),
+        ],
+        input_output_aliases={5: 3},
+        **kernel_options(f"chunk_{wave}_{front}_{part}", 10**9, 5 * 10**6, 4),
+    )(*index, inbound, tiles, sums)
 
 
 def combine_kernel(wave, part, has_through, final, *refs):
@@ -353,8 +390,9 @@
         final = wave == depth - 1
         chunks = []
         for c, inbound in enumerate(passed):
-            outer, inner, own = chunk_products(
-                wave, c // PARTS, c % PARTS, inbound, sources, held, index, blocks
+            sums = prepare(wave, c // PARTS, c % PARTS, sources, tile_size)
+            outer, inner, own, _ = chunk_products(
+                wave, c // PARTS, c % PARTS, inbound, held, sums, index, blocks
             )
             chunks.append((own, beside(inner), across(outer, wave)))
         if final:

time: 72.6 us -> 76 us (1.047)
  the two profiles are of different devices: /device:TPU:19 before, /device:TPU:22 now
where the time goes in v1:
time: 76 us; the launch traced here: 75.6 us
  starting transfers between devices  41.5 us (55%)
  Pallas kernels  18.9 us (25%)
  waiting for transfers between devices  14.2 us (19%)
  between operations  0.95 us (1%)
    ppermute x4, starting transfers between devices, down(): return lax.ppermute(payload, 'layer', layer_route)  25.4 us
    ppermute x8, starting transfers between devices, across(): return lax.ppermute(payload, ('layer', 'tile'), outer_route(wave, devices))  13.4 us
    pallas_call x4, Pallas kernels, chunk_products(): pl.pallas_call(functools.partial(chunk_kernel, wave, blocks), out_shape=[...  9.32 us
    ppermute x8, waiting for transfers between devices, across(): return lax.ppermute(payload, ('layer', 'tile'), outer_route(wave, devices))  9.13 us
    ppermute x4, waiting for transfers between devices, down(): return lax.ppermute(payload, 'layer', layer_route)  5.06 us
    pallas_call x4, Pallas kernels, prepare(): pl.pallas_call(functools.partial(prepare_kernel, wave, front, part), out_...  4.78 us
    ppermute x6, starting transfers between devices, beside(): return lax.ppermute(payload, 'tile', inner_route(devices))  2.74 us
    pallas_call x8, Pallas kernels, combine(): pl.pallas_call(functools.partial(combine_kernel, wave, part, through is n...  2.67 us
  transfers between devices with their start and end apart: 18, of which 4 were waited for; matrix products, arithmetic and copies ran while one was open for 0% of the time, Pallas kernels for 21%

profile of v1, /device:TPU:22, one launch (start us, length us, event | category | flops | bytes accessed | tf_op | source)
XLA Modules:
  0.0 75.6 jit_solution(16716402041136508229)
XLA Ops:
  0.7 2.0 %front_0.1 = (bf16[1024,128]{1,0:T(8,128)(2,1)S(1)}, bf16[1024,128]{1,0:T(8,128)(2,1)S(1)}, bf16[2048,128]{1,0:T(8,128)(2,1)S(1)}, f32[1024,128]{1,0:T(8,128)S(1...) custom-call(s32[1,12]{1,0:T(1,128)} %refs_0_.11, s32[1,12]{1,0:T(1,128)} %refs_1_.11, ...), custom_call_target="tpu_custom_call" | custom-call | flops 1000000000 | bytes 5000000 | tf_op jit(solution)/shard_map/front_0/pallas_call | solution.py:188
  2.7 0.7 collective-permute-start.7
  3.4 0.2 front_1.1
  3.6 0.7 collective-permute-start.2
  4.2 0.6 collective-permute-start
  4.9 0.7 collective-permute-start.8
  5.6 0.1 combine_0_0_1.1
  5.7 0.7 collective-permute-start.3
  6.4 22.6 %collective-permute-start.12 = (bf16[1024,128]{1,0:T(8,128)(2,1)S(1)}, bf16[1024,128]{1,0:T(8,128)(2,1)S(1)}, u32[]{:S(2)}, u32[]{:S(2)}) collective-permute-start(bf16[1024,128]{1,0:T(8,128)(2,1)S(1)} %get-tuple-element.53.refs_3_), channel_id=1, source_target_pairs={{0,16},{16,0},{1,17},{17,1},{2,18},{18,2},{3,19},{19,3},{4,20},{20... | collective-permute-start | bytes 786440 | tf_op jit(solution)/shard_map/ppermute | solution.py:357
  29.1 1.3 %prepare_1_0_1.1.refs_5_ = f32[6400,128]{1,0:T(8,128)S(1)} custom-call(bf16[1,2,2048,128]{3,2,1,0:T(8,128)(2,1)} %sources.7), custom_call_target="tpu_custom_call" | custom-call | flops 1000000 | bytes 1000000 | tf_op jit(solution)/shard_map/prepare_1_0_1/pallas_call | solution.py:220
  30.3 1.1 %prepare_1_0_0.1.refs_5_ = f32[6400,128]{1,0:T(8,128)S(1)} custom-call(bf16[1,2,2048,128]{3,2,1,0:T(8,128)(2,1)} %sources.7), custom_call_target="tpu_custom_call" | custom-call | flops 1000000 | bytes 1000000 | tf_op jit(solution)/shard_map/prepare_1_0_0/pallas_call | solution.py:220
  31.8 2.6 %collective-permute-start.4 = (bf16[1024,128]{1,0:T(8,128)(2,1)S(1)}, bf16[1024,128]{1,0:T(8,128)(2,1)S(1)}, u32[]{:S(2)}, u32[]{:S(2)}) collective-permute-start(bf16[1024,128]{1,0:T(8,128)(2,1)S(1)} %combine_0_1_1.1.refs_3_), channel_id=1, source_target_pairs={{0,16},{16,0},{1,17},{17,1},{2,18},{18,2},{3,19},{19,3},{4,20},{20... | collective-permute-start | bytes 786440 | tf_op jit(solution)/shard_map/ppermute | solution.py:357
  34.4 1.8 %collective-permute-done.12.refs_3_ = bf16[1024,128]{1,0:T(8,128)(2,1)S(1)} collective-permute-done((bf16[1024,128]{1,0:T(8,128)(2,1)S(1)}, bf16[1024,128]{1,0:T(8,128)(2,1)S(1)}, u32[]{:S(2)}, u32[]{:S(2)}) %collective-permute-start.12) | collective-permute-done | bytes 262176 | tf_op jit(solution)/shard_map/ppermute | solution.py:357
  36.2 2.3 %chunk_1_0_1.1 = (bf16[1024,128]{1,0:T(8,128)(2,1)S(1)}, bf16[1024,128]{1,0:T(8,128)(2,1)S(1)}, f32[1024,128]{1,0:T(8,128)S(1)}, f32[6400,128]{1,0:T(8,128)S(1)}) custom-call(s32[1,12]{1,0:T(1,128)} %refs_0_.11, s32[1,12]{1,0:T(1,128)} %refs_1_.11, s32[1,1]{1,0:T(1,128)S(6)} %copy.23.refs_2_, ...), custom_call_target="tpu_custom_call", output_to_operand_aliasing={{3}: (5, {})} | custom-call | flops 1000000000 | bytes 5000000 | tf_op jit(solution)/shard_map/chunk_1_0_1/pallas_call | solution.py:267
  38.5 3.2 %collective-permute-done.15.refs_3_ = bf16[1024,128]{1,0:T(8,128)(2,1)S(1)} collective-permute-done((bf16[1024,128]{1,0:T(8,128)(2,1)S(1)}, bf16[1024,128]{1,0:T(8,128)(2,1)S(1)}, u32[]{:S(2)}, u32[]{:S(2)}) %collective-permute-start.15) | collective-permute-done | bytes 262176 | tf_op jit(solution)/shard_map/ppermute | solution.py:357
  41.8 2.3 %chunk_1_0_0.1 = (bf16[1024,128]{1,0:T(8,128)(2,1)S(1)}, bf16[1024,128]{1,0:T(8,128)(2,1)S(1)}, f32[1024,128]{1,0:T(8,128)S(1)}, f32[6400,128]{1,0:T(8,128)S(1)}) custom-call(s32[1,12]{1,0:T(1,128)} %refs_0_.11, s32[1,12]{1,0:T(1,128)} %refs_1_.11, s32[1,1]{1,0:T(1,128)S(6)} %copy.23.refs_2_, ...), custom_call_target="tpu_custom_call", output_to_operand_aliasing={{3}: (5, {})} | custom-call | flops 1000000000 | bytes 5000000 | tf_op jit(solution)/shard_map/chunk_1_0_0/pallas_call | solution.py:267
  44.1 1.9 %collective-permute-start.17 = (bf16[1024,128]{1,0:T(8,128)(2,1)S(1)}, bf16[1024,128]{1,0:T(8,128)(2,1)S(1)}, u32[]{:S(2)}, u32[]{:S(2)}) collective-permute-start(bf16[1024,128]{1,0:T(8,128)(2,1)S(1)} %get-tuple-element.60), channel_id=1, source_target_pairs={{17,18},{19,20},{21,22},{23,24},{25,26},{27,28},{29,30},{18,17},{2... | collective-permute-start | bytes 786440 | tf_op jit(solution)/shard_map/ppermute | solution.py:351
  46.1 1.3 %prepare_1_1_1.1.refs_5_ = f32[6400,128]{1,0:T(8,128)S(1)} custom-call(bf16[1,2,2048,128]{3,2,1,0:T(8,128)(2,1)} %sources.7), custom_call_target="tpu_custom_call" | custom-call | flops 1000000 | bytes 1000000 | tf_op jit(solution)/shard_map/prepare_1_1_1/pallas_call | solution.py:220
  47.3 1.1 %prepare_1_1_0.1.refs_5_ = f32[6400,128]{1,0:T(8,128)S(1)} custom-call(bf16[1,2,2048,128]{3,2,1,0:T(8,128)(2,1)} %sources.7), custom_call_target="tpu_custom_call" | custom-call | flops 1000000 | bytes 1000000 | tf_op jit(solution)/shard_map/prepare_1_1_0/pallas_call | solution.py:220
  48.5 3.6 %collective-permute-start.14 = (bf16[1024,128]{1,0:T(8,128)(2,1)S(1)}, bf16[1024,128]{1,0:T(8,128)(2,1)S(1)}, u32[]{:S(2)}, u32[]{:S(2)}) collective-permute-start(bf16[1024,128]{1,0:T(8,128)(2,1)S(1)} %get-tuple-element.56), channel_id=1, source_target_pairs={{17,18},{19,20},{21,22},{23,24},{25,26},{27,28},{29,30},{18,17},{2... | collective-permute-start | bytes 786440 | tf_op jit(solution)/shard_map/ppermute | solution.py:351
  52.1 2.5 %chunk_1_1_0.1 = (bf16[1024,128]{1,0:T(8,128)(2,1)S(1)}, bf16[1024,128]{1,0:T(8,128)(2,1)S(1)}, f32[1024,128]{1,0:T(8,128)S(1)}, f32[6400,128]{1,0:T(8,128)S(1)}) custom-call(s32[1,12]{1,0:T(1,128)} %refs_0_.11, s32[1,12]{1,0:T(1,128)} %refs_1_.11, s32[1,1]{1,0:T(1,128)S(6)} %copy.23.refs_2_, ...), custom_call_target="tpu_custom_call", output_to_operand_aliasing={{3}: (5, {})} | custom-call | flops 1000000000 | bytes 5000000 | tf_op jit(solution)/shard_map/chunk_1_1_0/pallas_call | solution.py:267
  54.6 1.4 %collective-permute-start.10 = (bf16[1024,128]{1,0:T(8,128)(2,1)S(1)}, bf16[1024,128]{1,0:T(8,128)(2,1)S(1)}, u32[]{:S(2)}, u32[]{:S(2)}) collective-permute-start(bf16[1024,128]{1,0:T(8,128)(2,1)S(1)} %get-tuple-element.51), channel_id=1, source_target_pairs={{0,1},{1,0},{2,3},{3,2},{4,5},{5,4},{6,7},{7,6},{8,9},{9,8},{10,11... | collective-permute-start | bytes 786440 | tf_op jit(solution)/shard_map/ppermute | solution.py:354
  56.1 2.3 %chunk_1_1_1.1 = (bf16[1024,128]{1,0:T(8,128)(2,1)S(1)}, bf16[1024,128]{1,0:T(8,128)(2,1)S(1)}, f32[1024,128]{1,0:T(8,128)S(1)}, f32[6400,128]{1,0:T(8,128)S(1)}) custom-call(s32[1,12]{1,0:T(1,128)} %refs_0_.11, s32[1,12]{1,0:T(1,128)} %refs_1_.11, s32[1,1]{1,0:T(1,128)S(6)} %copy.23.refs_2_, ...), custom_call_target="tpu_custom_call", output_to_operand_aliasing={{3}: (5, {})} | custom-call | flops 1000000000 | bytes 5000000 | tf_op jit(solution)/shard_map/chunk_1_1_1/pallas_call | solution.py:267
  58.4 1.9 %collective-permute-start.11 = (bf16[1024,128]{1,0:T(8,128)(2,1)S(1)}, bf16[1024,128]{1,0:T(8,128)(2,1)S(1)}, u32[]{:S(2)}, u32[]{:S(2)}) collective-permute-start(bf16[1024,128]{1,0:T(8,128)(2,1)S(1)} %get-tuple-element.52), channel_id=1, source_target_pairs={{17,18},{19,20},{21,22},{23,24},{25,26},{27,28},{29,30},{18,17},{2... | collective-permute-start | bytes 786440 | tf_op jit(solution)/shard_map/ppermute | solution.py:351
  60.3 0.5 collective-permute-start.5
  60.9 3.2 %collective-permute-start.6 = (bf16[1024,128]{1,0:T(8,128)(2,1)S(1)}, bf16[1024,128]{1,0:T(8,128)(2,1)S(1)}, u32[]{:S(2)}, u32[]{:S(2)}) collective-permute-start(bf16[1024,128]{1,0:T(8,128)(2,1)S(1)} %get-tuple-element.44), channel_id=1, source_target_pairs={{17,18},{19,20},{21,22},{23,24},{25,26},{27,28},{29,30},{18,17},{2... | collective-permute-start | bytes 786440 | tf_op jit(solution)/shard_map/ppermute | solution.py:351
  64.1 0.1 combine_1_0_0.1.refs_4_
  64.2 1.1 %combine_1_0_1.1.refs_5_ = bf16[1,2,2048,128]{3,2,1,0:T(8,128)(2,1)} custom-call(f32[1024,128]{1,0:T(8,128)S(1)} %get-tuple-element.54.refs_0_, bf16[1024,128]{1,0:T(8,128)(2,1)S(1)} %collective-permute-done.13.refs_1_, bf16[1024,128]{1,0:T(8,128)(2,1)S(1)} %collective-permute-done.14.refs_2_, bf16[1024,128]{1,0:T(8,128)(2,1)S(1)} %get-tuple-element.53.refs_3_, ...), custom_call_target="tpu_custom_call" | custom-call | flops 1000000 | bytes 1000000 | tf_op jit(solution)/shard_map/combine_1_0_1/pallas_call | solution.py:330
  65.3 6.4 %collective-permute-done.11.refs_2_ = bf16[1024,128]{1,0:T(8,128)(2,1)S(1)} collective-permute-done((bf16[1024,128]{1,0:T(8,128)(2,1)S(1)}, bf16[1024,128]{1,0:T(8,128)(2,1)S(1)}, u32[]{:S(2)}, u32[]{:S(2)}) %collective-permute-start.11) | collective-permute-done | bytes 262176 | tf_op jit(solution)/shard_map/ppermute | solution.py:351
  71.7 0.1 combine_1_1_0.1.refs_4_
  71.8 2.7 %collective-permute-done.6.refs_2_ = bf16[1024,128]{1,0:T(8,128)(2,1)S(1)} collective-permute-done((bf16[1024,128]{1,0:T(8,128)(2,1)S(1)}, bf16[1024,128]{1,0:T(8,128)(2,1)S(1)}, u32[]{:S(2)}, u32[]{:S(2)}) %collective-permute-start.6) | collective-permute-done | bytes 262176 | tf_op jit(solution)/shard_map/ppermute | solution.py:351
  74.5 1.1 %combine_1_1_1.1 = bf16[1,2,2048,128]{3,2,1,0:T(8,128)(2,1)} custom-call(f32[1024,128]{1,0:T(8,128)S(1)} %get-tuple-element.42.refs_0_, bf16[1024,128]{1,0:T(8,128)(2,1)S(1)} %collective-permute-done.5.refs_1_, bf16[1024,128]{1,0:T(8,128)(2,1)S(1)} %collective-permute-done.6.refs_2_, ...), custom_call_target="tpu_custom_call", output_to_operand_aliasing={{}: (5, {})} | custom-call | flops 1000000 | bytes 1000000 | tf_op jit(solution)/shard_map/combine_1_1_1/pallas_call | solution.py:330
  (22 shorter events, 0.6 us)
Async XLA Ops:
  2.6 2.2 %collective-permute-start.1 = (bf16[2048,128]{1,0:T(8,128)(2,1)S(1)}, bf16[2048,128]{1,0:T(8,128)(2,1)S(1)}, u32[]{:S(2)}, u32[]{:S(2)}) collective-permute-start(bf16[2048,128]{1,0:T(8,128)(2,1)S(1)} %get-tuple-element.38), channel_id=1, source_target_pairs={{0,1},{1,0},{2,3},{3,2},{4,5},{5,4},{6,7},{7,6},{8,9},{9,8},{10,11... | collective-permute-start | bytes 1572872 | tf_op jit(solution)/shard_map/ppermute | solution.py:354
  2.7 2.1 %collective-permute-start.7 = (bf16[1024,128]{1,0:T(8,128)(2,1)S(1)}, bf16[1024,128]{1,0:T(8,128)(2,1)S(1)}, u32[]{:S(2)}, u32[]{:S(2)}) collective-permute-start(bf16[1024,128]{1,0:T(8,128)(2,1)S(1)} %get-tuple-element.47), channel_id=1, source_target_pairs={{1,2},{3,4},{5,6},{7,8},{9,10},{11,12},{13,14},{2,1},{4,3},{6,5},{... | collective-permute-start | bytes 786440 | tf_op jit(solution)/shard_map/ppermute | solution.py:351
  3.6 2.0 %collective-permute-start.2 = (bf16[1024,128]{1,0:T(8,128)(2,1)S(1)}, bf16[1024,128]{1,0:T(8,128)(2,1)S(1)}, u32[]{:S(2)}, u32[]{:S(2)}) collective-permute-start(bf16[1024,128]{1,0:T(8,128)(2,1)S(1)} %get-tuple-element.39), channel_id=1, source_target_pairs={{1,2},{3,4},{5,6},{7,8},{9,10},{11,12},{13,14},{2,1},{4,3},{6,5},{... | collective-permute-start | bytes 786440 | tf_op jit(solution)/shard_map/ppermute | solution.py:351
  4.2 27.2 %collective-permute-start = (bf16[2048,128]{1,0:T(8,128)(2,1)S(1)}, bf16[2048,128]{1,0:T(8,128)(2,1)S(1)}, u32[]{:S(2)}, u32[]{:S(2)}) collective-permute-start(bf16[2048,128]{1,0:T(8,128)(2,1)S(1)} %get-tuple-element.36), channel_id=1, source_target_pairs={{0,1},{1,0},{2,3},{3,2},{4,5},{5,4},{6,7},{7,6},{8,9},{9,8},{10,11... | collective-permute-start | bytes 1572872 | tf_op jit(solution)/shard_map/ppermute | solution.py:354
  4.9 26.6 %collective-permute-start.8 = (bf16[1024,128]{1,0:T(8,128)(2,1)S(1)}, bf16[1024,128]{1,0:T(8,128)(2,1)S(1)}, u32[]{:S(2)}, u32[]{:S(2)}) collective-permute-start(bf16[1024,128]{1,0:T(8,128)(2,1)S(1)} %get-tuple-element.49), channel_id=1, source_target_pairs={{1,2},{3,4},{5,6},{7,8},{9,10},{11,12},{13,14},{2,1},{4,3},{6,5},{... | collective-permute-start | bytes 786440 | tf_op jit(solution)/shard_map/ppermute | solution.py:351
  5.7 26.0 %collective-permute-start.3 = (bf16[1024,128]{1,0:T(8,128)(2,1)S(1)}, bf16[1024,128]{1,0:T(8,128)(2,1)S(1)}, u32[]{:S(2)}, u32[]{:S(2)}) collective-permute-start(bf16[1024,128]{1,0:T(8,128)(2,1)S(1)} %get-tuple-element.41), channel_id=1, source_target_pairs={{1,2},{3,4},{5,6},{7,8},{9,10},{11,12},{13,14},{2,1},{4,3},{6,5},{... | collective-permute-start | bytes 786440 | tf_op jit(solution)/shard_map/ppermute | solution.py:351
  6.4 29.8 %collective-permute-start.12 = (bf16[1024,128]{1,0:T(8,128)(2,1)S(1)}, bf16[1024,128]{1,0:T(8,128)(2,1)S(1)}, u32[]{:S(2)}, u32[]{:S(2)}) collective-permute-start(bf16[1024,128]{1,0:T(8,128)(2,1)S(1)} %get-tuple-element.53.refs_3_), channel_id=1, source_target_pairs={{0,16},{16,0},{1,17},{17,1},{2,18},{18,2},{3,19},{19,3},{4,20},{20... | collective-permute-start | bytes 786440 | tf_op jit(solution)/shard_map/ppermute | solution.py:357
  29.0 12.8 %collective-permute-start.15 = (bf16[1024,128]{1,0:T(8,128)(2,1)S(1)}, bf16[1024,128]{1,0:T(8,128)(2,1)S(1)}, u32[]{:S(2)}, u32[]{:S(2)}) collective-permute-start(bf16[1024,128]{1,0:T(8,128)(2,1)S(1)} %get-tuple-element.57.refs_3_), channel_id=1, source_target_pairs={{0,16},{16,0},{1,17},{17,1},{2,18},{18,2},{3,19},{19,3},{4,20},{20... | collective-permute-start | bytes 786440 | tf_op jit(solution)/shard_map/ppermute | solution.py:357
  31.6 16.9 %collective-permute-start.9 = (bf16[1024,128]{1,0:T(8,128)(2,1)S(1)}, bf16[1024,128]{1,0:T(8,128)(2,1)S(1)}, u32[]{:S(2)}, u32[]{:S(2)}) collective-permute-start(bf16[1024,128]{1,0:T(8,128)(2,1)S(1)} %combine_0_1_0.1.refs_3_), channel_id=1, source_target_pairs={{0,16},{16,0},{1,17},{17,1},{2,18},{18,2},{3,19},{19,3},{4,20},{20... | collective-permute-start | bytes 786440 | tf_op jit(solution)/shard_map/ppermute | solution.py:357
  31.8 22.9 %collective-permute-start.4 = (bf16[1024,128]{1,0:T(8,128)(2,1)S(1)}, bf16[1024,128]{1,0:T(8,128)(2,1)S(1)}, u32[]{:S(2)}, u32[]{:S(2)}) collective-permute-start(bf16[1024,128]{1,0:T(8,128)(2,1)S(1)} %combine_0_1_1.1.refs_3_), channel_id=1, source_target_pairs={{0,16},{16,0},{1,17},{17,1},{2,18},{18,2},{3,19},{19,3},{4,20},{20... | collective-permute-start | bytes 786440 | tf_op jit(solution)/shard_map/ppermute | solution.py:357
  38.4 19.9 %collective-permute-start.13 = (bf16[1024,128]{1,0:T(8,128)(2,1)S(1)}, bf16[1024,128]{1,0:T(8,128)(2,1)S(1)}, u32[]{:S(2)}, u32[]{:S(2)}) collective-permute-start(bf16[1024,128]{1,0:T(8,128)(2,1)S(1)} %get-tuple-element.55), channel_id=1, source_target_pairs={{0,1},{1,0},{2,3},{3,2},{4,5},{5,4},{6,7},{7,6},{8,9},{9,8},{10,11... | collective-permute-start | bytes 786440 | tf_op jit(solution)/shard_map/ppermute | solution.py:354
  44.1 16.3 %collective-permute-start.16 = (bf16[1024,128]{1,0:T(8,128)(2,1)S(1)}, bf16[1024,128]{1,0:T(8,128)(2,1)S(1)}, u32[]{:S(2)}, u32[]{:S(2)}) collective-permute-start(bf16[1024,128]{1,0:T(8,128)(2,1)S(1)} %get-tuple-element.59), channel_id=1, source_target_pairs={{0,1},{1,0},{2,3},{3,2},{4,5},{5,4},{6,7},{7,6},{8,9},{9,8},{10,11... | collective-permute-start | bytes 786440 | tf_op jit(solution)/shard_map/ppermute | solution.py:354
  44.1 16.7 %collective-permute-start.17 = (bf16[1024,128]{1,0:T(8,128)(2,1)S(1)}, bf16[1024,128]{1,0:T(8,128)(2,1)S(1)}, u32[]{:S(2)}, u32[]{:S(2)}) collective-permute-start(bf16[1024,128]{1,0:T(8,128)(2,1)S(1)} %get-tuple-element.60), channel_id=1, source_target_pairs={{17,18},{19,20},{21,22},{23,24},{25,26},{27,28},{29,30},{18,17},{2... | collective-permute-start | bytes 786440 | tf_op jit(solution)/shard_map/ppermute | solution.py:351
  48.5 15.7 %collective-permute-start.14 = (bf16[1024,128]{1,0:T(8,128)(2,1)S(1)}, bf16[1024,128]{1,0:T(8,128)(2,1)S(1)}, u32[]{:S(2)}, u32[]{:S(2)}) collective-permute-start(bf16[1024,128]{1,0:T(8,128)(2,1)S(1)} %get-tuple-element.56), channel_id=1, source_target_pairs={{17,18},{19,20},{21,22},{23,24},{25,26},{27,28},{29,30},{18,17},{2... | collective-permute-start | bytes 786440 | tf_op jit(solution)/shard_map/ppermute | solution.py:351
  54.6 10.6 %collective-permute-start.10 = (bf16[1024,128]{1,0:T(8,128)(2,1)S(1)}, bf16[1024,128]{1,0:T(8,128)(2,1)S(1)}, u32[]{:S(2)}, u32[]{:S(2)}) collective-permute-start(bf16[1024,128]{1,0:T(8,128)(2,1)S(1)} %get-tuple-element.51), channel_id=1, source_target_pairs={{0,1},{1,0},{2,3},{3,2},{4,5},{5,4},{6,7},{7,6},{8,9},{9,8},{10,11... | collective-permute-start | bytes 786440 | tf_op jit(solution)/shard_map/ppermute | solution.py:354
  58.4 13.3 %collective-permute-start.11 = (bf16[1024,128]{1,0:T(8,128)(2,1)S(1)}, bf16[1024,128]{1,0:T(8,128)(2,1)S(1)}, u32[]{:S(2)}, u32[]{:S(2)}) collective-permute-start(bf16[1024,128]{1,0:T(8,128)(2,1)S(1)} %get-tuple-element.52), channel_id=1, source_target_pairs={{17,18},{19,20},{21,22},{23,24},{25,26},{27,28},{29,30},{18,17},{2... | collective-permute-start | bytes 786440 | tf_op jit(solution)/shard_map/ppermute | solution.py:351
  60.3 11.5 %collective-permute-start.5 = (bf16[1024,128]{1,0:T(8,128)(2,1)S(1)}, bf16[1024,128]{1,0:T(8,128)(2,1)S(1)}, u32[]{:S(2)}, u32[]{:S(2)}) collective-permute-start(bf16[1024,128]{1,0:T(8,128)(2,1)S(1)} %get-tuple-element.43), channel_id=1, source_target_pairs={{0,1},{1,0},{2,3},{3,2},{4,5},{5,4},{6,7},{7,6},{8,9},{9,8},{10,11... | collective-permute-start | bytes 786440 | tf_op jit(solution)/shard_map/ppermute | solution.py:354
  60.9 13.6 %collective-permute-start.6 = (bf16[1024,128]{1,0:T(8,128)(2,1)S(1)}, bf16[1024,128]{1,0:T(8,128)(2,1)S(1)}, u32[]{:S(2)}, u32[]{:S(2)}) collective-permute-start(bf16[1024,128]{1,0:T(8,128)(2,1)S(1)} %get-tuple-element.44), channel_id=1, source_target_pairs={{17,18},{19,20},{21,22},{23,24},{25,26},{27,28},{29,30},{18,17},{2... | collective-permute-start | bytes 786440 | tf_op jit(solution)/shard_map/ppermute | solution.py:351

commit v2 on v1

--- a/solution.py
+++ b/solution.py
@@ -53,14 +53,16 @@
     return jnp.where(lane < half, -moved, moved)
 
 
-def accumulate(index_refs, rows_s, cols_s, tiles, pair, sums, blocks, ready):
+def accumulate(index_refs, rows_s, cols_s, tiles, pair, sums, blocks, skipped=None):
     tile_size = tiles.shape[-1]
     first = (lax.axis_index("tile") - 1) * blocks
     count = index_refs[2][0, 0]
     for i in range(tiles.shape[0]):
-        ready(i)
         live = i < count
-        row = jnp.where(live, rows_s[0, i] - first, 3 * blocks)
+        window = rows_s[0, i] - first
+        if skipped is not None:
+            live = live & (lax.div(window, blocks) != skipped)
+        row = jnp.where(live, window, 3 * blocks)
         column = jnp.where(live, cols_s[0, i], 0)
         rows = pl.ds(pl.multiple_of(column * tile_size, tile_size), tile_size)
         target = pl.ds(pl.multiple_of(row * tile_size, tile_size), tile_size)
@@ -78,87 +80,141 @@
     return sums[pl.ds(pl.multiple_of(start + r * tile_size, tile_size), tile_size), :]
 
 
-def front_kernel(front, blocks, *refs):
-    index_refs, incident, sources = refs[:3], refs[3], refs[4]
-    if front == 0:
-        stored, outer_refs, inner_ref, own_refs, tiles = refs[5], refs[6:8], refs[8], refs[9:11], refs[11]
-        rest = refs[12:]
-    else:
-        tiles, outer_refs, inner_ref, own_refs = refs[5], refs[7:9], refs[9], refs[10:12]
-        rest = refs[13:]
-    rows_s, cols_s, source_v, pair, sums, sems, tile_sems = rest
+def outer_window():
+    return 2 * lax.rem(lax.axis_index("tile"), 2)
+
+
+def open_kernel(blocks, *refs):
+    index_refs, (incident, stored, *outer_refs), (pair, tiles) = refs[:3], refs[3:7], refs[7:9]
+    rows_s, cols_s, sums, sems, tile_sems = refs[9:]
     slots, tile_size = tiles.shape[0], tiles.shape[-1]
-    rows_dev = pair.shape[1]
-    packed = rows_dev // 2
-
-    def tile_copy(i):
-        return pltpu.make_async_copy(stored.at[0, i], tiles.at[i], tile_sems.at[i])
-
+    half = tile_size // 2
     active = lax.axis_index("layer") == 0
     copies = [
         pltpu.make_async_copy(index_refs[0], rows_s, sems.at[0]),
         pltpu.make_async_copy(index_refs[1], cols_s, sems.at[1]),
-        pltpu.make_async_copy(incident.at[front], pair.at[0], sems.at[2]),
-        pltpu.make_async_copy(sources.at[0, front], source_v, sems.at[3]),
+        pltpu.make_async_copy(incident.at[0], pair.at[0], sems.at[2]),
     ]
 
-    @pl.when(active)
-    def _():
-        for copy in copies[:3]:
-            copy.start()
-
-    early = slots // 4 if front == 0 else 0
+    def tile_copy(i):
+        return pltpu.make_async_copy(stored.at[0, i], tiles.at[i], tile_sems.at[i])
+
+    for copy in copies:
+        copy.start()
+    early = slots // 4
     for i in range(early):
         tile_copy(i).start()
 
     @pl.when(active)
     def _():
         sums[...] = jnp.zeros(sums.shape, jnp.float32)
-        for copy in copies[:3]:
-            copy.wait()
-        if front == 0:
-            for i in range(early, slots):
-                tile_copy(i).start()
+
+    for copy in copies:
+        copy.wait()
+    for i in range(early, slots):
+        tile_copy(i).start()
+
+    @pl.when(active)
+    def _():
         for r in range(blocks):
             rows = pl.ds(r * tile_size, tile_size)
             pair[1, rows, :] = turn(pair[0, rows, :].astype(jnp.float32)).astype(jnp.bfloat16)
-        copies[3].start()
-        ready = (lambda i: tile_copy(i).wait()) if front == 0 else (lambda i: None)
-        accumulate(index_refs, rows_s, cols_s, tiles, pair, sums, blocks, ready)
+
+    count = index_refs[2][0, 0]
+    first = (lax.axis_index("tile") - 1) * blocks
+
+    @pl.loop(0, slots)
+    def _(i):
+        tile_copy(i).wait()
+        window = rows_s[0, i] - first
+
+        @pl.when(active & (i < count) & (lax.div(window, blocks) == outer_window()))
+        def _():
+            rows = pl.ds(pl.multiple_of(cols_s[0, i] * tile_size, tile_size), tile_size)
+            target = pl.ds(pl.multiple_of(lax.rem(window, blocks) * tile_size, tile_size), tile_size)
+            term = jnp.dot(tiles[i, 0], pair[0, rows, :], preferred_element_type=jnp.float32)
+            term += jnp.dot(tiles[i, 1], pair[1, rows, :], preferred_element_type=jnp.float32)
+            sums[target, :] += term
+
+    @pl.when(active)
+    def _():
+        for r in range(blocks):
+            block = sums[pl.ds(r * tile_size, tile_size), :]
+            for part in range(PARTS):
+                outer_refs[part][pl.ds(r * half, half), :] = pack(block, part).astype(jnp.bfloat16)
+
+
+def open_products(incident, tiles, index, blocks):
+    rows_dev, width = incident.shape[-2:]
+    slots, _, tile_size, _ = tiles.shape[-4:]
+    outer = pltpu.VMEM((rows_dev // 2, width), jnp.bfloat16)
+    return pl.pallas_call(
+        functools.partial(open_kernel, blocks),
+        out_shape=[
+            outer,
+            outer,
+            pltpu.VMEM((2, rows_dev, width), jnp.bfloat16),
+            pltpu.VMEM((slots, 2, tile_size, tile_size), jnp.bfloat16),
+        ],
+        in_specs=[HBM, HBM, SMEM, HBM, HBM],
+        out_specs=[VMEM] * 4,
+        scratch_shapes=[
+            pltpu.SMEM((1, slots), jnp.int32),
+            pltpu.SMEM((1, slots), jnp.int32),
+            pltpu.VMEM((rows_dev, width), jnp.float32),
+            pltpu.SemaphoreType.DMA((3,)),
+            pltpu.SemaphoreType.DMA((slots,)),
+        ],
+        **kernel_options("open", 5 * 10**8, 4 * 10**6, 4),
+    )(*index, incident, tiles)
+
+
+def front_kernel(front, blocks, *refs):
+    index_refs, sources, tiles, operand = refs[:3], refs[3], refs[4], refs[5]
+    outs, (rows_s, cols_s, source_v, sums, sems, *rest) = refs[6 : len(refs) - (5 if front == 0 else 6)], refs[
+        len(refs) - (5 if front == 0 else 6) :
+    ]
+    inner_ref, own_refs, outer_refs = outs[0], outs[1:3], outs[3:]
+    pair = operand if front == 0 else rest[0]
+    tile_size = tiles.shape[-1]
+    rows_dev = pair.shape[1]
+    packed = rows_dev // 2
+
+    @pl.when(lax.axis_index("layer") == 0)
+    def _():
+        copies = [
+            pltpu.make_async_copy(index_refs[0], rows_s, sems.at[0]),
+            pltpu.make_async_copy(index_refs[1], cols_s, sems.at[1]),
+            pltpu.make_async_copy(sources.at[0, front], source_v, sems.at[2]),
+        ]
+        if front > 0:
+            copies.append(pltpu.make_async_copy(operand.at[front], pair.at[0], sems.at[3]))
+        for copy in copies:
+            copy.start()
+        sums[...] = jnp.zeros(sums.shape, jnp.float32)
+        for copy in copies:
+            copy.wait()
+        if front > 0:
+            for r in range(blocks):
+                rows = pl.ds(r * tile_size, tile_size)
+                pair[1, rows, :] = turn(pair[0, rows, :].astype(jnp.float32)).astype(jnp.bfloat16)
+        accumulate(
+            index_refs, rows_s, cols_s, tiles, pair, sums, blocks, outer_window() if front == 0 else None
+        )
         inner_start, outer_start = side_starts(rows_dev)
-        copies[3].wait()
         half = tile_size // 2
         for r in range(blocks):
             own = sums[pl.ds(rows_dev + r * tile_size, tile_size), :]
             own = own + source_v[pl.ds(r * tile_size, tile_size), :].astype(jnp.float32)
             inner = read_block(sums, inner_start, r, tile_size)
-            outer = read_block(sums, outer_start, r, tile_size)
             for part in range(PARTS):
                 rows = pl.ds(r * half, half)
                 own_refs[part][rows, :] = pack(own, part)
-                outer_refs[part][rows, :] = pack(outer, part).astype(jnp.bfloat16)
                 inner_ref[pl.ds(part * packed + r * half, half), :] = pack(inner, part).astype(jnp.bfloat16)
-
-    if front == 0:
-
-        @pl.when(jnp.logical_not(active))
-        def _():
-            for i in range(early, slots):
-                tile_copy(i).start()
-            for i in range(slots):
-                tile_copy(i).wait()
-
-
-def scratch(slots, rows_dev, width, tile_size):
-    return [
-        pltpu.SMEM((1, slots), jnp.int32),
-        pltpu.SMEM((1, slots), jnp.int32),
-        pltpu.VMEM((rows_dev, width), jnp.bfloat16),
-        pltpu.VMEM((2, rows_dev, width), jnp.bfloat16),
-        pltpu.VMEM((3 * rows_dev + tile_size, width), jnp.float32),
-        pltpu.SemaphoreType.DMA((4,)),
-        pltpu.SemaphoreType.DMA((slots,)),
-    ]
+            if front > 0:
+                outer = read_block(sums, outer_start, r, tile_size)
+                for part in range(PARTS):
+                    outer_refs[part][pl.ds(r * half, half), :] = pack(outer, part).astype(jnp.bfloat16)
 
 
 def kernel_options(name, flops, moved, limit=20):
@@ -169,31 +225,29 @@
     )
 
 
-def front_products(front, incident, sources, tiles, index, blocks, through=None):
-    rows_dev, width = incident.shape[-2:]
-    slots, _, tile_size, _ = tiles.shape[-4:]
-    packed = rows_dev // 2
-    outer = pltpu.VMEM((packed, width), jnp.bfloat16)
-    own = pltpu.VMEM((packed, width), jnp.float32)
-    outs = [outer, outer, pltpu.VMEM((rows_dev, width), jnp.bfloat16), own, own]
-    args, specs, aliases = [*index, incident, sources, tiles], [HBM, HBM, SMEM, HBM, HBM], {}
-    if front == 0:
-        specs.append(HBM)
-        outs.append(pltpu.VMEM((slots, 2, tile_size, tile_size), jnp.bfloat16))
-    else:
-        specs += [VMEM, VMEM]
-        aliases = {len(args): len(outs)}
-        args.append(through)
-        outs.append(outer)
+def front_products(front, operand, sources, tiles, index, blocks):
+    rows_dev, width = sources.shape[-2:]
+    slots, _, tile_size, _ = tiles.shape
+    outer = pltpu.VMEM((rows_dev // 2, width), jnp.bfloat16)
+    own = pltpu.VMEM((rows_dev // 2, width), jnp.float32)
+    outs = [pltpu.VMEM((rows_dev, width), jnp.bfloat16), own, own] + ([outer, outer] if front else [])
+    scratch = [
+        pltpu.SMEM((1, slots), jnp.int32),
+        pltpu.SMEM((1, slots), jnp.int32),
+        pltpu.VMEM((rows_dev, width), jnp.bfloat16),
+        pltpu.VMEM((3 * rows_dev + tile_size, width), jnp.float32),
+        pltpu.SemaphoreType.DMA((4,)),
+    ]
+    if front:
+        scratch.append(pltpu.VMEM((2, rows_dev, width), jnp.bfloat16))
     return pl.pallas_call(
         functools.partial(front_kernel, front, blocks),
         out_shape=outs,
-        in_specs=specs,
+        in_specs=[HBM, HBM, SMEM, HBM, VMEM, HBM if front else VMEM],
         out_specs=[VMEM] * len(outs),
-        scratch_shapes=scratch(slots, rows_dev, width, tile_size),
-        input_output_aliases=aliases,
-        **kernel_options(f"front_{front}", 10**9, 5 * 10**6),
-    )(*args)
+        scratch_shapes=scratch,
+        **kernel_options(f"front_{front}", 10**9, 5 * 10**6, 6),
+    )(*index, sources, tiles, operand)
 
 
 def prepare_kernel(wave, front, part, sources, sums, source_v, sem):
@@ -251,7 +305,7 @@
                 pair[1, rows, :] = turn(value).astype(jnp.bfloat16)
         for copy in copies:
             copy.wait()
-        accumulate(index_refs, rows_s, cols_s, tiles, pair, sums, blocks, lambda i: None)
+        accumulate(index_refs, rows_s, cols_s, tiles, pair, sums, blocks)
         inner_start, outer_start = side_starts(rows_dev)
         for r in range(blocks):
             rows = pl.ds(r * half, half)
@@ -359,27 +413,20 @@
     def total(wave, chunk, *args, **kwargs):
         return combine(wave, chunk // PARTS, chunk % PARTS, *args, **kwargs)
 
-    chunks, payloads, held, waiting = [], [], green_tiles, None
+    first = open_products(incident, green_tiles, index, blocks)
+    payloads, held = list(first[:PARTS]), first[3]
+    chunks = []
     for front in range(fronts):
-        made = front_products(front, incident, sources, held, index, blocks, waiting)
-        if front == 0:
-            held, waiting = made[5], made[1]
-            payloads = [None] * PARTS
-            outers = [across(made[0], 0), None]
-        else:
-            if front == 1:
-                chunks[1][2] = across(made[5], 0)
-            payloads += made[:2]
-            outers = [None, None]
-            waiting = made[1]
-        inner = beside(made[2])
-        chunks += [[made[3 + part], inner, outers[part]] for part in range(PARTS)]
-    if fronts == 1:
-        chunks[1][2] = across(waiting, 0)
+        made = front_products(front, incident if front else first[2], sources, held, index, blocks)
+        inner = beside(made[0])
+        payloads += made[3:]
+        chunks += [[made[1 + part], inner, None] for part in range(PARTS)]
+    for c in range(min(PARTS + 1, len(chunks))):
+        chunks[c][2] = across(payloads[c], 0)
     passed, leaving = [], []
     for c in range(len(chunks)):
         behind = c + PARTS
-        through = payloads[behind] if behind < len(chunks) else None
+        through = payloads[behind] if PARTS < behind < len(chunks) else None
         made = total(0, c, *chunks[c], through=through)
         if through is not None:
             chunks[behind][2] = across(made[1], 0)

time: 76 us -> 77.1 us (1.014)
  waiting for transfers between devices: 14.2 us -> 8.88 us
  starting transfers between devices: 41.5 us -> 46.4 us
  Pallas kernels: 18.9 us -> 19.8 us
    ppermute x4, waiting for transfers between devices: 5.06 us -> 0.01 us  [down(): return lax.ppermute(payload, 'layer', layer_route)]
    ppermute x4, starting transfers between devices: 25.4 us -> 30 us  [down(): return lax.ppermute(payload, 'layer', layer_route)]
    pallas_call x0 -> x1, Pallas kernels: none -> 2.93 us  [open_products(): pl.pallas_call(functools.partial(open_kernel, blocks), out_shape=[outer,...]
    pallas_call x2, Pallas kernels: 2.13 us -> 0.11 us  [front_products(): pl.pallas_call(functools.partial(front_kernel, front, blocks), out_shape=...]
  transfers between devices with their start and end apart: 18 -> 18, of which waited for: 4 -> 2; matrix products, arithmetic and copies ran while one was open for 0% -> 0% of each run, Pallas kernels for 21% -> 21%
where the time goes in v2:
time: 77.1 us; the launch traced here: 76.1 us
  starting transfers between devices  46.4 us (60%)
  Pallas kernels  19.8 us (26%)
  waiting for transfers between devices  8.88 us (12%)
  between operations  0.96 us (1%)
    ppermute x4, starting transfers between devices, down(): return lax.ppermute(payload, 'layer', layer_route)  30 us
    ppermute x8, starting transfers between devices, across(): return lax.ppermute(payload, ('layer', 'tile'), outer_route(wave, devices))  13 us
    pallas_call x4, Pallas kernels, chunk_products(): pl.pallas_call(functools.partial(chunk_kernel, wave, blocks), out_shape=[...  9.33 us
    ppermute x8, waiting for transfers between devices, across(): return lax.ppermute(payload, ('layer', 'tile'), outer_route(wave, devices))  8.85 us
    pallas_call x4, Pallas kernels, prepare(): pl.pallas_call(functools.partial(prepare_kernel, wave, front, part), out_...  4.78 us
    ppermute x6, starting transfers between devices, beside(): return lax.ppermute(payload, 'tile', inner_route(devices))  3.4 us
    pallas_call x1, Pallas kernels, open_products(): pl.pallas_call(functools.partial(open_kernel, blocks), out_shape=[outer,...  2.93 us
    pallas_call x8, Pallas kernels, combine(): pl.pallas_call(functools.partial(combine_kernel, wave, part, through is n...  2.67 us
  transfers between devices with their start and end apart: 18, of which 2 were waited for; matrix products, arithmetic and copies ran while one was open for 0% of the time, Pallas kernels for 21%

profile of v2, /device:TPU:22, one launch (start us, length us, event | category | flops | bytes accessed | tf_op | source)
XLA Modules:
  0.0 76.1 jit_solution(1919984130940567377)
XLA Ops:
  0.7 2.9 %open.1 = (bf16[1024,128]{1,0:T(8,128)(2,1)S(1)}, bf16[1024,128]{1,0:T(8,128)(2,1)S(1)}, bf16[2,2048,128]{2,1,0:T(8,128)(2,1)S(1)}, bf16[12,2,256,256]{3,2,1,0:T(8,128)(2,1)S(1)}) custom-call(s32[1,12]{1,0:T(1,128)} %refs_0_.13, s32[1,12]{1,0:T(1,128)} %refs_1_.13, s32[1,1]{1,0:T(1,128)S(6)} %copy.19.refs_2_, bf16[2,2048,128]{2,1,0:T(8,128)(2,1)} %refs_5_.1, ...), custom_call_target="tpu_custom_call" | custom-call | flops 500000000 | bytes 4000000 | tf_op jit(solution)/shard_map/open/pallas_call | solution.py:151
  3.8 0.5 collective-permute-start
  4.3 0.7 collective-permute-start.2
  5.0 0.7 collective-permute-start.14
  5.7 0.7 collective-permute-start.7
  6.4 0.1 combine_0_0_1.1
  6.5 0.7 collective-permute-start.3
  7.2 0.1 combine_0_0_0.1.refs_3_
  7.3 25.2 %collective-permute-start.15 = (bf16[1024,128]{1,0:T(8,128)(2,1)S(1)}, bf16[1024,128]{1,0:T(8,128)(2,1)S(1)}, u32[]{:S(2)}, u32[]{:S(2)}) collective-permute-start(bf16[1024,128]{1,0:T(8,128)(2,1)S(1)} %combine_0_0_0.1.refs_3_), channel_id=1, source_target_pairs={{0,16},{16,0},{1,17},{17,1},{2,18},{18,2},{3,19},{19,3},{4,20},{20... | collective-permute-start | bytes 786440 | tf_op jit(solution)/shard_map/ppermute | solution.py:411
  32.5 2.7 %collective-permute-start.8 = (bf16[1024,128]{1,0:T(8,128)(2,1)S(1)}, bf16[1024,128]{1,0:T(8,128)(2,1)S(1)}, u32[]{:S(2)}, u32[]{:S(2)}) collective-permute-start(bf16[1024,128]{1,0:T(8,128)(2,1)S(1)} %combine_0_1_0.1.refs_3_), channel_id=1, source_target_pairs={{0,16},{16,0},{1,17},{17,1},{2,18},{18,2},{3,19},{19,3},{4,20},{20... | collective-permute-start | bytes 786440 | tf_op jit(solution)/shard_map/ppermute | solution.py:411
  35.2 1.1 %prepare_1_0_0.1.refs_5_ = f32[6400,128]{1,0:T(8,128)S(1)} custom-call(bf16[1,2,2048,128]{3,2,1,0:T(8,128)(2,1)} %sources.7), custom_call_target="tpu_custom_call" | custom-call | flops 1000000 | bytes 1000000 | tf_op jit(solution)/shard_map/prepare_1_0_0/pallas_call | solution.py:274
  36.4 1.1 %prepare_1_1_0.1.refs_5_ = f32[6400,128]{1,0:T(8,128)S(1)} custom-call(bf16[1,2,2048,128]{3,2,1,0:T(8,128)(2,1)} %sources.7), custom_call_target="tpu_custom_call" | custom-call | flops 1000000 | bytes 1000000 | tf_op jit(solution)/shard_map/prepare_1_1_0/pallas_call | solution.py:274
  37.7 2.1 %collective-permute-start.4 = (bf16[1024,128]{1,0:T(8,128)(2,1)S(1)}, bf16[1024,128]{1,0:T(8,128)(2,1)S(1)}, u32[]{:S(2)}, u32[]{:S(2)}) collective-permute-start(bf16[1024,128]{1,0:T(8,128)(2,1)S(1)} %combine_0_1_1.1.refs_3_), channel_id=1, source_target_pairs={{0,16},{16,0},{1,17},{17,1},{2,18},{18,2},{3,19},{19,3},{4,20},{20... | collective-permute-start | bytes 786440 | tf_op jit(solution)/shard_map/ppermute | solution.py:411
  39.8 2.3 %chunk_1_0_0.1 = (bf16[1024,128]{1,0:T(8,128)(2,1)S(1)}, bf16[1024,128]{1,0:T(8,128)(2,1)S(1)}, f32[1024,128]{1,0:T(8,128)S(1)}, f32[6400,128]{1,0:T(8,128)S(1)}) custom-call(s32[1,12]{1,0:T(1,128)} %refs_0_.13, s32[1,12]{1,0:T(1,128)} %refs_1_.13, s32[1,1]{1,0:T(1,128)S(6)} %copy.19.refs_2_, ...), custom_call_target="tpu_custom_call", output_to_operand_aliasing={{3}: (5, {})} | custom-call | flops 1000000000 | bytes 5000000 | tf_op jit(solution)/shard_map/chunk_1_0_0/pallas_call | solution.py:321
  42.1 1.9 %collective-permute-start.17 = (bf16[1024,128]{1,0:T(8,128)(2,1)S(1)}, bf16[1024,128]{1,0:T(8,128)(2,1)S(1)}, u32[]{:S(2)}, u32[]{:S(2)}) collective-permute-start(bf16[1024,128]{1,0:T(8,128)(2,1)S(1)} %get-tuple-element.56), channel_id=1, source_target_pairs={{17,18},{19,20},{21,22},{23,24},{25,26},{27,28},{29,30},{18,17},{2... | collective-permute-start | bytes 786440 | tf_op jit(solution)/shard_map/ppermute | solution.py:405
  44.1 2.3 %chunk_1_1_0.1 = (bf16[1024,128]{1,0:T(8,128)(2,1)S(1)}, bf16[1024,128]{1,0:T(8,128)(2,1)S(1)}, f32[1024,128]{1,0:T(8,128)S(1)}, f32[6400,128]{1,0:T(8,128)S(1)}) custom-call(s32[1,12]{1,0:T(1,128)} %refs_0_.13, s32[1,12]{1,0:T(1,128)} %refs_1_.13, s32[1,1]{1,0:T(1,128)S(6)} %copy.19.refs_2_, ...), custom_call_target="tpu_custom_call", output_to_operand_aliasing={{3}: (5, {})} | custom-call | flops 1000000000 | bytes 5000000 | tf_op jit(solution)/shard_map/chunk_1_1_0/pallas_call | solution.py:321
  46.4 3.6 %collective-permute-start.10 = (bf16[1024,128]{1,0:T(8,128)(2,1)S(1)}, bf16[1024,128]{1,0:T(8,128)(2,1)S(1)}, u32[]{:S(2)}, u32[]{:S(2)}) collective-permute-start(bf16[1024,128]{1,0:T(8,128)(2,1)S(1)} %get-tuple-element.47), channel_id=1, source_target_pairs={{17,18},{19,20},{21,22},{23,24},{25,26},{27,28},{29,30},{18,17},{2... | collective-permute-start | bytes 786440 | tf_op jit(solution)/shard_map/ppermute | solution.py:405
  50.0 1.3 %prepare_1_0_1.1.refs_5_ = f32[6400,128]{1,0:T(8,128)S(1)} custom-call(bf16[1,2,2048,128]{3,2,1,0:T(8,128)(2,1)} %sources.7), custom_call_target="tpu_custom_call" | custom-call | flops 1000000 | bytes 1000000 | tf_op jit(solution)/shard_map/prepare_1_0_1/pallas_call | solution.py:274
  51.3 1.3 %prepare_1_1_1.1.refs_5_ = f32[6400,128]{1,0:T(8,128)S(1)} custom-call(bf16[1,2,2048,128]{3,2,1,0:T(8,128)(2,1)} %sources.7), custom_call_target="tpu_custom_call" | custom-call | flops 1000000 | bytes 1000000 | tf_op jit(solution)/shard_map/prepare_1_1_1/pallas_call | solution.py:274
  52.6 2.5 %chunk_1_0_1.1 = (bf16[1024,128]{1,0:T(8,128)(2,1)S(1)}, bf16[1024,128]{1,0:T(8,128)(2,1)S(1)}, f32[1024,128]{1,0:T(8,128)S(1)}, f32[6400,128]{1,0:T(8,128)S(1)}) custom-call(s32[1,12]{1,0:T(1,128)} %refs_0_.13, s32[1,12]{1,0:T(1,128)} %refs_1_.13, s32[1,1]{1,0:T(1,128)S(6)} %copy.19.refs_2_, ...), custom_call_target="tpu_custom_call", output_to_operand_aliasing={{3}: (5, {})} | custom-call | flops 1000000000 | bytes 5000000 | tf_op jit(solution)/shard_map/chunk_1_0_1/pallas_call | solution.py:321
  55.1 1.5 %collective-permute-start.12 = (bf16[1024,128]{1,0:T(8,128)(2,1)S(1)}, bf16[1024,128]{1,0:T(8,128)(2,1)S(1)}, u32[]{:S(2)}, u32[]{:S(2)}) collective-permute-start(bf16[1024,128]{1,0:T(8,128)(2,1)S(1)} %get-tuple-element.50), channel_id=1, source_target_pairs={{0,1},{1,0},{2,3},{3,2},{4,5},{5,4},{6,7},{7,6},{8,9},{9,8},{10,11... | collective-permute-start | bytes 786440 | tf_op jit(solution)/shard_map/ppermute | solution.py:408
  56.5 0.1 collective-permute-start.9
  56.6 2.3 %chunk_1_1_1.1 = (bf16[1024,128]{1,0:T(8,128)(2,1)S(1)}, bf16[1024,128]{1,0:T(8,128)(2,1)S(1)}, f32[1024,128]{1,0:T(8,128)S(1)}, f32[6400,128]{1,0:T(8,128)S(1)}) custom-call(s32[1,12]{1,0:T(1,128)} %refs_0_.13, s32[1,12]{1,0:T(1,128)} %refs_1_.13, s32[1,1]{1,0:T(1,128)S(6)} %copy.19.refs_2_, ...), custom_call_target="tpu_custom_call", output_to_operand_aliasing={{3}: (5, {})} | custom-call | flops 1000000000 | bytes 5000000 | tf_op jit(solution)/shard_map/chunk_1_1_1/pallas_call | solution.py:321
  58.9 1.9 %collective-permute-start.13 = (bf16[1024,128]{1,0:T(8,128)(2,1)S(1)}, bf16[1024,128]{1,0:T(8,128)(2,1)S(1)}, u32[]{:S(2)}, u32[]{:S(2)}) collective-permute-start(bf16[1024,128]{1,0:T(8,128)(2,1)S(1)} %get-tuple-element.51), channel_id=1, source_target_pairs={{17,18},{19,20},{21,22},{23,24},{25,26},{27,28},{29,30},{18,17},{2... | collective-permute-start | bytes 786440 | tf_op jit(solution)/shard_map/ppermute | solution.py:405
  60.8 1.2 %collective-permute-start.5 = (bf16[1024,128]{1,0:T(8,128)(2,1)S(1)}, bf16[1024,128]{1,0:T(8,128)(2,1)S(1)}, u32[]{:S(2)}, u32[]{:S(2)}) collective-permute-start(bf16[1024,128]{1,0:T(8,128)(2,1)S(1)} %get-tuple-element.41), channel_id=1, source_target_pairs={{0,1},{1,0},{2,3},{3,2},{4,5},{5,4},{6,7},{7,6},{8,9},{9,8},{10,11... | collective-permute-start | bytes 786440 | tf_op jit(solution)/shard_map/ppermute | solution.py:408
  62.0 2.8 %collective-permute-start.6 = (bf16[1024,128]{1,0:T(8,128)(2,1)S(1)}, bf16[1024,128]{1,0:T(8,128)(2,1)S(1)}, u32[]{:S(2)}, u32[]{:S(2)}) collective-permute-start(bf16[1024,128]{1,0:T(8,128)(2,1)S(1)} %get-tuple-element.42), channel_id=1, source_target_pairs={{17,18},{19,20},{21,22},{23,24},{25,26},{27,28},{29,30},{18,17},{2... | collective-permute-start | bytes 786440 | tf_op jit(solution)/shard_map/ppermute | solution.py:405
  64.9 0.1 combine_1_0_0.1.refs_4_
  65.0 0.1 combine_1_1_0.1.refs_4_
  65.1 7.1 %collective-permute-done.13.refs_2_ = bf16[1024,128]{1,0:T(8,128)(2,1)S(1)} collective-permute-done((bf16[1024,128]{1,0:T(8,128)(2,1)S(1)}, bf16[1024,128]{1,0:T(8,128)(2,1)S(1)}, u32[]{:S(2)}, u32[]{:S(2)}) %collective-permute-start.13) | collective-permute-done | bytes 262176 | tf_op jit(solution)/shard_map/ppermute | solution.py:405
  72.2 1.1 %combine_1_0_1.1.refs_5_ = bf16[1,2,2048,128]{3,2,1,0:T(8,128)(2,1)} custom-call(f32[1024,128]{1,0:T(8,128)S(1)} %get-tuple-element.49.refs_0_, bf16[1024,128]{1,0:T(8,128)(2,1)S(1)} %collective-permute-done.12.refs_1_, bf16[1024,128]{1,0:T(8,128)(2,1)S(1)} %collective-permute-done.13.refs_2_, bf16[1024,128]{1,0:T(8,128)(2,1)S(1)} %get-tuple-element.48.refs_3_, ...), custom_call_target="tpu_custom_call" | custom-call | flops 1000000 | bytes 1000000 | tf_op jit(solution)/shard_map/combine_1_0_1/pallas_call | solution.py:384
  73.3 1.8 %collective-permute-done.6.refs_2_ = bf16[1024,128]{1,0:T(8,128)(2,1)S(1)} collective-permute-done((bf16[1024,128]{1,0:T(8,128)(2,1)S(1)}, bf16[1024,128]{1,0:T(8,128)(2,1)S(1)}, u32[]{:S(2)}, u32[]{:S(2)}) %collective-permute-start.6) | collective-permute-done | bytes 262176 | tf_op jit(solution)/shard_map/ppermute | solution.py:405
  75.0 1.1 %combine_1_1_1.1 = bf16[1,2,2048,128]{3,2,1,0:T(8,128)(2,1)} custom-call(f32[1024,128]{1,0:T(8,128)S(1)} %get-tuple-element.40.refs_0_, bf16[1024,128]{1,0:T(8,128)(2,1)S(1)} %collective-permute-done.5.refs_1_, bf16[1024,128]{1,0:T(8,128)(2,1)S(1)} %collective-permute-done.6.refs_2_, ...), custom_call_target="tpu_custom_call", output_to_operand_aliasing={{}: (5, {})} | custom-call | flops 1000000 | bytes 1000000 | tf_op jit(solution)/shard_map/combine_1_1_1/pallas_call | solution.py:384
  (23 shorter events, 0.5 us)
Async XLA Ops:
  3.7 2.7 %collective-permute-start.1 = (bf16[2048,128]{1,0:T(8,128)(2,1)S(1)}, bf16[2048,128]{1,0:T(8,128)(2,1)S(1)}, u32[]{:S(2)}, u32[]{:S(2)}) collective-permute-start(bf16[2048,128]{1,0:T(8,128)(2,1)S(1)} %get-tuple-element.36), channel_id=1, source_target_pairs={{0,1},{1,0},{2,3},{3,2},{4,5},{5,4},{6,7},{7,6},{8,9},{9,8},{10,11... | collective-permute-start | bytes 1572872 | tf_op jit(solution)/shard_map/ppermute | solution.py:408
  3.8 28.6 %collective-permute-start = (bf16[2048,128]{1,0:T(8,128)(2,1)S(1)}, bf16[2048,128]{1,0:T(8,128)(2,1)S(1)}, u32[]{:S(2)}, u32[]{:S(2)}) collective-permute-start(bf16[2048,128]{1,0:T(8,128)(2,1)S(1)} %get-tuple-element.33), channel_id=1, source_target_pairs={{0,1},{1,0},{2,3},{3,2},{4,5},{5,4},{6,7},{7,6},{8,9},{9,8},{10,11... | collective-permute-start | bytes 1572872 | tf_op jit(solution)/shard_map/ppermute | solution.py:408
  4.3 2.0 %collective-permute-start.2 = (bf16[1024,128]{1,0:T(8,128)(2,1)S(1)}, bf16[1024,128]{1,0:T(8,128)(2,1)S(1)}, u32[]{:S(2)}, u32[]{:S(2)}) collective-permute-start(bf16[1024,128]{1,0:T(8,128)(2,1)S(1)} %get-tuple-element.37), channel_id=1, source_target_pairs={{1,2},{3,4},{5,6},{7,8},{9,10},{11,12},{13,14},{2,1},{4,3},{6,5},{... | collective-permute-start | bytes 786440 | tf_op jit(solution)/shard_map/ppermute | solution.py:405
  5.0 2.2 %collective-permute-start.14 = (bf16[1024,128]{1,0:T(8,128)(2,1)S(1)}, bf16[1024,128]{1,0:T(8,128)(2,1)S(1)}, u32[]{:S(2)}, u32[]{:S(2)}) collective-permute-start(bf16[1024,128]{1,0:T(8,128)(2,1)S(1)} %get-tuple-element.53), channel_id=1, source_target_pairs={{1,2},{3,4},{5,6},{7,8},{9,10},{11,12},{13,14},{2,1},{4,3},{6,5},{... | collective-permute-start | bytes 786440 | tf_op jit(solution)/shard_map/ppermute | solution.py:405
  5.7 26.7 %collective-permute-start.7 = (bf16[1024,128]{1,0:T(8,128)(2,1)S(1)}, bf16[1024,128]{1,0:T(8,128)(2,1)S(1)}, u32[]{:S(2)}, u32[]{:S(2)}) collective-permute-start(bf16[1024,128]{1,0:T(8,128)(2,1)S(1)} %get-tuple-element.44), channel_id=1, source_target_pairs={{1,2},{3,4},{5,6},{7,8},{9,10},{11,12},{13,14},{2,1},{4,3},{6,5},{... | collective-permute-start | bytes 786440 | tf_op jit(solution)/shard_map/ppermute | solution.py:405
  6.5 31.1 %collective-permute-start.3 = (bf16[1024,128]{1,0:T(8,128)(2,1)S(1)}, bf16[1024,128]{1,0:T(8,128)(2,1)S(1)}, u32[]{:S(2)}, u32[]{:S(2)}) collective-permute-start(bf16[1024,128]{1,0:T(8,128)(2,1)S(1)} %get-tuple-element.39), channel_id=1, source_target_pairs={{1,2},{3,4},{5,6},{7,8},{9,10},{11,12},{13,14},{2,1},{4,3},{6,5},{... | collective-permute-start | bytes 786440 | tf_op jit(solution)/shard_map/ppermute | solution.py:405
  7.3 32.5 %collective-permute-start.15 = (bf16[1024,128]{1,0:T(8,128)(2,1)S(1)}, bf16[1024,128]{1,0:T(8,128)(2,1)S(1)}, u32[]{:S(2)}, u32[]{:S(2)}) collective-permute-start(bf16[1024,128]{1,0:T(8,128)(2,1)S(1)} %combine_0_0_0.1.refs_3_), channel_id=1, source_target_pairs={{0,16},{16,0},{1,17},{17,1},{2,18},{18,2},{3,19},{19,3},{4,20},{20... | collective-permute-start | bytes 786440 | tf_op jit(solution)/shard_map/ppermute | solution.py:411
  32.5 11.5 %collective-permute-start.8 = (bf16[1024,128]{1,0:T(8,128)(2,1)S(1)}, bf16[1024,128]{1,0:T(8,128)(2,1)S(1)}, u32[]{:S(2)}, u32[]{:S(2)}) collective-permute-start(bf16[1024,128]{1,0:T(8,128)(2,1)S(1)} %combine_0_1_0.1.refs_3_), channel_id=1, source_target_pairs={{0,16},{16,0},{1,17},{17,1},{2,18},{18,2},{3,19},{19,3},{4,20},{20... | collective-permute-start | bytes 786440 | tf_op jit(solution)/shard_map/ppermute | solution.py:411
  37.5 15.1 %collective-permute-start.11 = (bf16[1024,128]{1,0:T(8,128)(2,1)S(1)}, bf16[1024,128]{1,0:T(8,128)(2,1)S(1)}, u32[]{:S(2)}, u32[]{:S(2)}) collective-permute-start(bf16[1024,128]{1,0:T(8,128)(2,1)S(1)} %get-tuple-element.48.refs_3_), channel_id=1, source_target_pairs={{0,16},{16,0},{1,17},{17,1},{2,18},{18,2},{3,19},{19,3},{4,20},{20... | collective-permute-start | bytes 786440 | tf_op jit(solution)/shard_map/ppermute | solution.py:411
  37.7 18.8 %collective-permute-start.4 = (bf16[1024,128]{1,0:T(8,128)(2,1)S(1)}, bf16[1024,128]{1,0:T(8,128)(2,1)S(1)}, u32[]{:S(2)}, u32[]{:S(2)}) collective-permute-start(bf16[1024,128]{1,0:T(8,128)(2,1)S(1)} %combine_0_1_1.1.refs_3_), channel_id=1, source_target_pairs={{0,16},{16,0},{1,17},{17,1},{2,18},{18,2},{3,19},{19,3},{4,20},{20... | collective-permute-start | bytes 786440 | tf_op jit(solution)/shard_map/ppermute | solution.py:411
  42.0 16.8 %collective-permute-start.16 = (bf16[1024,128]{1,0:T(8,128)(2,1)S(1)}, bf16[1024,128]{1,0:T(8,128)(2,1)S(1)}, u32[]{:S(2)}, u32[]{:S(2)}) collective-permute-start(bf16[1024,128]{1,0:T(8,128)(2,1)S(1)} %get-tuple-element.55), channel_id=1, source_target_pairs={{0,1},{1,0},{2,3},{3,2},{4,5},{5,4},{6,7},{7,6},{8,9},{9,8},{10,11... | collective-permute-start | bytes 786440 | tf_op jit(solution)/shard_map/ppermute | solution.py:408
  42.1 18.7 %collective-permute-start.17 = (bf16[1024,128]{1,0:T(8,128)(2,1)S(1)}, bf16[1024,128]{1,0:T(8,128)(2,1)S(1)}, u32[]{:S(2)}, u32[]{:S(2)}) collective-permute-start(bf16[1024,128]{1,0:T(8,128)(2,1)S(1)} %get-tuple-element.56), channel_id=1, source_target_pairs={{17,18},{19,20},{21,22},{23,24},{25,26},{27,28},{29,30},{18,17},{2... | collective-permute-start | bytes 786440 | tf_op jit(solution)/shard_map/ppermute | solution.py:405
  46.4 15.6 %collective-permute-start.10 = (bf16[1024,128]{1,0:T(8,128)(2,1)S(1)}, bf16[1024,128]{1,0:T(8,128)(2,1)S(1)}, u32[]{:S(2)}, u32[]{:S(2)}) collective-permute-start(bf16[1024,128]{1,0:T(8,128)(2,1)S(1)} %get-tuple-element.47), channel_id=1, source_target_pairs={{17,18},{19,20},{21,22},{23,24},{25,26},{27,28},{29,30},{18,17},{2... | collective-permute-start | bytes 786440 | tf_op jit(solution)/shard_map/ppermute | solution.py:405
  55.1 10.1 %collective-permute-start.12 = (bf16[1024,128]{1,0:T(8,128)(2,1)S(1)}, bf16[1024,128]{1,0:T(8,128)(2,1)S(1)}, u32[]{:S(2)}, u32[]{:S(2)}) collective-permute-start(bf16[1024,128]{1,0:T(8,128)(2,1)S(1)} %get-tuple-element.50), channel_id=1, source_target_pairs={{0,1},{1,0},{2,3},{3,2},{4,5},{5,4},{6,7},{7,6},{8,9},{9,8},{10,11... | collective-permute-start | bytes 786440 | tf_op jit(solution)/shard_map/ppermute | solution.py:408
  56.5 8.5 %collective-permute-start.9 = (bf16[1024,128]{1,0:T(8,128)(2,1)S(1)}, bf16[1024,128]{1,0:T(8,128)(2,1)S(1)}, u32[]{:S(2)}, u32[]{:S(2)}) collective-permute-start(bf16[1024,128]{1,0:T(8,128)(2,1)S(1)} %get-tuple-element.46), channel_id=1, source_target_pairs={{0,1},{1,0},{2,3},{3,2},{4,5},{5,4},{6,7},{7,6},{8,9},{9,8},{10,11... | collective-permute-start | bytes 786440 | tf_op jit(solution)/shard_map/ppermute | solution.py:408
  58.9 13.3 %collective-permute-start.13 = (bf16[1024,128]{1,0:T(8,128)(2,1)S(1)}, bf16[1024,128]{1,0:T(8,128)(2,1)S(1)}, u32[]{:S(2)}, u32[]{:S(2)}) collective-permute-start(bf16[1024,128]{1,0:T(8,128)(2,1)S(1)} %get-tuple-element.51), channel_id=1, source_target_pairs={{17,18},{19,20},{21,22},{23,24},{25,26},{27,28},{29,30},{18,17},{2... | collective-permute-start | bytes 786440 | tf_op jit(solution)/shard_map/ppermute | solution.py:405
  60.8 12.4 %collective-permute-start.5 = (bf16[1024,128]{1,0:T(8,128)(2,1)S(1)}, bf16[1024,128]{1,0:T(8,128)(2,1)S(1)}, u32[]{:S(2)}, u32[]{:S(2)}) collective-permute-start(bf16[1024,128]{1,0:T(8,128)(2,1)S(1)} %get-tuple-element.41), channel_id=1, source_target_pairs={{0,1},{1,0},{2,3},{3,2},{4,5},{5,4},{6,7},{7,6},{8,9},{9,8},{10,11... | collective-permute-start | bytes 786440 | tf_op jit(solution)/shard_map/ppermute | solution.py:408
  62.0 13.0 %collective-permute-start.6 = (bf16[1024,128]{1,0:T(8,128)(2,1)S(1)}, bf16[1024,128]{1,0:T(8,128)(2,1)S(1)}, u32[]{:S(2)}, u32[]{:S(2)}) collective-permute-start(bf16[1024,128]{1,0:T(8,128)(2,1)S(1)} %get-tuple-element.42), channel_id=1, source_target_pairs={{17,18},{19,20},{21,22},{23,24},{25,26},{27,28},{29,30},{18,17},{2... | collective-permute-start | bytes 786440 | tf_op jit(solution)/shard_map/ppermute | solution.py:405

commit v3 on v2

--- a/solution.py
+++ b/solution.py
@@ -250,30 +250,29 @@
     )(*index, sources, tiles, operand)
 
 
-def prepare_kernel(wave, front, part, sources, sums, source_v, sem):
+def prepare_kernel(wave, front, part, blocks, sources, sums, source_v, sem):
     rows_dev, width = source_v.shape
+    tile_size, packed = rows_dev // blocks, rows_dev // 2
+    half = tile_size // 2
 
     @pl.when(lax.axis_index("layer") == wave)
     def _():
         copy = pltpu.make_async_copy(sources.at[0, front], source_v, sem)
         copy.start()
-        side = jnp.zeros((rows_dev, width), jnp.float32)
-        sums[pl.ds(0, rows_dev), :] = side
-        sums[pl.ds(2 * rows_dev, sums.shape[0] - 2 * rows_dev), :] = jnp.zeros(
-            (sums.shape[0] - 2 * rows_dev, width), jnp.float32
-        )
+        rest = sums.shape[0] - 2 * packed
+        sums[pl.ds(0, packed), :] = jnp.zeros((packed, width), jnp.float32)
+        sums[pl.ds(2 * packed, rest), :] = jnp.zeros((rest, width), jnp.float32)
         copy.wait()
-        source = source_v[...].astype(jnp.float32)
-        if part > 0:
-            source = pltpu.roll(source, width - width // 4, 1)
-        sums[pl.ds(rows_dev, rows_dev), :] = source
+        for r in range(blocks):
+            source = source_v[pl.ds(r * tile_size, tile_size), :].astype(jnp.float32)
+            sums[pl.ds(packed + r * half, half), :] = pack(source, part)
 
 
 def prepare(wave, front, part, sources, tile_size):
     rows_dev, width = sources.shape[-2:]
     return pl.pallas_call(
-        functools.partial(prepare_kernel, wave, front, part),
-        out_shape=pltpu.VMEM((3 * rows_dev + tile_size, width), jnp.float32),
+        functools.partial(prepare_kernel, wave, front, part, rows_dev // tile_size),
+        out_shape=pltpu.VMEM(((3 * rows_dev + tile_size) // 2, width), jnp.float32),
         in_specs=[HBM],
         out_specs=VMEM,
         scratch_shapes=[pltpu.VMEM((rows_dev, width), jnp.bfloat16), pltpu.SemaphoreType.DMA(())],
@@ -282,85 +281,95 @@
 
 
 def chunk_kernel(wave, blocks, *refs):
-    index_refs, (inbound, tiles, _, outer_ref, inner_ref, own_ref, sums) = refs[:3], refs[3:10]
-    rows_s, cols_s, pair, sems = refs[10:]
+    rows_s, cols_s, count_s, inbound, tiles, _, outer_ref, inner_ref, sums, operand = refs
     tile_size = tiles.shape[-1]
-    rows_dev, width = pair.shape[1:]
+    packed, width = inbound.shape
     half = tile_size // 2
+    first = quarters((half, width))
 
     @pl.when(lax.axis_index("layer") == wave)
     def _():
-        copies = [
-            pltpu.make_async_copy(index_refs[0], rows_s, sems.at[0]),
-            pltpu.make_async_copy(index_refs[1], cols_s, sems.at[1]),
-        ]
-        for copy in copies:
-            copy.start()
         for r in range(blocks):
-            upper = inbound[pl.ds(r * half, half), :].astype(jnp.float32)
-            lower = pltpu.roll(upper, width - width // 4, 1)
-            for j, value in enumerate((upper, lower)):
-                rows = pl.ds(r * tile_size + j * half, half)
-                pair[0, rows, :] = value.astype(jnp.bfloat16)
-                pair[1, rows, :] = turn(value).astype(jnp.bfloat16)
-        for copy in copies:
-            copy.wait()
-        accumulate(index_refs, rows_s, cols_s, tiles, pair, sums, blocks)
-        inner_start, outer_start = side_starts(rows_dev)
-        for r in range(blocks):
-            rows = pl.ds(r * half, half)
-            outer_ref[rows, :] = pack(read_block(sums, outer_start, r, tile_size), 0).astype(jnp.bfloat16)
-            inner_ref[rows, :] = pack(read_block(sums, inner_start, r, tile_size), 0).astype(jnp.bfloat16)
-            own_ref[rows, :] = pack(read_block(sums, rows_dev, r, tile_size), 0)
+            value = inbound[pl.ds(r * half, half), :].astype(jnp.float32)
+            for j, given in enumerate((value, turn(value))):
+                upper = jnp.where(first, given, 0.0)
+                lower = jnp.where(first, 0.0, given)
+                parts = (
+                    upper,
+                    pltpu.roll(lower, width - width // 4, 1),
+                    pltpu.roll(upper, width // 4, 1),
+                    lower,
+                )
+                for k, part in enumerate(parts):
+                    rows = pl.ds((8 * r + 4 * j + k) * half, half)
+                    operand[rows, :] = part.astype(jnp.bfloat16)
+        start = (lax.axis_index("tile") - 1) * blocks
+        count = count_s[0, 0]
+        for i in range(tiles.shape[0]):
+            live = i < count
+            row = jnp.where(live, rows_s[0, i] - start, 3 * blocks)
+            column = jnp.where(live, cols_s[0, i], 0)
+            rows = pl.ds(pl.multiple_of(column * 4 * tile_size, tile_size), 4 * tile_size)
+            target = pl.ds(pl.multiple_of(row * half, half), half)
+            left = jnp.concatenate(
+                [tiles[i, j, pl.ds(k * half, half), :] for j in range(2) for k in range(2)], axis=1
+            )
+            sums[target, :] += jnp.dot(left, operand[rows, :], preferred_element_type=jnp.float32)
+        inner_start, outer_start = side_starts(packed)
+        for ref, begin in ((outer_ref, outer_start), (inner_ref, inner_start)):
+            for r in range(blocks):
+                ref[pl.ds(r * half, half), :] = read_block(sums, begin, r, half).astype(jnp.bfloat16)
 
 
 def chunk_products(wave, front, part, inbound, tiles, sums, index, blocks):
-    slots, _, tile_size, _ = tiles.shape
-    rows_dev, width = blocks * tile_size, sums.shape[-1]
-    payload = pltpu.VMEM((rows_dev // 2, width), jnp.bfloat16)
+    tile_size = tiles.shape[-1]
+    packed, width = inbound.shape
+    payload = pltpu.VMEM((packed, width), jnp.bfloat16)
     return pl.pallas_call(
         functools.partial(chunk_kernel, wave, blocks),
-        out_shape=[payload, payload, pltpu.VMEM((rows_dev // 2, width), jnp.float32), pltpu.VMEM(sums.shape, sums.dtype)],
-        in_specs=[HBM, HBM, SMEM, VMEM, VMEM, VMEM],
-        out_specs=[VMEM] * 4,
-        scratch_shapes=[
-            pltpu.SMEM((1, slots), jnp.int32),
-            pltpu.SMEM((1, slots), jnp.int32),
-            pltpu.VMEM((2, rows_dev, width), jnp.bfloat16),
-            pltpu.SemaphoreType.DMA((2,)),
-        ],
-        input_output_aliases={5: 3},
+        out_shape=[payload, payload, pltpu.VMEM(sums.shape, sums.dtype)],
+        in_specs=[SMEM, SMEM, SMEM, VMEM, VMEM, VMEM],
+        out_specs=[VMEM] * 3,
+        scratch_shapes=[pltpu.VMEM((4 * blocks * tile_size, width), jnp.bfloat16)],
+        input_output_aliases={5: 2},
         **kernel_options(f"chunk_{wave}_{front}_{part}", 10**9, 5 * 10**6, 4),
     )(*index, inbound, tiles, sums)
 
 
 def combine_kernel(wave, part, has_through, final, *refs):
     own_ref, inner_ref, outer_ref = refs[:3]
-    packed, width = own_ref.shape
-    out_ref = refs[-1] if not has_through else refs[-2]
-    rows = pl.ds(part * packed if inner_ref.shape[0] > packed else 0, packed)
-    total = own_ref[...] + inner_ref[rows, :].astype(jnp.float32) + outer_ref[...].astype(jnp.float32)
+    packed, width = outer_ref.shape
+    own_rows = pl.ds(packed if own_ref.shape[0] > packed else 0, packed)
+    inner_rows = pl.ds(part * packed if inner_ref.shape[0] > packed else 0, packed)
+    total = own_ref[own_rows, :] + inner_ref[inner_rows, :].astype(jnp.float32) + outer_ref[...].astype(jnp.float32)
     if wave > 0:
         active = lax.axis_index("layer") == wave
         total = jnp.where(active, total, refs[3][...].astype(jnp.float32))
     if not (final and part == PARTS - 1):
+        out_ref = refs[-2] if has_through else refs[-1]
         out_ref[...] = total.astype(jnp.bfloat16)
         return
-    blocks, half = final
+    front, blocks, half = final
+    out_ref, staged, sems = refs[-3:]
     low, high = refs[4][...].astype(jnp.float32), total
     first = quarters((half, width))
+    copies = []
     for r in range(blocks):
         a, b = low[r * half : (r + 1) * half], high[r * half : (r + 1) * half]
         upper = jnp.where(first, a, pltpu.roll(b, width // 4, 1))
         lower = jnp.where(first, pltpu.roll(a, width - width // 4, 1), b)
-        out_ref[0, 0, pl.ds(2 * r * half, half), :] = upper.astype(jnp.bfloat16)
-        out_ref[0, 0, pl.ds((2 * r + 1) * half, half), :] = lower.astype(jnp.bfloat16)
+        staged[pl.ds(2 * r * half, half), :] = upper.astype(jnp.bfloat16)
+        staged[pl.ds((2 * r + 1) * half, half), :] = lower.astype(jnp.bfloat16)
+        rows = pl.ds(2 * r * half, 2 * half)
+        copies.append(pltpu.make_async_copy(staged.at[rows, :], out_ref.at[0, front, rows, :], sems.at[r]))
+        copies[-1].start()
+    for copy in copies:
+        copy.wait()
 
 
 def combine(wave, front, part, own, inner, outer, earlier=None, through=None, final=None, partner=None, result=None, fronts=0):
-    packed, width = own.shape
-    args, specs, aliases = [own, inner, outer], [VMEM] * 3, {}
-    grid = {}
+    packed, width = outer.shape
+    args, specs, aliases, scratch = [own, inner, outer], [VMEM] * 3, {}, []
     if wave > 0:
         args.append(earlier)
         specs.append(VMEM)
@@ -372,23 +381,24 @@
         outs.append(pltpu.VMEM(through.shape, through.dtype))
         out_specs.append(VMEM)
     if final and part == PARTS - 1:
-        grid = {"grid": (1,)}
+        final = (front, *final)
         args.append(partner)
         specs.append(VMEM)
         outs = [jax.ShapeDtypeStruct((1, fronts, 2 * packed, width), jnp.bfloat16)]
-        out_specs = [pl.BlockSpec((1, 1, 2 * packed, width), lambda i: (0, front, 0, 0))]
+        out_specs = [HBM]
+        scratch = [pltpu.VMEM((2 * packed, width), jnp.bfloat16), pltpu.SemaphoreType.DMA((final[1],))]
         if result is not None:
             aliases = {len(args): 0}
             args.append(result)
-            specs.append(pl.BlockSpec(memory_space=pl.ANY))
+            specs.append(HBM)
     return pl.pallas_call(
         functools.partial(combine_kernel, wave, part, through is not None, final),
         out_shape=outs,
         in_specs=specs,
         out_specs=out_specs,
+        scratch_shapes=scratch,
         input_output_aliases=aliases,
-        **grid,
-        **kernel_options(f"combine_{wave}_{front}_{part}", 10**6, 10**6, 12),
+        **kernel_options(f"combine_{wave}_{front}_{part}", 10**6, 10**6, 8),
     )(*args)
 
 
@@ -399,6 +409,8 @@
     tile_size = green_tiles.shape[-1]
     blocks = rows_dev // tile_size
     index = (in_hbm(tile_rows), in_hbm(tile_cols), tile_count)
+    resident = tuple(pltpu.with_memory_space_constraint(a, pltpu.SMEM) for a in (tile_rows, tile_cols))
+    resident = (*resident, tile_count)
     incident, sources, green_tiles = map(in_hbm, (incident, sources, green_tiles))
 
     def across(payload, wave):
@@ -438,8 +450,8 @@
         chunks = []
         for c, inbound in enumerate(passed):
             sums = prepare(wave, c // PARTS, c % PARTS, sources, tile_size)
-            outer, inner, own, _ = chunk_products(
-                wave, c // PARTS, c % PARTS, inbound, held, sums, index, blocks
+            outer, inner, own = chunk_products(
+                wave, c // PARTS, c % PARTS, inbound, held, sums, resident, blocks
             )
             chunks.append((own, beside(inner), across(outer, wave)))
         if final:

time: 77.1 us -> 76 us (0.986)
  Pallas kernels: 19.8 us -> 18.5 us
    pallas_call x4, Pallas kernels: 9.33 us -> 8.18 us  [chunk_products(): pl.pallas_call(functools.partial(chunk_kernel, wave, blocks), out_shape=[...]
  transfers between devices with their start and end apart: 18 -> 18, of which waited for: 2 -> 2; matrix products, arithmetic and copies ran while one was open for 0% -> 0% of each run, Pallas kernels for 21% -> 19%
where the time goes in v3:
time: 76 us; the launch traced here: 75 us
  starting transfers between devices  46.4 us (61%)
  Pallas kernels  18.5 us (24%)
  waiting for transfers between devices  8.94 us (12%)
  between operations  1.15 us (2%)
    ppermute x4, starting transfers between devices, down(): return lax.ppermute(payload, 'layer', layer_route)  30 us
    ppermute x8, starting transfers between devices, across(): return lax.ppermute(payload, ('layer', 'tile'), outer_route(wave, devices))  13.1 us
    ppermute x8, waiting for transfers between devices, across(): return lax.ppermute(payload, ('layer', 'tile'), outer_route(wave, devices))  8.92 us
    pallas_call x4, Pallas kernels, chunk_products(): pl.pallas_call(functools.partial(chunk_kernel, wave, blocks), out_shape=[...  8.18 us
    pallas_call x4, Pallas kernels, prepare(): pl.pallas_call(functools.partial(prepare_kernel, wave, front, part, rows_...  4.78 us
    ppermute x6, starting transfers between devices, beside(): return lax.ppermute(payload, 'tile', inner_route(devices))  3.31 us
    pallas_call x1, Pallas kernels, open_products(): pl.pallas_call(functools.partial(open_kernel, blocks), out_shape=[outer,...  2.93 us
    pallas_call x8, Pallas kernels, combine(): pl.pallas_call(functools.partial(combine_kernel, wave, part, through is n...  2.51 us
  transfers between devices with their start and end apart: 18, of which 2 were waited for; matrix products, arithmetic and copies ran while one was open for 0% of the time, Pallas kernels for 19%

profile of v3, /device:TPU:22, one launch (start us, length us, event | category | flops | bytes accessed | tf_op | source)
XLA Modules:
  0.0 75.0 jit_solution(11693670489379536278)
XLA Ops:
  0.7 2.9 %open.1 = (bf16[1024,128]{1,0:T(8,128)(2,1)S(1)}, bf16[1024,128]{1,0:T(8,128)(2,1)S(1)}, bf16[2,2048,128]{2,1,0:T(8,128)(2,1)S(1)}, bf16[12,2,256,256]{3,2,1,0:T(8,128)(2,1)S(1)}) custom-call(s32[1,12]{1,0:T(1,128)} %refs_0_.13, s32[1,12]{1,0:T(1,128)} %refs_1_.13, s32[1,1]{1,0:T(1,128)S(6)} %copy.19.refs_2_, bf16[2,2048,128]{2,1,0:T(8,128)(2,1)} %refs_5_.1, ...), custom_call_target="tpu_custom_call" | custom-call | flops 500000000 | bytes 4000000 | tf_op jit(solution)/shard_map/open/pallas_call | solution.py:151
  3.8 0.5 collective-permute-start
  4.3 0.7 collective-permute-start.2
  5.0 0.7 collective-permute-start.14
  5.7 0.7 collective-permute-start.7
  6.4 0.1 combine_0_0_1.1
  6.5 0.7 collective-permute-start.3
  7.2 0.1 combine_0_0_0.1.refs_3_
  7.3 25.2 %collective-permute-start.15 = (bf16[1024,128]{1,0:T(8,128)(2,1)S(1)}, bf16[1024,128]{1,0:T(8,128)(2,1)S(1)}, u32[]{:S(2)}, u32[]{:S(2)}) collective-permute-start(bf16[1024,128]{1,0:T(8,128)(2,1)S(1)} %combine_0_0_0.1.refs_3_), channel_id=1, source_target_pairs={{0,16},{16,0},{1,17},{17,1},{2,18},{18,2},{3,19},{19,3},{4,20},{20... | collective-permute-start | bytes 786440 | tf_op jit(solution)/shard_map/ppermute | solution.py:423
  32.5 2.7 %collective-permute-start.8 = (bf16[1024,128]{1,0:T(8,128)(2,1)S(1)}, bf16[1024,128]{1,0:T(8,128)(2,1)S(1)}, u32[]{:S(2)}, u32[]{:S(2)}) collective-permute-start(bf16[1024,128]{1,0:T(8,128)(2,1)S(1)} %combine_0_1_0.1.refs_3_), channel_id=1, source_target_pairs={{0,16},{16,0},{1,17},{17,1},{2,18},{18,2},{3,19},{19,3},{4,20},{20... | collective-permute-start | bytes 786440 | tf_op jit(solution)/shard_map/ppermute | solution.py:423
  35.2 1.2 %prepare_1_0_0.1.refs_5_ = f32[3200,128]{1,0:T(8,128)S(1)} custom-call(bf16[1,2,2048,128]{3,2,1,0:T(8,128)(2,1)} %sources.7), custom_call_target="tpu_custom_call" | custom-call | flops 1000000 | bytes 1000000 | tf_op jit(solution)/shard_map/prepare_1_0_0/pallas_call | solution.py:273
  36.5 1.2 %prepare_1_1_0.1.refs_5_ = f32[3200,128]{1,0:T(8,128)S(1)} custom-call(bf16[1,2,2048,128]{3,2,1,0:T(8,128)(2,1)} %sources.7), custom_call_target="tpu_custom_call" | custom-call | flops 1000000 | bytes 1000000 | tf_op jit(solution)/shard_map/prepare_1_1_0/pallas_call | solution.py:273
  37.9 2.1 %collective-permute-start.4 = (bf16[1024,128]{1,0:T(8,128)(2,1)S(1)}, bf16[1024,128]{1,0:T(8,128)(2,1)S(1)}, u32[]{:S(2)}, u32[]{:S(2)}) collective-permute-start(bf16[1024,128]{1,0:T(8,128)(2,1)S(1)} %combine_0_1_1.1.refs_3_), channel_id=1, source_target_pairs={{0,16},{16,0},{1,17},{17,1},{2,18},{18,2},{3,19},{19,3},{4,20},{20... | collective-permute-start | bytes 786440 | tf_op jit(solution)/shard_map/ppermute | solution.py:423
  39.9 2.0 %chunk_1_0_0.1 = (bf16[1024,128]{1,0:T(8,128)(2,1)S(1)}, bf16[1024,128]{1,0:T(8,128)(2,1)S(1)}, f32[3200,128]{1,0:T(8,128)S(1)}) custom-call(s32[1,12]{1,0:T(1,128)S(1)} %copy-done, s32[1,12]{1,0:T(1,128)S(1)} %copy-done.1, s32[1,1]{1,0:T(1,128)S(6)} %copy.19.refs_2_, ...), custom_call_target="tpu_custom_call", output_to_operand_aliasing={{2}: (5, {})} | custom-call | flops 1000000000 | bytes 5000000 | tf_op jit(solution)/shard_map/chunk_1_0_0/pallas_call | solution.py:328
  42.0 1.9 %collective-permute-start.17 = (bf16[1024,128]{1,0:T(8,128)(2,1)S(1)}, bf16[1024,128]{1,0:T(8,128)(2,1)S(1)}, u32[]{:S(2)}, u32[]{:S(2)}) collective-permute-start(bf16[1024,128]{1,0:T(8,128)(2,1)S(1)} %get-tuple-element.56), channel_id=1, source_target_pairs={{17,18},{19,20},{21,22},{23,24},{25,26},{27,28},{29,30},{18,17},{2... | collective-permute-start | bytes 786440 | tf_op jit(solution)/shard_map/ppermute | solution.py:417
  44.0 2.0 %chunk_1_1_0.1 = (bf16[1024,128]{1,0:T(8,128)(2,1)S(1)}, bf16[1024,128]{1,0:T(8,128)(2,1)S(1)}, f32[3200,128]{1,0:T(8,128)S(1)}) custom-call(s32[1,12]{1,0:T(1,128)S(1)} %copy-done, s32[1,12]{1,0:T(1,128)S(1)} %copy-done.1, s32[1,1]{1,0:T(1,128)S(6)} %copy.19.refs_2_, ...), custom_call_target="tpu_custom_call", output_to_operand_aliasing={{2}: (5, {})} | custom-call | flops 1000000000 | bytes 5000000 | tf_op jit(solution)/shard_map/chunk_1_1_0/pallas_call | solution.py:328
  46.0 3.6 %collective-permute-start.10 = (bf16[1024,128]{1,0:T(8,128)(2,1)S(1)}, bf16[1024,128]{1,0:T(8,128)(2,1)S(1)}, u32[]{:S(2)}, u32[]{:S(2)}) collective-permute-start(bf16[1024,128]{1,0:T(8,128)(2,1)S(1)} %get-tuple-element.47), channel_id=1, source_target_pairs={{17,18},{19,20},{21,22},{23,24},{25,26},{27,28},{29,30},{18,17},{2... | collective-permute-start | bytes 786440 | tf_op jit(solution)/shard_map/ppermute | solution.py:417
  49.6 1.2 %prepare_1_0_1.1.refs_5_ = f32[3200,128]{1,0:T(8,128)S(1)} custom-call(bf16[1,2,2048,128]{3,2,1,0:T(8,128)(2,1)} %sources.7), custom_call_target="tpu_custom_call" | custom-call | flops 1000000 | bytes 1000000 | tf_op jit(solution)/shard_map/prepare_1_0_1/pallas_call | solution.py:273
  50.8 1.2 %prepare_1_1_1.1.refs_5_ = f32[3200,128]{1,0:T(8,128)S(1)} custom-call(bf16[1,2,2048,128]{3,2,1,0:T(8,128)(2,1)} %sources.7), custom_call_target="tpu_custom_call" | custom-call | flops 1000000 | bytes 1000000 | tf_op jit(solution)/shard_map/prepare_1_1_1/pallas_call | solution.py:273
  52.0 2.0 %chunk_1_0_1.1 = (bf16[1024,128]{1,0:T(8,128)(2,1)S(1)}, bf16[1024,128]{1,0:T(8,128)(2,1)S(1)}, f32[3200,128]{1,0:T(8,128)S(1)}) custom-call(s32[1,12]{1,0:T(1,128)S(1)} %copy-done, s32[1,12]{1,0:T(1,128)S(1)} %copy-done.1, s32[1,1]{1,0:T(1,128)S(6)} %copy.19.refs_2_, ...), custom_call_target="tpu_custom_call", output_to_operand_aliasing={{2}: (5, {})} | custom-call | flops 1000000000 | bytes 5000000 | tf_op jit(solution)/shard_map/chunk_1_0_1/pallas_call | solution.py:328
  54.0 1.4 %collective-permute-start.12 = (bf16[1024,128]{1,0:T(8,128)(2,1)S(1)}, bf16[1024,128]{1,0:T(8,128)(2,1)S(1)}, u32[]{:S(2)}, u32[]{:S(2)}) collective-permute-start(bf16[1024,128]{1,0:T(8,128)(2,1)S(1)} %get-tuple-element.50), channel_id=1, source_target_pairs={{0,1},{1,0},{2,3},{3,2},{4,5},{5,4},{6,7},{7,6},{8,9},{9,8},{10,11... | collective-permute-start | bytes 786440 | tf_op jit(solution)/shard_map/ppermute | solution.py:420
  55.5 0.1 collective-permute-start.9
  55.6 2.2 %chunk_1_1_1.1 = (bf16[1024,128]{1,0:T(8,128)(2,1)S(1)}, bf16[1024,128]{1,0:T(8,128)(2,1)S(1)}, f32[3200,128]{1,0:T(8,128)S(1)}) custom-call(s32[1,12]{1,0:T(1,128)S(1)} %copy-done, s32[1,12]{1,0:T(1,128)S(1)} %copy-done.1, s32[1,1]{1,0:T(1,128)S(6)} %copy.19.refs_2_, ...), custom_call_target="tpu_custom_call", output_to_operand_aliasing={{2}: (5, {})} | custom-call | flops 1000000000 | bytes 5000000 | tf_op jit(solution)/shard_map/chunk_1_1_1/pallas_call | solution.py:328
  57.8 1.9 %collective-permute-start.13 = (bf16[1024,128]{1,0:T(8,128)(2,1)S(1)}, bf16[1024,128]{1,0:T(8,128)(2,1)S(1)}, u32[]{:S(2)}, u32[]{:S(2)}) collective-permute-start(bf16[1024,128]{1,0:T(8,128)(2,1)S(1)} %get-tuple-element.51), channel_id=1, source_target_pairs={{17,18},{19,20},{21,22},{23,24},{25,26},{27,28},{29,30},{18,17},{2... | collective-permute-start | bytes 786440 | tf_op jit(solution)/shard_map/ppermute | solution.py:417
  59.7 1.1 %collective-permute-start.5 = (bf16[1024,128]{1,0:T(8,128)(2,1)S(1)}, bf16[1024,128]{1,0:T(8,128)(2,1)S(1)}, u32[]{:S(2)}, u32[]{:S(2)}) collective-permute-start(bf16[1024,128]{1,0:T(8,128)(2,1)S(1)} %get-tuple-element.41), channel_id=1, source_target_pairs={{0,1},{1,0},{2,3},{3,2},{4,5},{5,4},{6,7},{7,6},{8,9},{9,8},{10,11... | collective-permute-start | bytes 786440 | tf_op jit(solution)/shard_map/ppermute | solution.py:420
  60.8 2.9 %collective-permute-start.6 = (bf16[1024,128]{1,0:T(8,128)(2,1)S(1)}, bf16[1024,128]{1,0:T(8,128)(2,1)S(1)}, u32[]{:S(2)}, u32[]{:S(2)}) collective-permute-start(bf16[1024,128]{1,0:T(8,128)(2,1)S(1)} %get-tuple-element.42), channel_id=1, source_target_pairs={{17,18},{19,20},{21,22},{23,24},{25,26},{27,28},{29,30},{18,17},{2... | collective-permute-start | bytes 786440 | tf_op jit(solution)/shard_map/ppermute | solution.py:417
  63.7 0.1 combine_1_0_0.1.refs_4_
  63.9 0.1 combine_1_1_0.1.refs_4_
  64.0 7.1 %collective-permute-done.13.refs_2_ = bf16[1024,128]{1,0:T(8,128)(2,1)S(1)} collective-permute-done((bf16[1024,128]{1,0:T(8,128)(2,1)S(1)}, bf16[1024,128]{1,0:T(8,128)(2,1)S(1)}, u32[]{:S(2)}, u32[]{:S(2)}) %collective-permute-start.13) | collective-permute-done | bytes 262176 | tf_op jit(solution)/shard_map/ppermute | solution.py:417
  71.1 1.0 %combine_1_0_1.1.refs_5_ = bf16[1,2,2048,128]{3,2,1,0:T(8,128)(2,1)} custom-call(f32[3200,128]{1,0:T(8,128)S(1)} %get-tuple-element.49.refs_0_, bf16[1024,128]{1,0:T(8,128)(2,1)S(1)} %collective-permute-done.12.refs_1_, bf16[1024,128]{1,0:T(8,128)(2,1)S(1)} %collective-permute-done.13.refs_2_, bf16[1024,128]{1,0:T(8,128)(2,1)S(1)} %get-tuple-element.48.refs_3_, ...), custom_call_target="tpu_custom_call" | custom-call | flops 1000000 | bytes 1000000 | tf_op jit(solution)/shard_map/combine_1_0_1/pallas_call | solution.py:394
  72.1 1.8 %collective-permute-done.6.refs_2_ = bf16[1024,128]{1,0:T(8,128)(2,1)S(1)} collective-permute-done((bf16[1024,128]{1,0:T(8,128)(2,1)S(1)}, bf16[1024,128]{1,0:T(8,128)(2,1)S(1)}, u32[]{:S(2)}, u32[]{:S(2)}) %collective-permute-start.6) | collective-permute-done | bytes 262176 | tf_op jit(solution)/shard_map/ppermute | solution.py:417
  73.9 1.0 %combine_1_1_1.1 = bf16[1,2,2048,128]{3,2,1,0:T(8,128)(2,1)} custom-call(f32[3200,128]{1,0:T(8,128)S(1)} %get-tuple-element.40.refs_0_, bf16[1024,128]{1,0:T(8,128)(2,1)S(1)} %collective-permute-done.5.refs_1_, bf16[1024,128]{1,0:T(8,128)(2,1)S(1)} %collective-permute-done.6.refs_2_, ...), custom_call_target="tpu_custom_call", output_to_operand_aliasing={{}: (5, {})} | custom-call | flops 1000000 | bytes 1000000 | tf_op jit(solution)/shard_map/combine_1_1_1/pallas_call | solution.py:394
  (27 shorter events, 0.5 us)
Async XLA Ops:
  3.7 2.7 %collective-permute-start.1 = (bf16[2048,128]{1,0:T(8,128)(2,1)S(1)}, bf16[2048,128]{1,0:T(8,128)(2,1)S(1)}, u32[]{:S(2)}, u32[]{:S(2)}) collective-permute-start(bf16[2048,128]{1,0:T(8,128)(2,1)S(1)} %get-tuple-element.36), channel_id=1, source_target_pairs={{0,1},{1,0},{2,3},{3,2},{4,5},{5,4},{6,7},{7,6},{8,9},{9,8},{10,11... | collective-permute-start | bytes 1572872 | tf_op jit(solution)/shard_map/ppermute | solution.py:420
  3.8 28.6 %collective-permute-start = (bf16[2048,128]{1,0:T(8,128)(2,1)S(1)}, bf16[2048,128]{1,0:T(8,128)(2,1)S(1)}, u32[]{:S(2)}, u32[]{:S(2)}) collective-permute-start(bf16[2048,128]{1,0:T(8,128)(2,1)S(1)} %get-tuple-element.33), channel_id=1, source_target_pairs={{0,1},{1,0},{2,3},{3,2},{4,5},{5,4},{6,7},{7,6},{8,9},{9,8},{10,11... | collective-permute-start | bytes 1572872 | tf_op jit(solution)/shard_map/ppermute | solution.py:420
  4.3 2.0 %collective-permute-start.2 = (bf16[1024,128]{1,0:T(8,128)(2,1)S(1)}, bf16[1024,128]{1,0:T(8,128)(2,1)S(1)}, u32[]{:S(2)}, u32[]{:S(2)}) collective-permute-start(bf16[1024,128]{1,0:T(8,128)(2,1)S(1)} %get-tuple-element.37), channel_id=1, source_target_pairs={{1,2},{3,4},{5,6},{7,8},{9,10},{11,12},{13,14},{2,1},{4,3},{6,5},{... | collective-permute-start | bytes 786440 | tf_op jit(solution)/shard_map/ppermute | solution.py:417
  5.0 2.2 %collective-permute-start.14 = (bf16[1024,128]{1,0:T(8,128)(2,1)S(1)}, bf16[1024,128]{1,0:T(8,128)(2,1)S(1)}, u32[]{:S(2)}, u32[]{:S(2)}) collective-permute-start(bf16[1024,128]{1,0:T(8,128)(2,1)S(1)} %get-tuple-element.53), channel_id=1, source_target_pairs={{1,2},{3,4},{5,6},{7,8},{9,10},{11,12},{13,14},{2,1},{4,3},{6,5},{... | collective-permute-start | bytes 786440 | tf_op jit(solution)/shard_map/ppermute | solution.py:417
  5.7 26.7 %collective-permute-start.7 = (bf16[1024,128]{1,0:T(8,128)(2,1)S(1)}, bf16[1024,128]{1,0:T(8,128)(2,1)S(1)}, u32[]{:S(2)}, u32[]{:S(2)}) collective-permute-start(bf16[1024,128]{1,0:T(8,128)(2,1)S(1)} %get-tuple-element.44), channel_id=1, source_target_pairs={{1,2},{3,4},{5,6},{7,8},{9,10},{11,12},{13,14},{2,1},{4,3},{6,5},{... | collective-permute-start | bytes 786440 | tf_op jit(solution)/shard_map/ppermute | solution.py:417
  6.5 31.3 %collective-permute-start.3 = (bf16[1024,128]{1,0:T(8,128)(2,1)S(1)}, bf16[1024,128]{1,0:T(8,128)(2,1)S(1)}, u32[]{:S(2)}, u32[]{:S(2)}) collective-permute-start(bf16[1024,128]{1,0:T(8,128)(2,1)S(1)} %get-tuple-element.39), channel_id=1, source_target_pairs={{1,2},{3,4},{5,6},{7,8},{9,10},{11,12},{13,14},{2,1},{4,3},{6,5},{... | collective-permute-start | bytes 786440 | tf_op jit(solution)/shard_map/ppermute | solution.py:417
  7.3 32.6 %collective-permute-start.15 = (bf16[1024,128]{1,0:T(8,128)(2,1)S(1)}, bf16[1024,128]{1,0:T(8,128)(2,1)S(1)}, u32[]{:S(2)}, u32[]{:S(2)}) collective-permute-start(bf16[1024,128]{1,0:T(8,128)(2,1)S(1)} %combine_0_0_0.1.refs_3_), channel_id=1, source_target_pairs={{0,16},{16,0},{1,17},{17,1},{2,18},{18,2},{3,19},{19,3},{4,20},{20... | collective-permute-start | bytes 786440 | tf_op jit(solution)/shard_map/ppermute | solution.py:423
  32.5 11.4 %collective-permute-start.8 = (bf16[1024,128]{1,0:T(8,128)(2,1)S(1)}, bf16[1024,128]{1,0:T(8,128)(2,1)S(1)}, u32[]{:S(2)}, u32[]{:S(2)}) collective-permute-start(bf16[1024,128]{1,0:T(8,128)(2,1)S(1)} %combine_0_1_0.1.refs_3_), channel_id=1, source_target_pairs={{0,16},{16,0},{1,17},{17,1},{2,18},{18,2},{3,19},{19,3},{4,20},{20... | collective-permute-start | bytes 786440 | tf_op jit(solution)/shard_map/ppermute | solution.py:423
  36.4 3.5 %copy-start = (s32[1,12]{1,0:T(1,128)S(1)}, s32[1,12]{1,0:T(1,128)}, u32[]{:S(2)}) copy-start(s32[1,12]{1,0:T(1,128)} %refs_0_.13) | copy-start | bytes 148
  36.5 3.5 %copy-start.1 = (s32[1,12]{1,0:T(1,128)S(1)}, s32[1,12]{1,0:T(1,128)}, u32[]{:S(2)}) copy-start(s32[1,12]{1,0:T(1,128)} %refs_1_.13) | copy-start | bytes 148
  37.7 14.4 %collective-permute-start.11 = (bf16[1024,128]{1,0:T(8,128)(2,1)S(1)}, bf16[1024,128]{1,0:T(8,128)(2,1)S(1)}, u32[]{:S(2)}, u32[]{:S(2)}) collective-permute-start(bf16[1024,128]{1,0:T(8,128)(2,1)S(1)} %get-tuple-element.48.refs_3_), channel_id=1, source_target_pairs={{0,16},{16,0},{1,17},{17,1},{2,18},{18,2},{3,19},{19,3},{4,20},{20... | collective-permute-start | bytes 786440 | tf_op jit(solution)/shard_map/ppermute | solution.py:423
  37.9 17.6 %collective-permute-start.4 = (bf16[1024,128]{1,0:T(8,128)(2,1)S(1)}, bf16[1024,128]{1,0:T(8,128)(2,1)S(1)}, u32[]{:S(2)}, u32[]{:S(2)}) collective-permute-start(bf16[1024,128]{1,0:T(8,128)(2,1)S(1)} %combine_0_1_1.1.refs_3_), channel_id=1, source_target_pairs={{0,16},{16,0},{1,17},{17,1},{2,18},{18,2},{3,19},{19,3},{4,20},{20... | collective-permute-start | bytes 786440 | tf_op jit(solution)/shard_map/ppermute | solution.py:423
  41.9 15.8 %collective-permute-start.16 = (bf16[1024,128]{1,0:T(8,128)(2,1)S(1)}, bf16[1024,128]{1,0:T(8,128)(2,1)S(1)}, u32[]{:S(2)}, u32[]{:S(2)}) collective-permute-start(bf16[1024,128]{1,0:T(8,128)(2,1)S(1)} %get-tuple-element.55), channel_id=1, source_target_pairs={{0,1},{1,0},{2,3},{3,2},{4,5},{5,4},{6,7},{7,6},{8,9},{9,8},{10,11... | collective-permute-start | bytes 786440 | tf_op jit(solution)/shard_map/ppermute | solution.py:420
  42.0 17.7 %collective-permute-start.17 = (bf16[1024,128]{1,0:T(8,128)(2,1)S(1)}, bf16[1024,128]{1,0:T(8,128)(2,1)S(1)}, u32[]{:S(2)}, u32[]{:S(2)}) collective-permute-start(bf16[1024,128]{1,0:T(8,128)(2,1)S(1)} %get-tuple-element.56), channel_id=1, source_target_pairs={{17,18},{19,20},{21,22},{23,24},{25,26},{27,28},{29,30},{18,17},{2... | collective-permute-start | bytes 786440 | tf_op jit(solution)/shard_map/ppermute | solution.py:417
  46.0 14.8 %collective-permute-start.10 = (bf16[1024,128]{1,0:T(8,128)(2,1)S(1)}, bf16[1024,128]{1,0:T(8,128)(2,1)S(1)}, u32[]{:S(2)}, u32[]{:S(2)}) collective-permute-start(bf16[1024,128]{1,0:T(8,128)(2,1)S(1)} %get-tuple-element.47), channel_id=1, source_target_pairs={{17,18},{19,20},{21,22},{23,24},{25,26},{27,28},{29,30},{18,17},{2... | collective-permute-start | bytes 786440 | tf_op jit(solution)/shard_map/ppermute | solution.py:417
  54.0 9.9 %collective-permute-start.12 = (bf16[1024,128]{1,0:T(8,128)(2,1)S(1)}, bf16[1024,128]{1,0:T(8,128)(2,1)S(1)}, u32[]{:S(2)}, u32[]{:S(2)}) collective-permute-start(bf16[1024,128]{1,0:T(8,128)(2,1)S(1)} %get-tuple-element.50), channel_id=1, source_target_pairs={{0,1},{1,0},{2,3},{3,2},{4,5},{5,4},{6,7},{7,6},{8,9},{9,8},{10,11... | collective-permute-start | bytes 786440 | tf_op jit(solution)/shard_map/ppermute | solution.py:420
  55.5 8.4 %collective-permute-start.9 = (bf16[1024,128]{1,0:T(8,128)(2,1)S(1)}, bf16[1024,128]{1,0:T(8,128)(2,1)S(1)}, u32[]{:S(2)}, u32[]{:S(2)}) collective-permute-start(bf16[1024,128]{1,0:T(8,128)(2,1)S(1)} %get-tuple-element.46), channel_id=1, source_target_pairs={{0,1},{1,0},{2,3},{3,2},{4,5},{5,4},{6,7},{7,6},{8,9},{9,8},{10,11... | collective-permute-start | bytes 786440 | tf_op jit(solution)/shard_map/ppermute | solution.py:420
  57.8 13.3 %collective-permute-start.13 = (bf16[1024,128]{1,0:T(8,128)(2,1)S(1)}, bf16[1024,128]{1,0:T(8,128)(2,1)S(1)}, u32[]{:S(2)}, u32[]{:S(2)}) collective-permute-start(bf16[1024,128]{1,0:T(8,128)(2,1)S(1)} %get-tuple-element.51), channel_id=1, source_target_pairs={{17,18},{19,20},{21,22},{23,24},{25,26},{27,28},{29,30},{18,17},{2... | collective-permute-start | bytes 786440 | tf_op jit(solution)/shard_map/ppermute | solution.py:417
  59.7 12.4 %collective-permute-start.5 = (bf16[1024,128]{1,0:T(8,128)(2,1)S(1)}, bf16[1024,128]{1,0:T(8,128)(2,1)S(1)}, u32[]{:S(2)}, u32[]{:S(2)}) collective-permute-start(bf16[1024,128]{1,0:T(8,128)(2,1)S(1)} %get-tuple-element.41), channel_id=1, source_target_pairs={{0,1},{1,0},{2,3},{3,2},{4,5},{5,4},{6,7},{7,6},{8,9},{9,8},{10,11... | collective-permute-start | bytes 786440 | tf_op jit(solution)/shard_map/ppermute | solution.py:420
  60.8 13.1 %collective-permute-start.6 = (bf16[1024,128]{1,0:T(8,128)(2,1)S(1)}, bf16[1024,128]{1,0:T(8,128)(2,1)S(1)}, u32[]{:S(2)}, u32[]{:S(2)}) collective-permute-start(bf16[1024,128]{1,0:T(8,128)(2,1)S(1)} %get-tuple-element.42), channel_id=1, source_target_pairs={{17,18},{19,20},{21,22},{23,24},{25,26},{27,28},{29,30},{18,17},{2... | collective-permute-start | bytes 786440 | tf_op jit(solution)/shard_map/ppermute | solution.py:417

commit v4 on v3

--- a/solution.py
+++ b/solution.py
@@ -19,9 +19,13 @@
     return [(i, i ^ 1) for i in range(devices)]
 
 
-def outer_route(wave, devices):
-    pairs = [(wave * devices + i, wave * devices + i + 1) for i in range(1, devices - 1, 2)]
-    return pairs + [(b, a) for a, b in pairs]
+def outer_route(wave, depth, devices):
+    pairs = []
+    for layer in range(depth):
+        for i in range(devices):
+            other = (i + 1 if i % 2 else i - 1) % devices if layer == wave else i ^ 1
+            pairs.append((layer * devices + i, layer * devices + other))
+    return pairs
 
 
 def down_route(depth):
@@ -281,7 +285,7 @@
 
 
 def chunk_kernel(wave, blocks, *refs):
-    rows_s, cols_s, count_s, inbound, tiles, _, outer_ref, inner_ref, sums, operand = refs
+    rows_ref, cols_ref, count_s, inbound, tiles, _, outer_ref, inner_ref, sums, operand, rows_s, cols_s, sems = refs
     tile_size = tiles.shape[-1]
     packed, width = inbound.shape
     half = tile_size // 2
@@ -289,6 +293,12 @@
 
     @pl.when(lax.axis_index("layer") == wave)
     def _():
+        copies = [
+            pltpu.make_async_copy(rows_ref, rows_s, sems.at[0]),
+            pltpu.make_async_copy(cols_ref, cols_s, sems.at[1]),
+        ]
+        for copy in copies:
+            copy.start()
         for r in range(blocks):
             value = inbound[pl.ds(r * half, half), :].astype(jnp.float32)
             for j, given in enumerate((value, turn(value))):
@@ -303,6 +313,8 @@
                 for k, part in enumerate(parts):
                     rows = pl.ds((8 * r + 4 * j + k) * half, half)
                     operand[rows, :] = part.astype(jnp.bfloat16)
+        for copy in copies:
+            copy.wait()
         start = (lax.axis_index("tile") - 1) * blocks
         count = count_s[0, 0]
         for i in range(tiles.shape[0]):
@@ -328,9 +340,14 @@
     return pl.pallas_call(
         functools.partial(chunk_kernel, wave, blocks),
         out_shape=[payload, payload, pltpu.VMEM(sums.shape, sums.dtype)],
-        in_specs=[SMEM, SMEM, SMEM, VMEM, VMEM, VMEM],
+        in_specs=[HBM, HBM, SMEM, VMEM, VMEM, VMEM],
         out_specs=[VMEM] * 3,
-        scratch_shapes=[pltpu.VMEM((4 * blocks * tile_size, width), jnp.bfloat16)],
+        scratch_shapes=[
+            pltpu.VMEM((4 * blocks * tile_size, width), jnp.bfloat16),
+            pltpu.SMEM((1, tiles.shape[0]), jnp.int32),
+            pltpu.SMEM((1, tiles.shape[0]), jnp.int32),
+            pltpu.SemaphoreType.DMA((2,)),
+        ],
         input_output_aliases={5: 2},
         **kernel_options(f"chunk_{wave}_{front}_{part}", 10**9, 5 * 10**6, 4),
     )(*index, inbound, tiles, sums)
@@ -409,12 +426,10 @@
     tile_size = green_tiles.shape[-1]
     blocks = rows_dev // tile_size
     index = (in_hbm(tile_rows), in_hbm(tile_cols), tile_count)
-    resident = tuple(pltpu.with_memory_space_constraint(a, pltpu.SMEM) for a in (tile_rows, tile_cols))
-    resident = (*resident, tile_count)
     incident, sources, green_tiles = map(in_hbm, (incident, sources, green_tiles))
 
     def across(payload, wave):
-        return lax.ppermute(payload, ("layer", "tile"), outer_route(wave, devices))
+        return lax.ppermute(payload, ("layer", "tile"), outer_route(wave, depth, devices))
 
     def beside(payload):
         return lax.ppermute(payload, "tile", inner_route(devices))
@@ -451,7 +466,7 @@
         for c, inbound in enumerate(passed):
             sums = prepare(wave, c // PARTS, c % PARTS, sources, tile_size)
             outer, inner, own = chunk_products(
-                wave, c // PARTS, c % PARTS, inbound, held, sums, resident, blocks
+                wave, c // PARTS, c % PARTS, inbound, held, sums, index, blocks
             )
             chunks.append((own, beside(inner), across(outer, wave)))
         if final:

time: 76 us -> 71.2 us (0.937)
  the two profiles are of different devices: /device:TPU:22 before, /device:TPU:3 now
where the time goes in v4:
time: 71.2 us; the launch traced here: 70.8 us
  starting transfers between devices  39.9 us (56%)
  Pallas kernels  19.6 us (28%)
  waiting for transfers between devices  10.3 us (14%)
  between operations  1.02 us (1%)
    ppermute x4, starting transfers between devices, down(): return lax.ppermute(payload, 'layer', layer_route)  27.7 us
    ppermute x8, waiting for transfers between devices, across(): lax.ppermute(payload, ('layer', 'tile'), outer_route(wave, depth, devices))  9.76 us
    pallas_call x4, Pallas kernels, chunk_products(): pl.pallas_call(functools.partial(chunk_kernel, wave, blocks), out_shape=[...  9.27 us
    ppermute x6, starting transfers between devices, beside(): return lax.ppermute(payload, 'tile', inner_route(devices))  8.2 us
    pallas_call x4, Pallas kernels, prepare(): pl.pallas_call(functools.partial(prepare_kernel, wave, front, part, rows_...  4.78 us
    ppermute x8, starting transfers between devices, across(): lax.ppermute(payload, ('layer', 'tile'), outer_route(wave, depth, devices))  3.99 us
    pallas_call x1, Pallas kernels, open_products(): pl.pallas_call(functools.partial(open_kernel, blocks), out_shape=[outer,...  2.93 us
    pallas_call x8, Pallas kernels, combine(): pl.pallas_call(functools.partial(combine_kernel, wave, part, through is n...  2.5 us
  transfers between devices with their start and end apart: 18, of which 4 were waited for; matrix products, arithmetic and copies ran while one was open for 0% of the time, Pallas kernels for 22%

profile of v4, /device:TPU:3, one launch (start us, length us, event | category | flops | bytes accessed | tf_op | source)
XLA Modules:
  0.0 70.8 jit_solution(8001686525607798133)
XLA Ops:
  0.7 2.9 %open.1 = (bf16[1024,128]{1,0:T(8,128)(2,1)S(1)}, bf16[1024,128]{1,0:T(8,128)(2,1)S(1)}, bf16[2,2048,128]{2,1,0:T(8,128)(2,1)S(1)}, bf16[12,2,256,256]{3,2,1,0:T(8,128)(2,1)S(1)}) custom-call(s32[1,12]{1,0:T(1,128)} %refs_0_.13, s32[1,12]{1,0:T(1,128)} %refs_1_.13, s32[1,1]{1,0:T(1,128)S(6)} %copy.19.refs_2_, bf16[2,2048,128]{2,1,0:T(8,128)(2,1)} %refs_5_.1, ...), custom_call_target="tpu_custom_call" | custom-call | flops 500000000 | bytes 4000000 | tf_op jit(solution)/shard_map/open/pallas_call | solution.py:155
  3.7 0.7 %collective-permute-start.1 = (bf16[2048,128]{1,0:T(8,128)(2,1)S(1)}, bf16[2048,128]{1,0:T(8,128)(2,1)S(1)}, u32[]{:S(2)}, u32[]{:S(2)}) collective-permute-start(bf16[2048,128]{1,0:T(8,128)(2,1)S(1)} %get-tuple-element.36), channel_id=1, source_target_pairs={{0,1},{1,0},{2,3},{3,2},{4,5},{5,4},{6,7},{7,6},{8,9},{9,8},{10,11... | collective-permute-start | bytes 1572872 | tf_op jit(solution)/shard_map/ppermute | solution.py:435
  4.4 0.1 collective-permute-start
  4.5 0.5 collective-permute-start.2
  5.1 0.4 collective-permute-start.7
  5.5 1.5 %collective-permute-done.2.refs_2_ = bf16[1024,128]{1,0:T(8,128)(2,1)S(1)} collective-permute-done((bf16[1024,128]{1,0:T(8,128)(2,1)S(1)}, bf16[1024,128]{1,0:T(8,128)(2,1)S(1)}, u32[]{:S(2)}, u32[]{:S(2)}) %collective-permute-start.2) | collective-permute-done | bytes 262176 | tf_op jit(solution)/shard_map/ppermute | solution.py:432
  7.1 0.4 collective-permute-start.3
  7.7 23.4 %collective-permute-start.15 = (bf16[1024,128]{1,0:T(8,128)(2,1)S(1)}, bf16[1024,128]{1,0:T(8,128)(2,1)S(1)}, u32[]{:S(2)}, u32[]{:S(2)}) collective-permute-start(bf16[1024,128]{1,0:T(8,128)(2,1)S(1)} %combine_0_0_0.1.refs_3_), channel_id=1, source_target_pairs={{0,16},{16,0},{1,17},{17,1},{2,18},{18,2},{3,19},{19,3},{4,20},{20... | collective-permute-start | bytes 786440 | tf_op jit(solution)/shard_map/ppermute | solution.py:438
  31.1 0.1 combine_0_1_0.1.refs_3_
  31.2 2.7 %collective-permute-start.8 = (bf16[1024,128]{1,0:T(8,128)(2,1)S(1)}, bf16[1024,128]{1,0:T(8,128)(2,1)S(1)}, u32[]{:S(2)}, u32[]{:S(2)}) collective-permute-start(bf16[1024,128]{1,0:T(8,128)(2,1)S(1)} %combine_0_1_0.1.refs_3_), channel_id=1, source_target_pairs={{0,16},{16,0},{1,17},{17,1},{2,18},{18,2},{3,19},{19,3},{4,20},{20... | collective-permute-start | bytes 786440 | tf_op jit(solution)/shard_map/ppermute | solution.py:438
  33.9 1.2 %prepare_1_0_0.1.refs_5_ = f32[3200,128]{1,0:T(8,128)S(1)} custom-call(bf16[1,2,2048,128]{3,2,1,0:T(8,128)(2,1)} %sources.7), custom_call_target="tpu_custom_call" | custom-call | flops 1000000 | bytes 1000000 | tf_op jit(solution)/shard_map/prepare_1_0_0/pallas_call | solution.py:277
  35.1 1.2 %prepare_1_1_0.1.refs_5_ = f32[3200,128]{1,0:T(8,128)S(1)} custom-call(bf16[1,2,2048,128]{3,2,1,0:T(8,128)(2,1)} %sources.7), custom_call_target="tpu_custom_call" | custom-call | flops 1000000 | bytes 1000000 | tf_op jit(solution)/shard_map/prepare_1_1_0/pallas_call | solution.py:277
  36.4 0.1 combine_0_1_1.1.refs_3_
  36.5 1.5 %collective-permute-start.4 = (bf16[1024,128]{1,0:T(8,128)(2,1)S(1)}, bf16[1024,128]{1,0:T(8,128)(2,1)S(1)}, u32[]{:S(2)}, u32[]{:S(2)}) collective-permute-start(bf16[1024,128]{1,0:T(8,128)(2,1)S(1)} %combine_0_1_1.1.refs_3_), channel_id=1, source_target_pairs={{0,16},{16,0},{1,17},{17,1},{2,18},{18,2},{3,19},{19,3},{4,20},{20... | collective-permute-start | bytes 786440 | tf_op jit(solution)/shard_map/ppermute | solution.py:438
  38.0 2.3 %chunk_1_0_0.1 = (bf16[1024,128]{1,0:T(8,128)(2,1)S(1)}, bf16[1024,128]{1,0:T(8,128)(2,1)S(1)}, f32[3200,128]{1,0:T(8,128)S(1)}) custom-call(s32[1,12]{1,0:T(1,128)} %refs_0_.13, s32[1,12]{1,0:T(1,128)} %refs_1_.13, s32[1,1]{1,0:T(1,128)S(6)} %copy.19.refs_2_, ...), custom_call_target="tpu_custom_call", output_to_operand_aliasing={{2}: (5, {})} | custom-call | flops 1000000000 | bytes 5000000 | tf_op jit(solution)/shard_map/chunk_1_0_0/pallas_call | solution.py:340
  40.4 2.4 %collective-permute-start.17 = (bf16[1024,128]{1,0:T(8,128)(2,1)S(1)}, bf16[1024,128]{1,0:T(8,128)(2,1)S(1)}, u32[]{:S(2)}, u32[]{:S(2)}) collective-permute-start(bf16[1024,128]{1,0:T(8,128)(2,1)S(1)} %get-tuple-element.56), channel_id=1, source_target_pairs={{0,1},{1,0},{2,3},{3,2},{4,5},{5,4},{6,7},{7,6},{8,9},{9,8},{10,11... | collective-permute-start | bytes 786440 | tf_op jit(solution)/shard_map/ppermute | solution.py:432
  42.7 0.5 collective-permute-done.8.refs_3_
  43.3 2.3 %chunk_1_1_0.1 = (bf16[1024,128]{1,0:T(8,128)(2,1)S(1)}, bf16[1024,128]{1,0:T(8,128)(2,1)S(1)}, f32[3200,128]{1,0:T(8,128)S(1)}) custom-call(s32[1,12]{1,0:T(1,128)} %refs_0_.13, s32[1,12]{1,0:T(1,128)} %refs_1_.13, s32[1,1]{1,0:T(1,128)S(6)} %copy.19.refs_2_, bf16[1024,128]{1,0:T(8,128)(2,1)S(1)} %collective-permute-done.8.refs_3_, ...), custom_call_target="tpu_custom_call", output_to_operand_aliasing={{2}: (5, {})} | custom-call | flops 1000000000 | bytes 5000000 | tf_op jit(solution)/shard_map/chunk_1_1_0/pallas_call | solution.py:340
  45.7 1.2 %prepare_1_0_1.1.refs_5_ = f32[3200,128]{1,0:T(8,128)S(1)} custom-call(bf16[1,2,2048,128]{3,2,1,0:T(8,128)(2,1)} %sources.7), custom_call_target="tpu_custom_call" | custom-call | flops 1000000 | bytes 1000000 | tf_op jit(solution)/shard_map/prepare_1_0_1/pallas_call | solution.py:277
  46.9 1.2 %prepare_1_1_1.1.refs_5_ = f32[3200,128]{1,0:T(8,128)S(1)} custom-call(bf16[1,2,2048,128]{3,2,1,0:T(8,128)(2,1)} %sources.7), custom_call_target="tpu_custom_call" | custom-call | flops 1000000 | bytes 1000000 | tf_op jit(solution)/shard_map/prepare_1_1_1/pallas_call | solution.py:277
  48.1 2.3 %chunk_1_0_1.1 = (bf16[1024,128]{1,0:T(8,128)(2,1)S(1)}, bf16[1024,128]{1,0:T(8,128)(2,1)S(1)}, f32[3200,128]{1,0:T(8,128)S(1)}) custom-call(s32[1,12]{1,0:T(1,128)} %refs_0_.13, s32[1,12]{1,0:T(1,128)} %refs_1_.13, s32[1,1]{1,0:T(1,128)S(6)} %copy.19.refs_2_, ...), custom_call_target="tpu_custom_call", output_to_operand_aliasing={{2}: (5, {})} | custom-call | flops 1000000000 | bytes 5000000 | tf_op jit(solution)/shard_map/chunk_1_0_1/pallas_call | solution.py:340
  50.4 2.5 %collective-permute-start.12 = (bf16[1024,128]{1,0:T(8,128)(2,1)S(1)}, bf16[1024,128]{1,0:T(8,128)(2,1)S(1)}, u32[]{:S(2)}, u32[]{:S(2)}) collective-permute-start(bf16[1024,128]{1,0:T(8,128)(2,1)S(1)} %get-tuple-element.50), channel_id=1, source_target_pairs={{0,1},{1,0},{2,3},{3,2},{4,5},{5,4},{6,7},{7,6},{8,9},{9,8},{10,11... | collective-permute-start | bytes 786440 | tf_op jit(solution)/shard_map/ppermute | solution.py:435
  52.9 0.1 collective-permute-start.9
  53.0 2.4 %chunk_1_1_1.1 = (bf16[1024,128]{1,0:T(8,128)(2,1)S(1)}, bf16[1024,128]{1,0:T(8,128)(2,1)S(1)}, f32[3200,128]{1,0:T(8,128)S(1)}) custom-call(s32[1,12]{1,0:T(1,128)} %refs_0_.13, s32[1,12]{1,0:T(1,128)} %refs_1_.13, s32[1,1]{1,0:T(1,128)S(6)} %copy.19.refs_2_, bf16[1024,128]{1,0:T(8,128)(2,1)S(1)} %collective-permute-done.4.refs_3_, ...), custom_call_target="tpu_custom_call", output_to_operand_aliasing={{2}: (5, {})} | custom-call | flops 1000000000 | bytes 5000000 | tf_op jit(solution)/shard_map/chunk_1_1_1/pallas_call | solution.py:340
  55.4 0.1 collective-permute-start.13
  55.5 4.7 %collective-permute-start.5 = (bf16[1024,128]{1,0:T(8,128)(2,1)S(1)}, bf16[1024,128]{1,0:T(8,128)(2,1)S(1)}, u32[]{:S(2)}, u32[]{:S(2)}) collective-permute-start(bf16[1024,128]{1,0:T(8,128)(2,1)S(1)} %get-tuple-element.41), channel_id=1, source_target_pairs={{0,1},{1,0},{2,3},{3,2},{4,5},{5,4},{6,7},{7,6},{8,9},{9,8},{10,11... | collective-permute-start | bytes 786440 | tf_op jit(solution)/shard_map/ppermute | solution.py:435
  60.2 0.1 combine_1_0_0.1.refs_4_
  60.4 0.1 combine_1_1_0.1.refs_4_
  60.5 4.0 %collective-permute-done.13.refs_2_ = bf16[1024,128]{1,0:T(8,128)(2,1)S(1)} collective-permute-done((bf16[1024,128]{1,0:T(8,128)(2,1)S(1)}, bf16[1024,128]{1,0:T(8,128)(2,1)S(1)}, u32[]{:S(2)}, u32[]{:S(2)}) %collective-permute-start.13) | collective-permute-done | bytes 262176 | tf_op jit(solution)/shard_map/ppermute | solution.py:432
  64.5 1.0 %combine_1_0_1.1.refs_5_ = bf16[1,2,2048,128]{3,2,1,0:T(8,128)(2,1)} custom-call(f32[3200,128]{1,0:T(8,128)S(1)} %get-tuple-element.49.refs_0_, bf16[1024,128]{1,0:T(8,128)(2,1)S(1)} %collective-permute-done.12.refs_1_, bf16[1024,128]{1,0:T(8,128)(2,1)S(1)} %collective-permute-done.13.refs_2_, bf16[1024,128]{1,0:T(8,128)(2,1)S(1)} %get-tuple-element.48.refs_3_, ...), custom_call_target="tpu_custom_call" | custom-call | flops 1000000 | bytes 1000000 | tf_op jit(solution)/shard_map/combine_1_0_1/pallas_call | solution.py:411
  65.5 4.2 %collective-permute-done.6.refs_2_ = bf16[1024,128]{1,0:T(8,128)(2,1)S(1)} collective-permute-done((bf16[1024,128]{1,0:T(8,128)(2,1)S(1)}, bf16[1024,128]{1,0:T(8,128)(2,1)S(1)}, u32[]{:S(2)}, u32[]{:S(2)}) %collective-permute-start.6) | collective-permute-done | bytes 262176 | tf_op jit(solution)/shard_map/ppermute | solution.py:432
  69.7 1.0 %combine_1_1_1.1 = bf16[1,2,2048,128]{3,2,1,0:T(8,128)(2,1)} custom-call(f32[3200,128]{1,0:T(8,128)S(1)} %get-tuple-element.40.refs_0_, bf16[1024,128]{1,0:T(8,128)(2,1)S(1)} %collective-permute-done.5.refs_1_, bf16[1024,128]{1,0:T(8,128)(2,1)S(1)} %collective-permute-done.6.refs_2_, ...), custom_call_target="tpu_custom_call", output_to_operand_aliasing={{}: (5, {})} | custom-call | flops 1000000 | bytes 1000000 | tf_op jit(solution)/shard_map/combine_1_1_1/pallas_call | solution.py:411
  (23 shorter events, 0.6 us)
Async XLA Ops:
  3.7 3.4 %collective-permute-start.1 = (bf16[2048,128]{1,0:T(8,128)(2,1)S(1)}, bf16[2048,128]{1,0:T(8,128)(2,1)S(1)}, u32[]{:S(2)}, u32[]{:S(2)}) collective-permute-start(bf16[2048,128]{1,0:T(8,128)(2,1)S(1)} %get-tuple-element.36), channel_id=1, source_target_pairs={{0,1},{1,0},{2,3},{3,2},{4,5},{5,4},{6,7},{7,6},{8,9},{9,8},{10,11... | collective-permute-start | bytes 1572872 | tf_op jit(solution)/shard_map/ppermute | solution.py:435
  4.4 26.7 %collective-permute-start = (bf16[2048,128]{1,0:T(8,128)(2,1)S(1)}, bf16[2048,128]{1,0:T(8,128)(2,1)S(1)}, u32[]{:S(2)}, u32[]{:S(2)}) collective-permute-start(bf16[2048,128]{1,0:T(8,128)(2,1)S(1)} %get-tuple-element.33), channel_id=1, source_target_pairs={{0,1},{1,0},{2,3},{3,2},{4,5},{5,4},{6,7},{7,6},{8,9},{9,8},{10,11... | collective-permute-start | bytes 1572872 | tf_op jit(solution)/shard_map/ppermute | solution.py:435
  4.5 2.5 %collective-permute-start.2 = (bf16[1024,128]{1,0:T(8,128)(2,1)S(1)}, bf16[1024,128]{1,0:T(8,128)(2,1)S(1)}, u32[]{:S(2)}, u32[]{:S(2)}) collective-permute-start(bf16[1024,128]{1,0:T(8,128)(2,1)S(1)} %get-tuple-element.37), channel_id=1, source_target_pairs={{0,15},{1,2},{2,1},{3,4},{4,3},{5,6},{6,5},{7,8},{8,7},{9,10},{10,... | collective-permute-start | bytes 786440 | tf_op jit(solution)/shard_map/ppermute | solution.py:432
  5.0 2.6 %collective-permute-start.14 = (bf16[1024,128]{1,0:T(8,128)(2,1)S(1)}, bf16[1024,128]{1,0:T(8,128)(2,1)S(1)}, u32[]{:S(2)}, u32[]{:S(2)}) collective-permute-start(bf16[1024,128]{1,0:T(8,128)(2,1)S(1)} %get-tuple-element.53), channel_id=1, source_target_pairs={{0,15},{1,2},{2,1},{3,4},{4,3},{5,6},{6,5},{7,8},{8,7},{9,10},{10,... | collective-permute-start | bytes 786440 | tf_op jit(solution)/shard_map/ppermute | solution.py:432
  5.1 26.0 %collective-permute-start.7 = (bf16[1024,128]{1,0:T(8,128)(2,1)S(1)}, bf16[1024,128]{1,0:T(8,128)(2,1)S(1)}, u32[]{:S(2)}, u32[]{:S(2)}) collective-permute-start(bf16[1024,128]{1,0:T(8,128)(2,1)S(1)} %get-tuple-element.44), channel_id=1, source_target_pairs={{0,15},{1,2},{2,1},{3,4},{4,3},{5,6},{6,5},{7,8},{8,7},{9,10},{10,... | collective-permute-start | bytes 786440 | tf_op jit(solution)/shard_map/ppermute | solution.py:432
  7.1 29.3 %collective-permute-start.3 = (bf16[1024,128]{1,0:T(8,128)(2,1)S(1)}, bf16[1024,128]{1,0:T(8,128)(2,1)S(1)}, u32[]{:S(2)}, u32[]{:S(2)}) collective-permute-start(bf16[1024,128]{1,0:T(8,128)(2,1)S(1)} %get-tuple-element.39), channel_id=1, source_target_pairs={{0,15},{1,2},{2,1},{3,4},{4,3},{5,6},{6,5},{7,8},{8,7},{9,10},{10,... | collective-permute-start | bytes 786440 | tf_op jit(solution)/shard_map/ppermute | solution.py:432
  7.7 30.3 %collective-permute-start.15 = (bf16[1024,128]{1,0:T(8,128)(2,1)S(1)}, bf16[1024,128]{1,0:T(8,128)(2,1)S(1)}, u32[]{:S(2)}, u32[]{:S(2)}) collective-permute-start(bf16[1024,128]{1,0:T(8,128)(2,1)S(1)} %combine_0_0_0.1.refs_3_), channel_id=1, source_target_pairs={{0,16},{16,0},{1,17},{17,1},{2,18},{18,2},{3,19},{19,3},{4,20},{20... | collective-permute-start | bytes 786440 | tf_op jit(solution)/shard_map/ppermute | solution.py:438
  31.2 12.1 %collective-permute-start.8 = (bf16[1024,128]{1,0:T(8,128)(2,1)S(1)}, bf16[1024,128]{1,0:T(8,128)(2,1)S(1)}, u32[]{:S(2)}, u32[]{:S(2)}) collective-permute-start(bf16[1024,128]{1,0:T(8,128)(2,1)S(1)} %combine_0_1_0.1.refs_3_), channel_id=1, source_target_pairs={{0,16},{16,0},{1,17},{17,1},{2,18},{18,2},{3,19},{19,3},{4,20},{20... | collective-permute-start | bytes 786440 | tf_op jit(solution)/shard_map/ppermute | solution.py:438
  36.3 11.7 %collective-permute-start.11 = (bf16[1024,128]{1,0:T(8,128)(2,1)S(1)}, bf16[1024,128]{1,0:T(8,128)(2,1)S(1)}, u32[]{:S(2)}, u32[]{:S(2)}) collective-permute-start(bf16[1024,128]{1,0:T(8,128)(2,1)S(1)} %get-tuple-element.48.refs_3_), channel_id=1, source_target_pairs={{0,16},{16,0},{1,17},{17,1},{2,18},{18,2},{3,19},{19,3},{4,20},{20... | collective-permute-start | bytes 786440 | tf_op jit(solution)/shard_map/ppermute | solution.py:438
  36.5 16.4 %collective-permute-start.4 = (bf16[1024,128]{1,0:T(8,128)(2,1)S(1)}, bf16[1024,128]{1,0:T(8,128)(2,1)S(1)}, u32[]{:S(2)}, u32[]{:S(2)}) collective-permute-start(bf16[1024,128]{1,0:T(8,128)(2,1)S(1)} %combine_0_1_1.1.refs_3_), channel_id=1, source_target_pairs={{0,16},{16,0},{1,17},{17,1},{2,18},{18,2},{3,19},{19,3},{4,20},{20... | collective-permute-start | bytes 786440 | tf_op jit(solution)/shard_map/ppermute | solution.py:438
  40.3 15.1 %collective-permute-start.16 = (bf16[1024,128]{1,0:T(8,128)(2,1)S(1)}, bf16[1024,128]{1,0:T(8,128)(2,1)S(1)}, u32[]{:S(2)}, u32[]{:S(2)}) collective-permute-start(bf16[1024,128]{1,0:T(8,128)(2,1)S(1)} %get-tuple-element.55), channel_id=1, source_target_pairs={{0,1},{1,0},{2,3},{3,2},{4,5},{5,4},{6,7},{7,6},{8,9},{9,8},{10,11... | collective-permute-start | bytes 786440 | tf_op jit(solution)/shard_map/ppermute | solution.py:435
  40.4 15.2 %collective-permute-start.17 = (bf16[1024,128]{1,0:T(8,128)(2,1)S(1)}, bf16[1024,128]{1,0:T(8,128)(2,1)S(1)}, u32[]{:S(2)}, u32[]{:S(2)}) collective-permute-start(bf16[1024,128]{1,0:T(8,128)(2,1)S(1)} %get-tuple-element.56), channel_id=1, source_target_pairs={{0,1},{1,0},{2,3},{3,2},{4,5},{5,4},{6,7},{7,6},{8,9},{9,8},{10,11... | collective-permute-start | bytes 786440 | tf_op jit(solution)/shard_map/ppermute | solution.py:432
  45.6 14.7 %collective-permute-start.10 = (bf16[1024,128]{1,0:T(8,128)(2,1)S(1)}, bf16[1024,128]{1,0:T(8,128)(2,1)S(1)}, u32[]{:S(2)}, u32[]{:S(2)}) collective-permute-start(bf16[1024,128]{1,0:T(8,128)(2,1)S(1)} %get-tuple-element.47), channel_id=1, source_target_pairs={{0,1},{1,0},{2,3},{3,2},{4,5},{5,4},{6,7},{7,6},{8,9},{9,8},{10,11... | collective-permute-start | bytes 786440 | tf_op jit(solution)/shard_map/ppermute | solution.py:432
  50.4 10.1 %collective-permute-start.12 = (bf16[1024,128]{1,0:T(8,128)(2,1)S(1)}, bf16[1024,128]{1,0:T(8,128)(2,1)S(1)}, u32[]{:S(2)}, u32[]{:S(2)}) collective-permute-start(bf16[1024,128]{1,0:T(8,128)(2,1)S(1)} %get-tuple-element.50), channel_id=1, source_target_pairs={{0,1},{1,0},{2,3},{3,2},{4,5},{5,4},{6,7},{7,6},{8,9},{9,8},{10,11... | collective-permute-start | bytes 786440 | tf_op jit(solution)/shard_map/ppermute | solution.py:435
  52.9 7.4 %collective-permute-start.9 = (bf16[1024,128]{1,0:T(8,128)(2,1)S(1)}, bf16[1024,128]{1,0:T(8,128)(2,1)S(1)}, u32[]{:S(2)}, u32[]{:S(2)}) collective-permute-start(bf16[1024,128]{1,0:T(8,128)(2,1)S(1)} %get-tuple-element.46), channel_id=1, source_target_pairs={{0,1},{1,0},{2,3},{3,2},{4,5},{5,4},{6,7},{7,6},{8,9},{9,8},{10,11... | collective-permute-start | bytes 786440 | tf_op jit(solution)/shard_map/ppermute | solution.py:435
  55.4 9.1 %collective-permute-start.13 = (bf16[1024,128]{1,0:T(8,128)(2,1)S(1)}, bf16[1024,128]{1,0:T(8,128)(2,1)S(1)}, u32[]{:S(2)}, u32[]{:S(2)}) collective-permute-start(bf16[1024,128]{1,0:T(8,128)(2,1)S(1)} %get-tuple-element.51), channel_id=1, source_target_pairs={{0,1},{1,0},{2,3},{3,2},{4,5},{5,4},{6,7},{7,6},{8,9},{9,8},{10,11... | collective-permute-start | bytes 786440 | tf_op jit(solution)/shard_map/ppermute | solution.py:432
  55.5 9.9 %collective-permute-start.5 = (bf16[1024,128]{1,0:T(8,128)(2,1)S(1)}, bf16[1024,128]{1,0:T(8,128)(2,1)S(1)}, u32[]{:S(2)}, u32[]{:S(2)}) collective-permute-start(bf16[1024,128]{1,0:T(8,128)(2,1)S(1)} %get-tuple-element.41), channel_id=1, source_target_pairs={{0,1},{1,0},{2,3},{3,2},{4,5},{5,4},{6,7},{7,6},{8,9},{9,8},{10,11... | collective-permute-start | bytes 786440 | tf_op jit(solution)/shard_map/ppermute | solution.py:435
  60.2 9.5 %collective-permute-start.6 = (bf16[1024,128]{1,0:T(8,128)(2,1)S(1)}, bf16[1024,128]{1,0:T(8,128)(2,1)S(1)}, u32[]{:S(2)}, u32[]{:S(2)}) collective-permute-start(bf16[1024,128]{1,0:T(8,128)(2,1)S(1)} %get-tuple-element.42), channel_id=1, source_target_pairs={{0,1},{1,0},{2,3},{3,2},{4,5},{5,4},{6,7},{7,6},{8,9},{9,8},{10,11... | collective-permute-start | bytes 786440 | tf_op jit(solution)/shard_map/ppermute | solution.py:432

commit v5 on v3

--- a/solution.py
+++ b/solution.py
@@ -19,9 +19,13 @@
     return [(i, i ^ 1) for i in range(devices)]
 
 
-def outer_route(wave, devices):
-    pairs = [(wave * devices + i, wave * devices + i + 1) for i in range(1, devices - 1, 2)]
-    return pairs + [(b, a) for a, b in pairs]
+def outer_route(wave, depth, devices):
+    pairs = []
+    for layer in range(depth):
+        for i in range(devices):
+            other = (i + 1 if i % 2 else i - 1) % devices if layer == wave else i ^ 1
+            pairs.append((layer * devices + i, layer * devices + other))
+    return pairs
 
 
 def down_route(depth):
@@ -53,10 +57,11 @@
     return jnp.where(lane < half, -moved, moved)
 
 
-def accumulate(index_refs, rows_s, cols_s, tiles, pair, sums, blocks, skipped=None):
+def accumulate(index_refs, tiles, pair, sums, blocks, skipped=None):
+    rows_s, cols_s, count_s = index_refs
     tile_size = tiles.shape[-1]
     first = (lax.axis_index("tile") - 1) * blocks
-    count = index_refs[2][0, 0]
+    count = count_s[0, 0]
     for i in range(tiles.shape[0]):
         live = i < count
         window = rows_s[0, i] - first
@@ -155,12 +160,12 @@
             outer,
             pltpu.VMEM((2, rows_dev, width), jnp.bfloat16),
             pltpu.VMEM((slots, 2, tile_size, tile_size), jnp.bfloat16),
+            pltpu.SMEM((1, slots), jnp.int32),
+            pltpu.SMEM((1, slots), jnp.int32),
         ],
         in_specs=[HBM, HBM, SMEM, HBM, HBM],
-        out_specs=[VMEM] * 4,
+        out_specs=[VMEM] * 4 + [SMEM] * 2,
         scratch_shapes=[
-            pltpu.SMEM((1, slots), jnp.int32),
-            pltpu.SMEM((1, slots), jnp.int32),
             pltpu.VMEM((rows_dev, width), jnp.float32),
             pltpu.SemaphoreType.DMA((3,)),
             pltpu.SemaphoreType.DMA((slots,)),
@@ -171,9 +176,8 @@
 
 def front_kernel(front, blocks, *refs):
     index_refs, sources, tiles, operand = refs[:3], refs[3], refs[4], refs[5]
-    outs, (rows_s, cols_s, source_v, sums, sems, *rest) = refs[6 : len(refs) - (5 if front == 0 else 6)], refs[
-        len(refs) - (5 if front == 0 else 6) :
-    ]
+    own = 3 if front == 0 else 4
+    outs, (source_v, sums, sems, *rest) = refs[6:-own], refs[-own:]
     inner_ref, own_refs, outer_refs = outs[0], outs[1:3], outs[3:]
     pair = operand if front == 0 else rest[0]
     tile_size = tiles.shape[-1]
@@ -182,25 +186,19 @@
 
     @pl.when(lax.axis_index("layer") == 0)
     def _():
-        copies = [
-            pltpu.make_async_copy(index_refs[0], rows_s, sems.at[0]),
-            pltpu.make_async_copy(index_refs[1], cols_s, sems.at[1]),
-            pltpu.make_async_copy(sources.at[0, front], source_v, sems.at[2]),
-        ]
+        copies = [pltpu.make_async_copy(sources.at[0, front], source_v, sems.at[0])]
         if front > 0:
-            copies.append(pltpu.make_async_copy(operand.at[front], pair.at[0], sems.at[3]))
+            copies.insert(0, pltpu.make_async_copy(operand.at[front], pair.at[0], sems.at[1]))
         for copy in copies:
             copy.start()
         sums[...] = jnp.zeros(sums.shape, jnp.float32)
-        for copy in copies:
-            copy.wait()
         if front > 0:
+            copies[0].wait()
             for r in range(blocks):
                 rows = pl.ds(r * tile_size, tile_size)
                 pair[1, rows, :] = turn(pair[0, rows, :].astype(jnp.float32)).astype(jnp.bfloat16)
-        accumulate(
-            index_refs, rows_s, cols_s, tiles, pair, sums, blocks, outer_window() if front == 0 else None
-        )
+        accumulate(index_refs, tiles, pair, sums, blocks, outer_window() if front == 0 else None)
+        copies[-1].wait()
         inner_start, outer_start = side_starts(rows_dev)
         half = tile_size // 2
         for r in range(blocks):
@@ -227,23 +225,21 @@
 
 def front_products(front, operand, sources, tiles, index, blocks):
     rows_dev, width = sources.shape[-2:]
-    slots, _, tile_size, _ = tiles.shape
+    tile_size = tiles.shape[-1]
     outer = pltpu.VMEM((rows_dev // 2, width), jnp.bfloat16)
     own = pltpu.VMEM((rows_dev // 2, width), jnp.float32)
     outs = [pltpu.VMEM((rows_dev, width), jnp.bfloat16), own, own] + ([outer, outer] if front else [])
     scratch = [
-        pltpu.SMEM((1, slots), jnp.int32),
-        pltpu.SMEM((1, slots), jnp.int32),
         pltpu.VMEM((rows_dev, width), jnp.bfloat16),
         pltpu.VMEM((3 * rows_dev + tile_size, width), jnp.float32),
-        pltpu.SemaphoreType.DMA((4,)),
+        pltpu.SemaphoreType.DMA((2,)),
     ]
     if front:
         scratch.append(pltpu.VMEM((2, rows_dev, width), jnp.bfloat16))
     return pl.pallas_call(
         functools.partial(front_kernel, front, blocks),
         out_shape=outs,
-        in_specs=[HBM, HBM, SMEM, HBM, VMEM, HBM if front else VMEM],
+        in_specs=[SMEM, SMEM, SMEM, HBM, VMEM, HBM if front else VMEM],
         out_specs=[VMEM] * len(outs),
         scratch_shapes=scratch,
         **kernel_options(f"front_{front}", 10**9, 5 * 10**6, 6),
@@ -409,12 +405,10 @@
     tile_size = green_tiles.shape[-1]
     blocks = rows_dev // tile_size
     index = (in_hbm(tile_rows), in_hbm(tile_cols), tile_count)
-    resident = tuple(pltpu.with_memory_space_constraint(a, pltpu.SMEM) for a in (tile_rows, tile_cols))
-    resident = (*resident, tile_count)
     incident, sources, green_tiles = map(in_hbm, (incident, sources, green_tiles))
 
     def across(payload, wave):
-        return lax.ppermute(payload, ("layer", "tile"), outer_route(wave, devices))
+        return lax.ppermute(payload, ("layer", "tile"), outer_route(wave, depth, devices))
 
     def beside(payload):
         return lax.ppermute(payload, "tile", inner_route(devices))
@@ -427,6 +421,7 @@
 
     first = open_products(incident, green_tiles, index, blocks)
     payloads, held = list(first[:PARTS]), first[3]
+    index = (*first[4:], tile_count)
     chunks = []
     for front in range(fronts):
         made = front_products(front, incident if front else first[2], sources, held, index, blocks)
@@ -451,7 +446,7 @@
         for c, inbound in enumerate(passed):
             sums = prepare(wave, c // PARTS, c % PARTS, sources, tile_size)
             outer, inner, own = chunk_products(
-                wave, c // PARTS, c % PARTS, inbound, held, sums, resident, blocks
+                wave, c // PARTS, c % PARTS, inbound, held, sums, index, blocks
             )
             chunks.append((own, beside(inner), across(outer, wave)))
         if final:

time: 76 us -> 67.4 us (0.89)
  the two profiles are of different devices: /device:TPU:22 before, /device:TPU:3 now
where the time goes in v5:
time: 67.4 us; the launch traced here: 67.1 us
  starting transfers between devices  38.7 us (57%)
  Pallas kernels  16.2 us (24%)
  waiting for transfers between devices  11.2 us (17%)
  between operations  1.02 us (2%)
    ppermute x4, starting transfers between devices, down(): return lax.ppermute(payload, 'layer', layer_route)  27.4 us
    ppermute x8, waiting for transfers between devices, across(): lax.ppermute(payload, ('layer', 'tile'), outer_route(wave, depth, devices))  9.78 us
    ppermute x6, starting transfers between devices, beside(): return lax.ppermute(payload, 'tile', inner_route(devices))  6.96 us
    pallas_call x4, Pallas kernels, chunk_products(): pl.pallas_call(functools.partial(chunk_kernel, wave, blocks), out_shape=[...  5.9 us
    pallas_call x4, Pallas kernels, prepare(): pl.pallas_call(functools.partial(prepare_kernel, wave, front, part, rows_...  4.78 us
    ppermute x8, starting transfers between devices, across(): lax.ppermute(payload, ('layer', 'tile'), outer_route(wave, depth, devices))  4.37 us
    pallas_call x1, Pallas kernels, open_products(): pl.pallas_call(functools.partial(open_kernel, blocks), out_shape=[outer,...  2.93 us
    pallas_call x8, Pallas kernels, combine(): pl.pallas_call(functools.partial(combine_kernel, wave, part, through is n...  2.5 us
  transfers between devices with their start and end apart: 18, of which 4 were waited for; matrix products, arithmetic and copies ran while one was open for 0% of the time, Pallas kernels for 18%

profile of v5, /device:TPU:3, one launch (start us, length us, event | category | flops | bytes accessed | tf_op | source)
XLA Modules:
  0.0 67.1 jit_solution(4847935951790863745)
XLA Ops:
  0.7 2.9 %open.1 = (bf16[1024,128]{1,0:T(8,128)(2,1)S(1)}, bf16[1024,128]{1,0:T(8,128)(2,1)S(1)}, bf16[2,2048,128]{2,1,0:T(8,128)(2,1)S(1)}, bf16[12,2,256,256]{3,2,1,0:T...) custom-call(s32[1,12]{1,0:T(1,128)} %refs_0_.1, s32[1,12]{1,0:T(1,128)} %refs_1_.1, s32[1,1]{1,0:T(1,128)S(6)} %copy.19.refs_2_, ...), custom_call_target="tpu_custom_call" | custom-call | flops 500000000 | bytes 4000000 | tf_op jit(solution)/shard_map/open/pallas_call | solution.py:156
  3.6 0.7 %collective-permute-start.1 = (bf16[2048,128]{1,0:T(8,128)(2,1)S(1)}, bf16[2048,128]{1,0:T(8,128)(2,1)S(1)}, u32[]{:S(2)}, u32[]{:S(2)}) collective-permute-start(bf16[2048,128]{1,0:T(8,128)(2,1)S(1)} %get-tuple-element.40), channel_id=1, source_target_pairs={{0,1},{1,0},{2,3},{3,2},{4,5},{5,4},{6,7},{7,6},{8,9},{9,8},{10,11... | collective-permute-start | bytes 1572872 | tf_op jit(solution)/shard_map/ppermute | solution.py:414
  4.4 0.1 collective-permute-start
  4.5 0.5 collective-permute-start.2
  5.1 0.4 collective-permute-start.7
  5.5 1.5 %collective-permute-done.2.refs_2_ = bf16[1024,128]{1,0:T(8,128)(2,1)S(1)} collective-permute-done((bf16[1024,128]{1,0:T(8,128)(2,1)S(1)}, bf16[1024,128]{1,0:T(8,128)(2,1)S(1)}, u32[]{:S(2)}, u32[]{:S(2)}) %collective-permute-start.2) | collective-permute-done | bytes 262176 | tf_op jit(solution)/shard_map/ppermute | solution.py:411
  7.1 0.4 collective-permute-start.3
  7.7 23.1 %collective-permute-start.15 = (bf16[1024,128]{1,0:T(8,128)(2,1)S(1)}, bf16[1024,128]{1,0:T(8,128)(2,1)S(1)}, u32[]{:S(2)}, u32[]{:S(2)}) collective-permute-start(bf16[1024,128]{1,0:T(8,128)(2,1)S(1)} %combine_0_0_0.1.refs_3_), channel_id=1, source_target_pairs={{0,16},{16,0},{1,17},{17,1},{2,18},{18,2},{3,19},{19,3},{4,20},{20... | collective-permute-start | bytes 786440 | tf_op jit(solution)/shard_map/ppermute | solution.py:417
  30.7 0.1 combine_0_1_0.1.refs_3_
  30.8 2.7 %collective-permute-start.8 = (bf16[1024,128]{1,0:T(8,128)(2,1)S(1)}, bf16[1024,128]{1,0:T(8,128)(2,1)S(1)}, u32[]{:S(2)}, u32[]{:S(2)}) collective-permute-start(bf16[1024,128]{1,0:T(8,128)(2,1)S(1)} %combine_0_1_0.1.refs_3_), channel_id=1, source_target_pairs={{0,16},{16,0},{1,17},{17,1},{2,18},{18,2},{3,19},{19,3},{4,20},{20... | collective-permute-start | bytes 786440 | tf_op jit(solution)/shard_map/ppermute | solution.py:417
  33.5 1.2 %prepare_1_0_0.1.refs_5_ = f32[3200,128]{1,0:T(8,128)S(1)} custom-call(bf16[1,2,2048,128]{3,2,1,0:T(8,128)(2,1)} %sources.7), custom_call_target="tpu_custom_call" | custom-call | flops 1000000 | bytes 1000000 | tf_op jit(solution)/shard_map/prepare_1_0_0/pallas_call | solution.py:269
  34.7 1.2 %prepare_1_1_0.1.refs_5_ = f32[3200,128]{1,0:T(8,128)S(1)} custom-call(bf16[1,2,2048,128]{3,2,1,0:T(8,128)(2,1)} %sources.7), custom_call_target="tpu_custom_call" | custom-call | flops 1000000 | bytes 1000000 | tf_op jit(solution)/shard_map/prepare_1_1_0/pallas_call | solution.py:269
  36.0 0.1 combine_0_1_1.1.refs_3_
  36.1 1.5 %collective-permute-start.4 = (bf16[1024,128]{1,0:T(8,128)(2,1)S(1)}, bf16[1024,128]{1,0:T(8,128)(2,1)S(1)}, u32[]{:S(2)}, u32[]{:S(2)}) collective-permute-start(bf16[1024,128]{1,0:T(8,128)(2,1)S(1)} %combine_0_1_1.1.refs_3_), channel_id=1, source_target_pairs={{0,16},{16,0},{1,17},{17,1},{2,18},{18,2},{3,19},{19,3},{4,20},{20... | collective-permute-start | bytes 786440 | tf_op jit(solution)/shard_map/ppermute | solution.py:417
  37.6 1.4 %chunk_1_0_0.1 = (bf16[1024,128]{1,0:T(8,128)(2,1)S(1)}, bf16[1024,128]{1,0:T(8,128)(2,1)S(1)}, f32[3200,128]{1,0:T(8,128)S(1)}) custom-call(s32[1,12]{1,0:T(1,128)S(4)} %get-tuple-element.33.refs_0_, s32[1,12]{1,0:T(1,128)S(4)} %get-tuple-element.34.refs_1_, s32[1,1]{1,0:T(1,128)S(6)} %copy.19.refs_2_, ...), custom_call_target="tpu_custom_call", output_to_operand_aliasing={{2}: (5, {})} | custom-call | flops 1000000000 | bytes 5000000 | tf_op jit(solution)/shard_map/chunk_1_0_0/pallas_call | solution.py:324
  39.2 2.4 %collective-permute-start.17 = (bf16[1024,128]{1,0:T(8,128)(2,1)S(1)}, bf16[1024,128]{1,0:T(8,128)(2,1)S(1)}, u32[]{:S(2)}, u32[]{:S(2)}) collective-permute-start(bf16[1024,128]{1,0:T(8,128)(2,1)S(1)} %get-tuple-element.60), channel_id=1, source_target_pairs={{0,1},{1,0},{2,3},{3,2},{4,5},{5,4},{6,7},{7,6},{8,9},{9,8},{10,11... | collective-permute-start | bytes 786440 | tf_op jit(solution)/shard_map/ppermute | solution.py:411
  41.5 1.4 %collective-permute-done.8.refs_3_ = bf16[1024,128]{1,0:T(8,128)(2,1)S(1)} collective-permute-done((bf16[1024,128]{1,0:T(8,128)(2,1)S(1)}, bf16[1024,128]{1,0:T(8,128)(2,1)S(1)}, u32[]{:S(2)}, u32[]{:S(2)}) %collective-permute-start.8) | collective-permute-done | bytes 262176 | tf_op jit(solution)/shard_map/ppermute | solution.py:417
  42.9 1.4 %chunk_1_1_0.1 = (bf16[1024,128]{1,0:T(8,128)(2,1)S(1)}, bf16[1024,128]{1,0:T(8,128)(2,1)S(1)}, f32[3200,128]{1,0:T(8,128)S(1)}) custom-call(s32[1,12]{1,0:T(1,128)S(4)} %get-tuple-element.33.refs_0_, s32[1,12]{1,0:T(1,128)S(4)} %get-tuple-element.34.refs_1_, s32[1,1]{1,0:T(1,128)S(6)} %copy.19.refs_2_, ...), custom_call_target="tpu_custom_call", output_to_operand_aliasing={{2}: (5, {})} | custom-call | flops 1000000000 | bytes 5000000 | tf_op jit(solution)/shard_map/chunk_1_1_0/pallas_call | solution.py:324
  44.4 1.2 %prepare_1_0_1.1.refs_5_ = f32[3200,128]{1,0:T(8,128)S(1)} custom-call(bf16[1,2,2048,128]{3,2,1,0:T(8,128)(2,1)} %sources.7), custom_call_target="tpu_custom_call" | custom-call | flops 1000000 | bytes 1000000 | tf_op jit(solution)/shard_map/prepare_1_0_1/pallas_call | solution.py:269
  45.6 1.2 %prepare_1_1_1.1.refs_5_ = f32[3200,128]{1,0:T(8,128)S(1)} custom-call(bf16[1,2,2048,128]{3,2,1,0:T(8,128)(2,1)} %sources.7), custom_call_target="tpu_custom_call" | custom-call | flops 1000000 | bytes 1000000 | tf_op jit(solution)/shard_map/prepare_1_1_1/pallas_call | solution.py:269
  46.8 1.5 %chunk_1_0_1.1 = (bf16[1024,128]{1,0:T(8,128)(2,1)S(1)}, bf16[1024,128]{1,0:T(8,128)(2,1)S(1)}, f32[3200,128]{1,0:T(8,128)S(1)}) custom-call(s32[1,12]{1,0:T(1,128)S(4)} %get-tuple-element.33.refs_0_, s32[1,12]{1,0:T(1,128)S(4)} %get-tuple-element.34.refs_1_, s32[1,1]{1,0:T(1,128)S(6)} %copy.19.refs_2_, ...), custom_call_target="tpu_custom_call", output_to_operand_aliasing={{2}: (5, {})} | custom-call | flops 1000000000 | bytes 5000000 | tf_op jit(solution)/shard_map/chunk_1_0_1/pallas_call | solution.py:324
  48.3 1.7 %collective-permute-start.12 = (bf16[1024,128]{1,0:T(8,128)(2,1)S(1)}, bf16[1024,128]{1,0:T(8,128)(2,1)S(1)}, u32[]{:S(2)}, u32[]{:S(2)}) collective-permute-start(bf16[1024,128]{1,0:T(8,128)(2,1)S(1)} %get-tuple-element.54), channel_id=1, source_target_pairs={{0,1},{1,0},{2,3},{3,2},{4,5},{5,4},{6,7},{7,6},{8,9},{9,8},{10,11... | collective-permute-start | bytes 786440 | tf_op jit(solution)/shard_map/ppermute | solution.py:414
  50.0 0.1 collective-permute-start.9
  50.1 1.5 %chunk_1_1_1.1 = (bf16[1024,128]{1,0:T(8,128)(2,1)S(1)}, bf16[1024,128]{1,0:T(8,128)(2,1)S(1)}, f32[3200,128]{1,0:T(8,128)S(1)}) custom-call(s32[1,12]{1,0:T(1,128)S(4)} %get-tuple-element.33.refs_0_, s32[1,12]{1,0:T(1,128)S(4)} %get-tuple-element.34.refs_1_, s32[1,1]{1,0:T(1,128)S(6)} %copy.19.refs_2_, ...), custom_call_target="tpu_custom_call", output_to_operand_aliasing={{2}: (5, {})} | custom-call | flops 1000000000 | bytes 5000000 | tf_op jit(solution)/shard_map/chunk_1_1_1/pallas_call | solution.py:324
  51.6 0.5 collective-permute-start.13
  52.1 4.3 %collective-permute-start.5 = (bf16[1024,128]{1,0:T(8,128)(2,1)S(1)}, bf16[1024,128]{1,0:T(8,128)(2,1)S(1)}, u32[]{:S(2)}, u32[]{:S(2)}) collective-permute-start(bf16[1024,128]{1,0:T(8,128)(2,1)S(1)} %get-tuple-element.45), channel_id=1, source_target_pairs={{0,1},{1,0},{2,3},{3,2},{4,5},{5,4},{6,7},{7,6},{8,9},{9,8},{10,11... | collective-permute-start | bytes 786440 | tf_op jit(solution)/shard_map/ppermute | solution.py:414
  56.5 0.1 combine_1_0_0.1.refs_4_
  56.6 0.1 combine_1_1_0.1.refs_4_
  56.7 5.0 %collective-permute-done.13.refs_2_ = bf16[1024,128]{1,0:T(8,128)(2,1)S(1)} collective-permute-done((bf16[1024,128]{1,0:T(8,128)(2,1)S(1)}, bf16[1024,128]{1,0:T(8,128)(2,1)S(1)}, u32[]{:S(2)}, u32[]{:S(2)}) %collective-permute-start.13) | collective-permute-done | bytes 262176 | tf_op jit(solution)/shard_map/ppermute | solution.py:411
  61.7 1.0 %combine_1_0_1.1.refs_5_ = bf16[1,2,2048,128]{3,2,1,0:T(8,128)(2,1)} custom-call(f32[3200,128]{1,0:T(8,128)S(1)} %get-tuple-element.53.refs_0_, bf16[1024,128]{1,0:T(8,128)(2,1)S(1)} %collective-permute-done.12.refs_1_, bf16[1024,128]{1,0:T(8,128)(2,1)S(1)} %collective-permute-done.13.refs_2_, bf16[1024,128]{1,0:T(8,128)(2,1)S(1)} %get-tuple-element.52.refs_3_, ...), custom_call_target="tpu_custom_call" | custom-call | flops 1000000 | bytes 1000000 | tf_op jit(solution)/shard_map/combine_1_0_1/pallas_call | solution.py:390
  62.7 3.3 %collective-permute-done.6.refs_2_ = bf16[1024,128]{1,0:T(8,128)(2,1)S(1)} collective-permute-done((bf16[1024,128]{1,0:T(8,128)(2,1)S(1)}, bf16[1024,128]{1,0:T(8,128)(2,1)S(1)}, u32[]{:S(2)}, u32[]{:S(2)}) %collective-permute-start.6) | collective-permute-done | bytes 262176 | tf_op jit(solution)/shard_map/ppermute | solution.py:411
  65.9 1.0 %combine_1_1_1.1 = bf16[1,2,2048,128]{3,2,1,0:T(8,128)(2,1)} custom-call(f32[3200,128]{1,0:T(8,128)S(1)} %get-tuple-element.44.refs_0_, bf16[1024,128]{1,0:T(8,128)(2,1)S(1)} %collective-permute-done.5.refs_1_, bf16[1024,128]{1,0:T(8,128)(2,1)S(1)} %collective-permute-done.6.refs_2_, ...), custom_call_target="tpu_custom_call", output_to_operand_aliasing={{}: (5, {})} | custom-call | flops 1000000 | bytes 1000000 | tf_op jit(solution)/shard_map/combine_1_1_1/pallas_call | solution.py:390
  (23 shorter events, 0.5 us)
Async XLA Ops:
  3.6 3.4 %collective-permute-start.1 = (bf16[2048,128]{1,0:T(8,128)(2,1)S(1)}, bf16[2048,128]{1,0:T(8,128)(2,1)S(1)}, u32[]{:S(2)}, u32[]{:S(2)}) collective-permute-start(bf16[2048,128]{1,0:T(8,128)(2,1)S(1)} %get-tuple-element.40), channel_id=1, source_target_pairs={{0,1},{1,0},{2,3},{3,2},{4,5},{5,4},{6,7},{7,6},{8,9},{9,8},{10,11... | collective-permute-start | bytes 1572872 | tf_op jit(solution)/shard_map/ppermute | solution.py:414
  4.4 26.3 %collective-permute-start = (bf16[2048,128]{1,0:T(8,128)(2,1)S(1)}, bf16[2048,128]{1,0:T(8,128)(2,1)S(1)}, u32[]{:S(2)}, u32[]{:S(2)}) collective-permute-start(bf16[2048,128]{1,0:T(8,128)(2,1)S(1)} %get-tuple-element.37), channel_id=1, source_target_pairs={{0,1},{1,0},{2,3},{3,2},{4,5},{5,4},{6,7},{7,6},{8,9},{9,8},{10,11... | collective-permute-start | bytes 1572872 | tf_op jit(solution)/shard_map/ppermute | solution.py:414
  4.5 2.5 %collective-permute-start.2 = (bf16[1024,128]{1,0:T(8,128)(2,1)S(1)}, bf16[1024,128]{1,0:T(8,128)(2,1)S(1)}, u32[]{:S(2)}, u32[]{:S(2)}) collective-permute-start(bf16[1024,128]{1,0:T(8,128)(2,1)S(1)} %get-tuple-element.41), channel_id=1, source_target_pairs={{0,15},{1,2},{2,1},{3,4},{4,3},{5,6},{6,5},{7,8},{8,7},{9,10},{10,... | collective-permute-start | bytes 786440 | tf_op jit(solution)/shard_map/ppermute | solution.py:411
  5.0 2.6 %collective-permute-start.14 = (bf16[1024,128]{1,0:T(8,128)(2,1)S(1)}, bf16[1024,128]{1,0:T(8,128)(2,1)S(1)}, u32[]{:S(2)}, u32[]{:S(2)}) collective-permute-start(bf16[1024,128]{1,0:T(8,128)(2,1)S(1)} %get-tuple-element.57), channel_id=1, source_target_pairs={{0,15},{1,2},{2,1},{3,4},{4,3},{5,6},{6,5},{7,8},{8,7},{9,10},{10,... | collective-permute-start | bytes 786440 | tf_op jit(solution)/shard_map/ppermute | solution.py:411
  5.1 25.7 %collective-permute-start.7 = (bf16[1024,128]{1,0:T(8,128)(2,1)S(1)}, bf16[1024,128]{1,0:T(8,128)(2,1)S(1)}, u32[]{:S(2)}, u32[]{:S(2)}) collective-permute-start(bf16[1024,128]{1,0:T(8,128)(2,1)S(1)} %get-tuple-element.48), channel_id=1, source_target_pairs={{0,15},{1,2},{2,1},{3,4},{4,3},{5,6},{6,5},{7,8},{8,7},{9,10},{10,... | collective-permute-start | bytes 786440 | tf_op jit(solution)/shard_map/ppermute | solution.py:411
  7.1 28.9 %collective-permute-start.3 = (bf16[1024,128]{1,0:T(8,128)(2,1)S(1)}, bf16[1024,128]{1,0:T(8,128)(2,1)S(1)}, u32[]{:S(2)}, u32[]{:S(2)}) collective-permute-start(bf16[1024,128]{1,0:T(8,128)(2,1)S(1)} %get-tuple-element.43), channel_id=1, source_target_pairs={{0,15},{1,2},{2,1},{3,4},{4,3},{5,6},{6,5},{7,8},{8,7},{9,10},{10,... | collective-permute-start | bytes 786440 | tf_op jit(solution)/shard_map/ppermute | solution.py:411
  7.7 30.0 %collective-permute-start.15 = (bf16[1024,128]{1,0:T(8,128)(2,1)S(1)}, bf16[1024,128]{1,0:T(8,128)(2,1)S(1)}, u32[]{:S(2)}, u32[]{:S(2)}) collective-permute-start(bf16[1024,128]{1,0:T(8,128)(2,1)S(1)} %combine_0_0_0.1.refs_3_), channel_id=1, source_target_pairs={{0,16},{16,0},{1,17},{17,1},{2,18},{18,2},{3,19},{19,3},{4,20},{20... | collective-permute-start | bytes 786440 | tf_op jit(solution)/shard_map/ppermute | solution.py:417
  30.8 12.1 %collective-permute-start.8 = (bf16[1024,128]{1,0:T(8,128)(2,1)S(1)}, bf16[1024,128]{1,0:T(8,128)(2,1)S(1)}, u32[]{:S(2)}, u32[]{:S(2)}) collective-permute-start(bf16[1024,128]{1,0:T(8,128)(2,1)S(1)} %combine_0_1_0.1.refs_3_), channel_id=1, source_target_pairs={{0,16},{16,0},{1,17},{17,1},{2,18},{18,2},{3,19},{19,3},{4,20},{20... | collective-permute-start | bytes 786440 | tf_op jit(solution)/shard_map/ppermute | solution.py:417
  35.9 10.9 %collective-permute-start.11 = (bf16[1024,128]{1,0:T(8,128)(2,1)S(1)}, bf16[1024,128]{1,0:T(8,128)(2,1)S(1)}, u32[]{:S(2)}, u32[]{:S(2)}) collective-permute-start(bf16[1024,128]{1,0:T(8,128)(2,1)S(1)} %get-tuple-element.52.refs_3_), channel_id=1, source_target_pairs={{0,16},{16,0},{1,17},{17,1},{2,18},{18,2},{3,19},{19,3},{4,20},{20... | collective-permute-start | bytes 786440 | tf_op jit(solution)/shard_map/ppermute | solution.py:417
  36.1 13.9 %collective-permute-start.4 = (bf16[1024,128]{1,0:T(8,128)(2,1)S(1)}, bf16[1024,128]{1,0:T(8,128)(2,1)S(1)}, u32[]{:S(2)}, u32[]{:S(2)}) collective-permute-start(bf16[1024,128]{1,0:T(8,128)(2,1)S(1)} %combine_0_1_1.1.refs_3_), channel_id=1, source_target_pairs={{0,16},{16,0},{1,17},{17,1},{2,18},{18,2},{3,19},{19,3},{4,20},{20... | collective-permute-start | bytes 786440 | tf_op jit(solution)/shard_map/ppermute | solution.py:417
  39.1 12.5 %collective-permute-start.16 = (bf16[1024,128]{1,0:T(8,128)(2,1)S(1)}, bf16[1024,128]{1,0:T(8,128)(2,1)S(1)}, u32[]{:S(2)}, u32[]{:S(2)}) collective-permute-start(bf16[1024,128]{1,0:T(8,128)(2,1)S(1)} %get-tuple-element.59), channel_id=1, source_target_pairs={{0,1},{1,0},{2,3},{3,2},{4,5},{5,4},{6,7},{7,6},{8,9},{9,8},{10,11... | collective-permute-start | bytes 786440 | tf_op jit(solution)/shard_map/ppermute | solution.py:414
  39.2 13.0 %collective-permute-start.17 = (bf16[1024,128]{1,0:T(8,128)(2,1)S(1)}, bf16[1024,128]{1,0:T(8,128)(2,1)S(1)}, u32[]{:S(2)}, u32[]{:S(2)}) collective-permute-start(bf16[1024,128]{1,0:T(8,128)(2,1)S(1)} %get-tuple-element.60), channel_id=1, source_target_pairs={{0,1},{1,0},{2,3},{3,2},{4,5},{5,4},{6,7},{7,6},{8,9},{9,8},{10,11... | collective-permute-start | bytes 786440 | tf_op jit(solution)/shard_map/ppermute | solution.py:411
  44.3 12.1 %collective-permute-start.10 = (bf16[1024,128]{1,0:T(8,128)(2,1)S(1)}, bf16[1024,128]{1,0:T(8,128)(2,1)S(1)}, u32[]{:S(2)}, u32[]{:S(2)}) collective-permute-start(bf16[1024,128]{1,0:T(8,128)(2,1)S(1)} %get-tuple-element.51), channel_id=1, source_target_pairs={{0,1},{1,0},{2,3},{3,2},{4,5},{5,4},{6,7},{7,6},{8,9},{9,8},{10,11... | collective-permute-start | bytes 786440 | tf_op jit(solution)/shard_map/ppermute | solution.py:411
  48.3 8.4 %collective-permute-start.12 = (bf16[1024,128]{1,0:T(8,128)(2,1)S(1)}, bf16[1024,128]{1,0:T(8,128)(2,1)S(1)}, u32[]{:S(2)}, u32[]{:S(2)}) collective-permute-start(bf16[1024,128]{1,0:T(8,128)(2,1)S(1)} %get-tuple-element.54), channel_id=1, source_target_pairs={{0,1},{1,0},{2,3},{3,2},{4,5},{5,4},{6,7},{7,6},{8,9},{9,8},{10,11... | collective-permute-start | bytes 786440 | tf_op jit(solution)/shard_map/ppermute | solution.py:414
  50.0 6.6 %collective-permute-start.9 = (bf16[1024,128]{1,0:T(8,128)(2,1)S(1)}, bf16[1024,128]{1,0:T(8,128)(2,1)S(1)}, u32[]{:S(2)}, u32[]{:S(2)}) collective-permute-start(bf16[1024,128]{1,0:T(8,128)(2,1)S(1)} %get-tuple-element.50), channel_id=1, source_target_pairs={{0,1},{1,0},{2,3},{3,2},{4,5},{5,4},{6,7},{7,6},{8,9},{9,8},{10,11... | collective-permute-start | bytes 786440 | tf_op jit(solution)/shard_map/ppermute | solution.py:414
  51.6 10.0 %collective-permute-start.13 = (bf16[1024,128]{1,0:T(8,128)(2,1)S(1)}, bf16[1024,128]{1,0:T(8,128)(2,1)S(1)}, u32[]{:S(2)}, u32[]{:S(2)}) collective-permute-start(bf16[1024,128]{1,0:T(8,128)(2,1)S(1)} %get-tuple-element.55), channel_id=1, source_target_pairs={{0,1},{1,0},{2,3},{3,2},{4,5},{5,4},{6,7},{7,6},{8,9},{9,8},{10,11... | collective-permute-start | bytes 786440 | tf_op jit(solution)/shard_map/ppermute | solution.py:411
  52.1 10.5 %collective-permute-start.5 = (bf16[1024,128]{1,0:T(8,128)(2,1)S(1)}, bf16[1024,128]{1,0:T(8,128)(2,1)S(1)}, u32[]{:S(2)}, u32[]{:S(2)}) collective-permute-start(bf16[1024,128]{1,0:T(8,128)(2,1)S(1)} %get-tuple-element.45), channel_id=1, source_target_pairs={{0,1},{1,0},{2,3},{3,2},{4,5},{5,4},{6,7},{7,6},{8,9},{9,8},{10,11... | collective-permute-start | bytes 786440 | tf_op jit(solution)/shard_map/ppermute | solution.py:414
  56.5 9.5 %collective-permute-start.6 = (bf16[1024,128]{1,0:T(8,128)(2,1)S(1)}, bf16[1024,128]{1,0:T(8,128)(2,1)S(1)}, u32[]{:S(2)}, u32[]{:S(2)}) collective-permute-start(bf16[1024,128]{1,0:T(8,128)(2,1)S(1)} %get-tuple-element.46), channel_id=1, source_target_pairs={{0,1},{1,0},{2,3},{3,2},{4,5},{5,4},{6,7},{7,6},{8,9},{9,8},{10,11... | collective-permute-start | bytes 786440 | tf_op jit(solution)/shard_map/ppermute | solution.py:411

commit v6 on v5

--- a/solution.py
+++ b/solution.py
@@ -19,12 +19,21 @@
     return [(i, i ^ 1) for i in range(devices)]
 
 
-def outer_route(wave, depth, devices):
+def outer_route(wave, depth, devices, near):
+    twin = (wave + 1) % depth
+    near = near and depth > 1
     pairs = []
     for layer in range(depth):
         for i in range(devices):
-            other = (i + 1 if i % 2 else i - 1) % devices if layer == wave else i ^ 1
-            pairs.append((layer * devices + i, layer * devices + other))
+            to, other = layer, (i + 1 if i % 2 else i - 1)
+            if layer != wave and not (near and layer == twin):
+                other = i ^ 1
+            elif not 0 <= other < devices:
+                if near:
+                    to, other = (twin if layer == wave else wave), i
+                else:
+                    other %= devices
+            pairs.append((layer * devices + i, to * devices + other))
     return pairs
 
 
@@ -332,12 +341,14 @@
     )(*index, inbound, tiles, sums)
 
 
-def combine_kernel(wave, part, has_through, final, *refs):
+def combine_kernel(wave, part, has_through, final, devices, *refs):
     own_ref, inner_ref, outer_ref = refs[:3]
+    partner = lax.axis_index("tile") + outer_window() - 1
+    outer = jnp.where((partner >= 0) & (partner < devices), outer_ref[...].astype(jnp.float32), 0.0)
     packed, width = outer_ref.shape
     own_rows = pl.ds(packed if own_ref.shape[0] > packed else 0, packed)
     inner_rows = pl.ds(part * packed if inner_ref.shape[0] > packed else 0, packed)
-    total = own_ref[own_rows, :] + inner_ref[inner_rows, :].astype(jnp.float32) + outer_ref[...].astype(jnp.float32)
+    total = own_ref[own_rows, :] + inner_ref[inner_rows, :].astype(jnp.float32) + outer
     if wave > 0:
         active = lax.axis_index("layer") == wave
         total = jnp.where(active, total, refs[3][...].astype(jnp.float32))
@@ -388,7 +399,7 @@
             args.append(result)
             specs.append(HBM)
     return pl.pallas_call(
-        functools.partial(combine_kernel, wave, part, through is not None, final),
+        functools.partial(combine_kernel, wave, part, through is not None, final, lax.axis_size("tile")),
         out_shape=outs,
         in_specs=specs,
         out_specs=out_specs,
@@ -407,8 +418,8 @@
     index = (in_hbm(tile_rows), in_hbm(tile_cols), tile_count)
     incident, sources, green_tiles = map(in_hbm, (incident, sources, green_tiles))
 
-    def across(payload, wave):
-        return lax.ppermute(payload, ("layer", "tile"), outer_route(wave, depth, devices))
+    def across(payload, wave, chunk):
+        return lax.ppermute(payload, ("layer", "tile"), outer_route(wave, depth, devices, wave == 0 and chunk < PARTS))
 
     def beside(payload):
         return lax.ppermute(payload, "tile", inner_route(devices))
@@ -429,14 +440,14 @@
         payloads += made[3:]
         chunks += [[made[1 + part], inner, None] for part in range(PARTS)]
     for c in range(min(PARTS + 1, len(chunks))):
-        chunks[c][2] = across(payloads[c], 0)
+        chunks[c][2] = across(payloads[c], 0, c)
     passed, leaving = [], []
     for c in range(len(chunks)):
         behind = c + PARTS
         through = payloads[behind] if PARTS < behind < len(chunks) else None
         made = total(0, c, *chunks[c], through=through)
         if through is not None:
-            chunks[behind][2] = across(made[1], 0)
+            chunks[behind][2] = across(made[1], 0, behind)
         leaving.append(made[0])
         if depth > 1:
             passed.append(down(made[0]))
@@ -448,7 +459,7 @@
             outer, inner, own = chunk_products(
                 wave, c // PARTS, c % PARTS, inbound, held, sums, index, blocks
             )
-            chunks.append((own, beside(inner), across(outer, wave)))
+            chunks.append((own, beside(inner), across(outer, wave, c)))
         if final:
             break
         leaving = [total(wave, c, *chunk, leaving[c])[0] for c, chunk in enumerate(chunks)]

time: 67.4 us -> 66.7 us (0.990)
  the two profiles are of different devices: /device:TPU:3 before, /device:TPU:22 now
where the time goes in v6:
time: 66.7 us; the launch traced here: 65.9 us
  starting transfers between devices  25.1 us (38%)
  waiting for transfers between devices  23.3 us (35%)
  Pallas kernels  16.3 us (24%)
  between operations  1.05 us (2%)
    ppermute x8, waiting for transfers between devices, across(): lax.ppermute(payload, ('layer', 'tile'), outer_route(wave, depth, devices...  23.3 us
    ppermute x4, starting transfers between devices, down(): return lax.ppermute(payload, 'layer', layer_route)  16.4 us
    ppermute x8, starting transfers between devices, across(): lax.ppermute(payload, ('layer', 'tile'), outer_route(wave, depth, devices...  6.59 us
    pallas_call x4, Pallas kernels, chunk_products(): pl.pallas_call(functools.partial(chunk_kernel, wave, blocks), out_shape=[...  5.91 us
    pallas_call x4, Pallas kernels, prepare(): pl.pallas_call(functools.partial(prepare_kernel, wave, front, part, rows_...  4.77 us
    pallas_call x1, Pallas kernels, open_products(): pl.pallas_call(functools.partial(open_kernel, blocks), out_shape=[outer,...  2.93 us
    pallas_call x8, Pallas kernels, combine(): pl.pallas_call(functools.partial(combine_kernel, wave, part, through is n...  2.67 us
    ppermute x6, starting transfers between devices, beside(): return lax.ppermute(payload, 'tile', inner_route(devices))  2.17 us
  transfers between devices with their start and end apart: 18, of which 6 were waited for; matrix products, arithmetic and copies ran while one was open for 0% of the time, Pallas kernels for 19%

profile of v6, /device:TPU:22, one launch (start us, length us, event | category | flops | bytes accessed | tf_op | source)
XLA Modules:
  0.0 65.9 jit_solution(1902503509191442115)
XLA Ops:
  0.7 2.9 %open.1 = (bf16[1024,128]{1,0:T(8,128)(2,1)S(1)}, bf16[1024,128]{1,0:T(8,128)(2,1)S(1)}, bf16[2,2048,128]{2,1,0:T(8,128)(2,1)S(1)}, bf16[12,2,256,256]{3,2,1,0:T...) custom-call(s32[1,12]{1,0:T(1,128)} %refs_0_.1, s32[1,12]{1,0:T(1,128)} %refs_1_.1, s32[1,1]{1,0:T(1,128)S(6)} %copy.19.refs_2_, ...), custom_call_target="tpu_custom_call" | custom-call | flops 500000000 | bytes 4000000 | tf_op jit(solution)/shard_map/open/pallas_call | solution.py:165
  3.8 0.5 collective-permute-start
  4.3 0.2 collective-permute-start.2
  4.5 1.6 %collective-permute-start.14 = (bf16[1024,128]{1,0:T(8,128)(2,1)S(1)}, bf16[1024,128]{1,0:T(8,128)(2,1)S(1)}, u32[]{:S(2)}, u32[]{:S(2)}) collective-permute-start(bf16[1024,128]{1,0:T(8,128)(2,1)S(1)} %get-tuple-element.57), channel_id=1, source_target_pairs={{0,16},{1,2},{2,1},{3,4},{4,3},{5,6},{6,5},{7,8},{8,7},{9,10},{10,... | collective-permute-start | bytes 786440 | tf_op jit(solution)/shard_map/ppermute | solution.py:422
  6.0 1.0 %collective-permute-start.7 = (bf16[1024,128]{1,0:T(8,128)(2,1)S(1)}, bf16[1024,128]{1,0:T(8,128)(2,1)S(1)}, u32[]{:S(2)}, u32[]{:S(2)}) collective-permute-start(bf16[1024,128]{1,0:T(8,128)(2,1)S(1)} %get-tuple-element.48), channel_id=1, source_target_pairs={{0,15},{1,2},{2,1},{3,4},{4,3},{5,6},{6,5},{7,8},{8,7},{9,10},{10,... | collective-permute-start | bytes 786440 | tf_op jit(solution)/shard_map/ppermute | solution.py:422
  7.0 8.7 %collective-permute-done.2.refs_2_ = bf16[1024,128]{1,0:T(8,128)(2,1)S(1)} collective-permute-done((bf16[1024,128]{1,0:T(8,128)(2,1)S(1)}, bf16[1024,128]{1,0:T(8,128)(2,1)S(1)}, u32[]{:S(2)}, u32[]{:S(2)}) %collective-permute-start.2) | collective-permute-done | bytes 262176 | tf_op jit(solution)/shard_map/ppermute | solution.py:422
  15.9 2.6 %collective-permute-done.14.refs_2_ = bf16[1024,128]{1,0:T(8,128)(2,1)S(1)} collective-permute-done((bf16[1024,128]{1,0:T(8,128)(2,1)S(1)}, bf16[1024,128]{1,0:T(8,128)(2,1)S(1)}, u32[]{:S(2)}, u32[]{:S(2)}) %collective-permute-start.14) | collective-permute-done | bytes 262176 | tf_op jit(solution)/shard_map/ppermute | solution.py:422
  18.5 0.1 combine_0_0_0.1.refs_3_
  18.6 11.5 %collective-permute-start.15 = (bf16[1024,128]{1,0:T(8,128)(2,1)S(1)}, bf16[1024,128]{1,0:T(8,128)(2,1)S(1)}, u32[]{:S(2)}, u32[]{:S(2)}) collective-permute-start(bf16[1024,128]{1,0:T(8,128)(2,1)S(1)} %combine_0_0_0.1.refs_3_), channel_id=1, source_target_pairs={{0,16},{16,0},{1,17},{17,1},{2,18},{18,2},{3,19},{19,3},{4,20},{20... | collective-permute-start | bytes 786440 | tf_op jit(solution)/shard_map/ppermute | solution.py:428
  30.2 0.1 combine_0_1_0.1.refs_3_
  30.3 2.7 %collective-permute-start.8 = (bf16[1024,128]{1,0:T(8,128)(2,1)S(1)}, bf16[1024,128]{1,0:T(8,128)(2,1)S(1)}, u32[]{:S(2)}, u32[]{:S(2)}) collective-permute-start(bf16[1024,128]{1,0:T(8,128)(2,1)S(1)} %combine_0_1_0.1.refs_3_), channel_id=1, source_target_pairs={{0,16},{16,0},{1,17},{17,1},{2,18},{18,2},{3,19},{19,3},{4,20},{20... | collective-permute-start | bytes 786440 | tf_op jit(solution)/shard_map/ppermute | solution.py:428
  33.0 1.2 %prepare_1_0_0.1.refs_5_ = f32[3200,128]{1,0:T(8,128)S(1)} custom-call(bf16[1,2,2048,128]{3,2,1,0:T(8,128)(2,1)} %sources.7), custom_call_target="tpu_custom_call" | custom-call | flops 1000000 | bytes 1000000 | tf_op jit(solution)/shard_map/prepare_1_0_0/pallas_call | solution.py:278
  34.2 1.2 %prepare_1_1_0.1.refs_5_ = f32[3200,128]{1,0:T(8,128)S(1)} custom-call(bf16[1,2,2048,128]{3,2,1,0:T(8,128)(2,1)} %sources.7), custom_call_target="tpu_custom_call" | custom-call | flops 1000000 | bytes 1000000 | tf_op jit(solution)/shard_map/prepare_1_1_0/pallas_call | solution.py:278
  35.5 0.1 combine_0_1_1.1.refs_3_
  35.6 2.1 %collective-permute-start.4 = (bf16[1024,128]{1,0:T(8,128)(2,1)S(1)}, bf16[1024,128]{1,0:T(8,128)(2,1)S(1)}, u32[]{:S(2)}, u32[]{:S(2)}) collective-permute-start(bf16[1024,128]{1,0:T(8,128)(2,1)S(1)} %combine_0_1_1.1.refs_3_), channel_id=1, source_target_pairs={{0,16},{16,0},{1,17},{17,1},{2,18},{18,2},{3,19},{19,3},{4,20},{20... | collective-permute-start | bytes 786440 | tf_op jit(solution)/shard_map/ppermute | solution.py:428
  37.7 1.4 %chunk_1_0_0.1 = (bf16[1024,128]{1,0:T(8,128)(2,1)S(1)}, bf16[1024,128]{1,0:T(8,128)(2,1)S(1)}, f32[3200,128]{1,0:T(8,128)S(1)}) custom-call(s32[1,12]{1,0:T(1,128)S(4)} %get-tuple-element.33.refs_0_, s32[1,12]{1,0:T(1,128)S(4)} %get-tuple-element.34.refs_1_, s32[1,1]{1,0:T(1,128)S(6)} %copy.19.refs_2_, ...), custom_call_target="tpu_custom_call", output_to_operand_aliasing={{2}: (5, {})} | custom-call | flops 1000000000 | bytes 5000000 | tf_op jit(solution)/shard_map/chunk_1_0_0/pallas_call | solution.py:333
  39.3 1.5 %chunk_1_1_0.1 = (bf16[1024,128]{1,0:T(8,128)(2,1)S(1)}, bf16[1024,128]{1,0:T(8,128)(2,1)S(1)}, f32[3200,128]{1,0:T(8,128)S(1)}) custom-call(s32[1,12]{1,0:T(1,128)S(4)} %get-tuple-element.33.refs_0_, s32[1,12]{1,0:T(1,128)S(4)} %get-tuple-element.34.refs_1_, s32[1,1]{1,0:T(1,128)S(6)} %copy.19.refs_2_, ...), custom_call_target="tpu_custom_call", output_to_operand_aliasing={{2}: (5, {})} | custom-call | flops 1000000000 | bytes 5000000 | tf_op jit(solution)/shard_map/chunk_1_1_0/pallas_call | solution.py:333
  40.7 1.8 %collective-permute-start.10 = (bf16[1024,128]{1,0:T(8,128)(2,1)S(1)}, bf16[1024,128]{1,0:T(8,128)(2,1)S(1)}, u32[]{:S(2)}, u32[]{:S(2)}) collective-permute-start(bf16[1024,128]{1,0:T(8,128)(2,1)S(1)} %get-tuple-element.51), channel_id=1, source_target_pairs={{0,1},{1,0},{2,3},{3,2},{4,5},{5,4},{6,7},{7,6},{8,9},{9,8},{10,11... | collective-permute-start | bytes 786440 | tf_op jit(solution)/shard_map/ppermute | solution.py:422
  42.5 1.2 %prepare_1_0_1.1.refs_5_ = f32[3200,128]{1,0:T(8,128)S(1)} custom-call(bf16[1,2,2048,128]{3,2,1,0:T(8,128)(2,1)} %sources.7), custom_call_target="tpu_custom_call" | custom-call | flops 1000000 | bytes 1000000 | tf_op jit(solution)/shard_map/prepare_1_0_1/pallas_call | solution.py:278
  43.7 1.2 %prepare_1_1_1.1.refs_5_ = f32[3200,128]{1,0:T(8,128)S(1)} custom-call(bf16[1,2,2048,128]{3,2,1,0:T(8,128)(2,1)} %sources.7), custom_call_target="tpu_custom_call" | custom-call | flops 1000000 | bytes 1000000 | tf_op jit(solution)/shard_map/prepare_1_1_1/pallas_call | solution.py:278
  44.9 1.5 %chunk_1_0_1.1 = (bf16[1024,128]{1,0:T(8,128)(2,1)S(1)}, bf16[1024,128]{1,0:T(8,128)(2,1)S(1)}, f32[3200,128]{1,0:T(8,128)S(1)}) custom-call(s32[1,12]{1,0:T(1,128)S(4)} %get-tuple-element.33.refs_0_, s32[1,12]{1,0:T(1,128)S(4)} %get-tuple-element.34.refs_1_, s32[1,1]{1,0:T(1,128)S(6)} %copy.19.refs_2_, ...), custom_call_target="tpu_custom_call", output_to_operand_aliasing={{2}: (5, {})} | custom-call | flops 1000000000 | bytes 5000000 | tf_op jit(solution)/shard_map/chunk_1_0_1/pallas_call | solution.py:333
  46.4 1.4 %collective-permute-start.12 = (bf16[1024,128]{1,0:T(8,128)(2,1)S(1)}, bf16[1024,128]{1,0:T(8,128)(2,1)S(1)}, u32[]{:S(2)}, u32[]{:S(2)}) collective-permute-start(bf16[1024,128]{1,0:T(8,128)(2,1)S(1)} %get-tuple-element.54), channel_id=1, source_target_pairs={{0,1},{1,0},{2,3},{3,2},{4,5},{5,4},{6,7},{7,6},{8,9},{9,8},{10,11... | collective-permute-start | bytes 786440 | tf_op jit(solution)/shard_map/ppermute | solution.py:425
  47.9 1.5 %chunk_1_1_1.1 = (bf16[1024,128]{1,0:T(8,128)(2,1)S(1)}, bf16[1024,128]{1,0:T(8,128)(2,1)S(1)}, f32[3200,128]{1,0:T(8,128)S(1)}) custom-call(s32[1,12]{1,0:T(1,128)S(4)} %get-tuple-element.33.refs_0_, s32[1,12]{1,0:T(1,128)S(4)} %get-tuple-element.34.refs_1_, s32[1,1]{1,0:T(1,128)S(6)} %copy.19.refs_2_, ...), custom_call_target="tpu_custom_call", output_to_operand_aliasing={{2}: (5, {})} | custom-call | flops 1000000000 | bytes 5000000 | tf_op jit(solution)/shard_map/chunk_1_1_1/pallas_call | solution.py:333
  49.5 1.1 %collective-permute-done.17.refs_2_ = bf16[1024,128]{1,0:T(8,128)(2,1)S(1)} collective-permute-done((bf16[1024,128]{1,0:T(8,128)(2,1)S(1)}, bf16[1024,128]{1,0:T(8,128)(2,1)S(1)}, u32[]{:S(2)}, u32[]{:S(2)}) %collective-permute-start.17) | collective-permute-done | bytes 262176 | tf_op jit(solution)/shard_map/ppermute | solution.py:422
  50.7 6.6 %collective-permute-done.10.refs_2_ = bf16[1024,128]{1,0:T(8,128)(2,1)S(1)} collective-permute-done((bf16[1024,128]{1,0:T(8,128)(2,1)S(1)}, bf16[1024,128]{1,0:T(8,128)(2,1)S(1)}, u32[]{:S(2)}, u32[]{:S(2)}) %collective-permute-start.10) | collective-permute-done | bytes 262176 | tf_op jit(solution)/shard_map/ppermute | solution.py:422
  57.2 1.9 %collective-permute-start.6 = (bf16[1024,128]{1,0:T(8,128)(2,1)S(1)}, bf16[1024,128]{1,0:T(8,128)(2,1)S(1)}, u32[]{:S(2)}, u32[]{:S(2)}) collective-permute-start(bf16[1024,128]{1,0:T(8,128)(2,1)S(1)} %get-tuple-element.46), channel_id=1, source_target_pairs={{0,1},{1,0},{2,3},{3,2},{4,5},{5,4},{6,7},{7,6},{8,9},{9,8},{10,11... | collective-permute-start | bytes 786440 | tf_op jit(solution)/shard_map/ppermute | solution.py:422
  59.1 0.1 combine_1_0_0.1.refs_4_
  59.3 0.1 combine_1_1_0.1.refs_4_
  59.4 2.5 %collective-permute-done.13.refs_2_ = bf16[1024,128]{1,0:T(8,128)(2,1)S(1)} collective-permute-done((bf16[1024,128]{1,0:T(8,128)(2,1)S(1)}, bf16[1024,128]{1,0:T(8,128)(2,1)S(1)}, u32[]{:S(2)}, u32[]{:S(2)}) %collective-permute-start.13) | collective-permute-done | bytes 262176 | tf_op jit(solution)/shard_map/ppermute | solution.py:422
  61.9 1.0 %combine_1_0_1.1.refs_5_ = bf16[1,2,2048,128]{3,2,1,0:T(8,128)(2,1)} custom-call(f32[3200,128]{1,0:T(8,128)S(1)} %get-tuple-element.53.refs_0_, bf16[1024,128]{1,0:T(8,128)(2,1)S(1)} %collective-permute-done.12.refs_1_, bf16[1024,128]{1,0:T(8,128)(2,1)S(1)} %collective-permute-done.13.refs_2_, bf16[1024,128]{1,0:T(8,128)(2,1)S(1)} %get-tuple-element.52.refs_3_, ...), custom_call_target="tpu_custom_call" | custom-call | flops 1000000 | bytes 1000000 | tf_op jit(solution)/shard_map/combine_1_0_1/pallas_call | solution.py:401
  62.9 1.8 %collective-permute-done.6.refs_2_ = bf16[1024,128]{1,0:T(8,128)(2,1)S(1)} collective-permute-done((bf16[1024,128]{1,0:T(8,128)(2,1)S(1)}, bf16[1024,128]{1,0:T(8,128)(2,1)S(1)}, u32[]{:S(2)}, u32[]{:S(2)}) %collective-permute-start.6) | collective-permute-done | bytes 262176 | tf_op jit(solution)/shard_map/ppermute | solution.py:422
  64.7 1.0 %combine_1_1_1.1 = bf16[1,2,2048,128]{3,2,1,0:T(8,128)(2,1)} custom-call(f32[3200,128]{1,0:T(8,128)S(1)} %get-tuple-element.44.refs_0_, bf16[1024,128]{1,0:T(8,128)(2,1)S(1)} %collective-permute-done.5.refs_1_, bf16[1024,128]{1,0:T(8,128)(2,1)S(1)} %collective-permute-done.6.refs_2_, ...), custom_call_target="tpu_custom_call", output_to_operand_aliasing={{}: (5, {})} | custom-call | flops 1000000 | bytes 1000000 | tf_op jit(solution)/shard_map/combine_1_1_1/pallas_call | solution.py:401
  (23 shorter events, 0.7 us)
Async XLA Ops:
  3.6 12.1 %collective-permute-start.1 = (bf16[2048,128]{1,0:T(8,128)(2,1)S(1)}, bf16[2048,128]{1,0:T(8,128)(2,1)S(1)}, u32[]{:S(2)}, u32[]{:S(2)}) collective-permute-start(bf16[2048,128]{1,0:T(8,128)(2,1)S(1)} %get-tuple-element.40), channel_id=1, source_target_pairs={{0,1},{1,0},{2,3},{3,2},{4,5},{5,4},{6,7},{7,6},{8,9},{9,8},{10,11... | collective-permute-start | bytes 1572872 | tf_op jit(solution)/shard_map/ppermute | solution.py:425
  3.8 26.4 %collective-permute-start = (bf16[2048,128]{1,0:T(8,128)(2,1)S(1)}, bf16[2048,128]{1,0:T(8,128)(2,1)S(1)}, u32[]{:S(2)}, u32[]{:S(2)}) collective-permute-start(bf16[2048,128]{1,0:T(8,128)(2,1)S(1)} %get-tuple-element.37), channel_id=1, source_target_pairs={{0,1},{1,0},{2,3},{3,2},{4,5},{5,4},{6,7},{7,6},{8,9},{9,8},{10,11... | collective-permute-start | bytes 1572872 | tf_op jit(solution)/shard_map/ppermute | solution.py:425
  4.3 11.4 %collective-permute-start.2 = (bf16[1024,128]{1,0:T(8,128)(2,1)S(1)}, bf16[1024,128]{1,0:T(8,128)(2,1)S(1)}, u32[]{:S(2)}, u32[]{:S(2)}) collective-permute-start(bf16[1024,128]{1,0:T(8,128)(2,1)S(1)} %get-tuple-element.41), channel_id=1, source_target_pairs={{0,16},{1,2},{2,1},{3,4},{4,3},{5,6},{6,5},{7,8},{8,7},{9,10},{10,... | collective-permute-start | bytes 786440 | tf_op jit(solution)/shard_map/ppermute | solution.py:422
  4.5 14.0 %collective-permute-start.14 = (bf16[1024,128]{1,0:T(8,128)(2,1)S(1)}, bf16[1024,128]{1,0:T(8,128)(2,1)S(1)}, u32[]{:S(2)}, u32[]{:S(2)}) collective-permute-start(bf16[1024,128]{1,0:T(8,128)(2,1)S(1)} %get-tuple-element.57), channel_id=1, source_target_pairs={{0,16},{1,2},{2,1},{3,4},{4,3},{5,6},{6,5},{7,8},{8,7},{9,10},{10,... | collective-permute-start | bytes 786440 | tf_op jit(solution)/shard_map/ppermute | solution.py:422
  6.0 24.1 %collective-permute-start.7 = (bf16[1024,128]{1,0:T(8,128)(2,1)S(1)}, bf16[1024,128]{1,0:T(8,128)(2,1)S(1)}, u32[]{:S(2)}, u32[]{:S(2)}) collective-permute-start(bf16[1024,128]{1,0:T(8,128)(2,1)S(1)} %get-tuple-element.48), channel_id=1, source_target_pairs={{0,15},{1,2},{2,1},{3,4},{4,3},{5,6},{6,5},{7,8},{8,7},{9,10},{10,... | collective-permute-start | bytes 786440 | tf_op jit(solution)/shard_map/ppermute | solution.py:422
  15.8 19.6 %collective-permute-start.3 = (bf16[1024,128]{1,0:T(8,128)(2,1)S(1)}, bf16[1024,128]{1,0:T(8,128)(2,1)S(1)}, u32[]{:S(2)}, u32[]{:S(2)}) collective-permute-start(bf16[1024,128]{1,0:T(8,128)(2,1)S(1)} %get-tuple-element.43), channel_id=1, source_target_pairs={{0,15},{1,2},{2,1},{3,4},{4,3},{5,6},{6,5},{7,8},{8,7},{9,10},{10,... | collective-permute-start | bytes 786440 | tf_op jit(solution)/shard_map/ppermute | solution.py:422
  18.6 19.0 %collective-permute-start.15 = (bf16[1024,128]{1,0:T(8,128)(2,1)S(1)}, bf16[1024,128]{1,0:T(8,128)(2,1)S(1)}, u32[]{:S(2)}, u32[]{:S(2)}) collective-permute-start(bf16[1024,128]{1,0:T(8,128)(2,1)S(1)} %combine_0_0_0.1.refs_3_), channel_id=1, source_target_pairs={{0,16},{16,0},{1,17},{17,1},{2,18},{18,2},{3,19},{19,3},{4,20},{20... | collective-permute-start | bytes 786440 | tf_op jit(solution)/shard_map/ppermute | solution.py:428
  30.3 9.0 %collective-permute-start.8 = (bf16[1024,128]{1,0:T(8,128)(2,1)S(1)}, bf16[1024,128]{1,0:T(8,128)(2,1)S(1)}, u32[]{:S(2)}, u32[]{:S(2)}) collective-permute-start(bf16[1024,128]{1,0:T(8,128)(2,1)S(1)} %combine_0_1_0.1.refs_3_), channel_id=1, source_target_pairs={{0,16},{16,0},{1,17},{17,1},{2,18},{18,2},{3,19},{19,3},{4,20},{20... | collective-permute-start | bytes 786440 | tf_op jit(solution)/shard_map/ppermute | solution.py:428
  35.4 9.5 %collective-permute-start.11 = (bf16[1024,128]{1,0:T(8,128)(2,1)S(1)}, bf16[1024,128]{1,0:T(8,128)(2,1)S(1)}, u32[]{:S(2)}, u32[]{:S(2)}) collective-permute-start(bf16[1024,128]{1,0:T(8,128)(2,1)S(1)} %get-tuple-element.52.refs_3_), channel_id=1, source_target_pairs={{0,16},{16,0},{1,17},{17,1},{2,18},{18,2},{3,19},{19,3},{4,20},{20... | collective-permute-start | bytes 786440 | tf_op jit(solution)/shard_map/ppermute | solution.py:428
  35.6 12.2 %collective-permute-start.4 = (bf16[1024,128]{1,0:T(8,128)(2,1)S(1)}, bf16[1024,128]{1,0:T(8,128)(2,1)S(1)}, u32[]{:S(2)}, u32[]{:S(2)}) collective-permute-start(bf16[1024,128]{1,0:T(8,128)(2,1)S(1)} %combine_0_1_1.1.refs_3_), channel_id=1, source_target_pairs={{0,16},{16,0},{1,17},{17,1},{2,18},{18,2},{3,19},{19,3},{4,20},{20... | collective-permute-start | bytes 786440 | tf_op jit(solution)/shard_map/ppermute | solution.py:428
  39.1 10.3 %collective-permute-start.16 = (bf16[1024,128]{1,0:T(8,128)(2,1)S(1)}, bf16[1024,128]{1,0:T(8,128)(2,1)S(1)}, u32[]{:S(2)}, u32[]{:S(2)}) collective-permute-start(bf16[1024,128]{1,0:T(8,128)(2,1)S(1)} %get-tuple-element.59), channel_id=1, source_target_pairs={{0,1},{1,0},{2,3},{3,2},{4,5},{5,4},{6,7},{7,6},{8,9},{9,8},{10,11... | collective-permute-start | bytes 786440 | tf_op jit(solution)/shard_map/ppermute | solution.py:425
  39.2 11.5 %collective-permute-start.17 = (bf16[1024,128]{1,0:T(8,128)(2,1)S(1)}, bf16[1024,128]{1,0:T(8,128)(2,1)S(1)}, u32[]{:S(2)}, u32[]{:S(2)}) collective-permute-start(bf16[1024,128]{1,0:T(8,128)(2,1)S(1)} %get-tuple-element.60), channel_id=1, source_target_pairs={{0,1},{1,0},{2,3},{3,2},{4,5},{5,4},{6,7},{7,6},{8,9},{9,8},{10,11... | collective-permute-start | bytes 786440 | tf_op jit(solution)/shard_map/ppermute | solution.py:422
  40.7 16.5 %collective-permute-start.10 = (bf16[1024,128]{1,0:T(8,128)(2,1)S(1)}, bf16[1024,128]{1,0:T(8,128)(2,1)S(1)}, u32[]{:S(2)}, u32[]{:S(2)}) collective-permute-start(bf16[1024,128]{1,0:T(8,128)(2,1)S(1)} %get-tuple-element.51), channel_id=1, source_target_pairs={{0,1},{1,0},{2,3},{3,2},{4,5},{5,4},{6,7},{7,6},{8,9},{9,8},{10,11... | collective-permute-start | bytes 786440 | tf_op jit(solution)/shard_map/ppermute | solution.py:422
  46.4 13.0 %collective-permute-start.12 = (bf16[1024,128]{1,0:T(8,128)(2,1)S(1)}, bf16[1024,128]{1,0:T(8,128)(2,1)S(1)}, u32[]{:S(2)}, u32[]{:S(2)}) collective-permute-start(bf16[1024,128]{1,0:T(8,128)(2,1)S(1)} %get-tuple-element.54), channel_id=1, source_target_pairs={{0,1},{1,0},{2,3},{3,2},{4,5},{5,4},{6,7},{7,6},{8,9},{9,8},{10,11... | collective-permute-start | bytes 786440 | tf_op jit(solution)/shard_map/ppermute | solution.py:425
  47.8 11.4 %collective-permute-start.9 = (bf16[1024,128]{1,0:T(8,128)(2,1)S(1)}, bf16[1024,128]{1,0:T(8,128)(2,1)S(1)}, u32[]{:S(2)}, u32[]{:S(2)}) collective-permute-start(bf16[1024,128]{1,0:T(8,128)(2,1)S(1)} %get-tuple-element.50), channel_id=1, source_target_pairs={{0,1},{1,0},{2,3},{3,2},{4,5},{5,4},{6,7},{7,6},{8,9},{9,8},{10,11... | collective-permute-start | bytes 786440 | tf_op jit(solution)/shard_map/ppermute | solution.py:425
  49.5 12.5 %collective-permute-start.13 = (bf16[1024,128]{1,0:T(8,128)(2,1)S(1)}, bf16[1024,128]{1,0:T(8,128)(2,1)S(1)}, u32[]{:S(2)}, u32[]{:S(2)}) collective-permute-start(bf16[1024,128]{1,0:T(8,128)(2,1)S(1)} %get-tuple-element.55), channel_id=1, source_target_pairs={{0,1},{1,0},{2,3},{3,2},{4,5},{5,4},{6,7},{7,6},{8,9},{9,8},{10,11... | collective-permute-start | bytes 786440 | tf_op jit(solution)/shard_map/ppermute | solution.py:422
  50.7 12.2 %collective-permute-start.5 = (bf16[1024,128]{1,0:T(8,128)(2,1)S(1)}, bf16[1024,128]{1,0:T(8,128)(2,1)S(1)}, u32[]{:S(2)}, u32[]{:S(2)}) collective-permute-start(bf16[1024,128]{1,0:T(8,128)(2,1)S(1)} %get-tuple-element.45), channel_id=1, source_target_pairs={{0,1},{1,0},{2,3},{3,2},{4,5},{5,4},{6,7},{7,6},{8,9},{9,8},{10,11... | collective-permute-start | bytes 786440 | tf_op jit(solution)/shard_map/ppermute | solution.py:425
  57.2 7.5 %collective-permute-start.6 = (bf16[1024,128]{1,0:T(8,128)(2,1)S(1)}, bf16[1024,128]{1,0:T(8,128)(2,1)S(1)}, u32[]{:S(2)}, u32[]{:S(2)}) collective-permute-start(bf16[1024,128]{1,0:T(8,128)(2,1)S(1)} %get-tuple-element.46), channel_id=1, source_target_pairs={{0,1},{1,0},{2,3},{3,2},{4,5},{5,4},{6,7},{7,6},{8,9},{9,8},{10,11... | collective-permute-start | bytes 786440 | tf_op jit(solution)/shard_map/ppermute | solution.py:422

commit v7 on v5

--- a/solution.py
+++ b/solution.py
@@ -332,12 +332,14 @@
     )(*index, inbound, tiles, sums)
 
 
-def combine_kernel(wave, part, has_through, final, *refs):
+def combine_kernel(wave, part, has_through, final, devices, *refs):
     own_ref, inner_ref, outer_ref = refs[:3]
+    partner = lax.axis_index("tile") + outer_window() - 1
+    outer = jnp.where((partner >= 0) & (partner < devices), outer_ref[...].astype(jnp.float32), 0.0)
     packed, width = outer_ref.shape
     own_rows = pl.ds(packed if own_ref.shape[0] > packed else 0, packed)
     inner_rows = pl.ds(part * packed if inner_ref.shape[0] > packed else 0, packed)
-    total = own_ref[own_rows, :] + inner_ref[inner_rows, :].astype(jnp.float32) + outer_ref[...].astype(jnp.float32)
+    total = own_ref[own_rows, :] + inner_ref[inner_rows, :].astype(jnp.float32) + outer
     if wave > 0:
         active = lax.axis_index("layer") == wave
         total = jnp.where(active, total, refs[3][...].astype(jnp.float32))
@@ -388,7 +390,7 @@
             args.append(result)
             specs.append(HBM)
     return pl.pallas_call(
-        functools.partial(combine_kernel, wave, part, through is not None, final),
+        functools.partial(combine_kernel, wave, part, through is not None, final, lax.axis_size("tile")),
         out_shape=outs,
         in_specs=specs,
         out_specs=out_specs,

time: 67.4 us -> 67.4 us (level)
  no operation moved by 1% of the time
where the time goes in v7:
time: 67.4 us; the launch traced here: 67.1 us
  starting transfers between devices  38.7 us (57%)
  Pallas kernels  16.3 us (24%)
  waiting for transfers between devices  11.1 us (16%)
  between operations  1.02 us (2%)
    ppermute x4, starting transfers between devices, down(): return lax.ppermute(payload, 'layer', layer_route)  27.3 us
    ppermute x8, waiting for transfers between devices, across(): lax.ppermute(payload, ('layer', 'tile'), outer_route(wave, depth, devices))  9.71 us
    ppermute x6, starting transfers between devices, beside(): return lax.ppermute(payload, 'tile', inner_route(devices))  7 us
    pallas_call x4, Pallas kernels, chunk_products(): pl.pallas_call(functools.partial(chunk_kernel, wave, blocks), out_shape=[...  5.89 us
    pallas_call x4, Pallas kernels, prepare(): pl.pallas_call(functools.partial(prepare_kernel, wave, front, part, rows_...  4.78 us
    ppermute x8, starting transfers between devices, across(): lax.ppermute(payload, ('layer', 'tile'), outer_route(wave, depth, devices))  4.35 us
    pallas_call x1, Pallas kernels, open_products(): pl.pallas_call(functools.partial(open_kernel, blocks), out_shape=[outer,...  2.93 us
    pallas_call x8, Pallas kernels, combine(): pl.pallas_call(functools.partial(combine_kernel, wave, part, through is n...  2.67 us
  transfers between devices with their start and end apart: 18, of which 4 were waited for; matrix products, arithmetic and copies ran while one was open for 0% of the time, Pallas kernels for 18%

profile of v7, /device:TPU:3, one launch (start us, length us, event | category | flops | bytes accessed | tf_op | source)
XLA Modules:
  0.0 67.1 jit_solution(3277040514585722268)
XLA Ops:
  0.7 2.9 %open.1 = (bf16[1024,128]{1,0:T(8,128)(2,1)S(1)}, bf16[1024,128]{1,0:T(8,128)(2,1)S(1)}, bf16[2,2048,128]{2,1,0:T(8,128)(2,1)S(1)}, bf16[12,2,256,256]{3,2,1,0:T...) custom-call(s32[1,12]{1,0:T(1,128)} %refs_0_.1, s32[1,12]{1,0:T(1,128)} %refs_1_.1, s32[1,1]{1,0:T(1,128)S(6)} %copy.19.refs_2_, ...), custom_call_target="tpu_custom_call" | custom-call | flops 500000000 | bytes 4000000 | tf_op jit(solution)/shard_map/open/pallas_call | solution.py:156
  3.6 0.7 %collective-permute-start.1 = (bf16[2048,128]{1,0:T(8,128)(2,1)S(1)}, bf16[2048,128]{1,0:T(8,128)(2,1)S(1)}, u32[]{:S(2)}, u32[]{:S(2)}) collective-permute-start(bf16[2048,128]{1,0:T(8,128)(2,1)S(1)} %get-tuple-element.40), channel_id=1, source_target_pairs={{0,1},{1,0},{2,3},{3,2},{4,5},{5,4},{6,7},{7,6},{8,9},{9,8},{10,11... | collective-permute-start | bytes 1572872 | tf_op jit(solution)/shard_map/ppermute | solution.py:416
  4.5 0.5 collective-permute-start.2
  5.1 0.4 collective-permute-start.7
  5.5 1.5 %collective-permute-done.2.refs_2_ = bf16[1024,128]{1,0:T(8,128)(2,1)S(1)} collective-permute-done((bf16[1024,128]{1,0:T(8,128)(2,1)S(1)}, bf16[1024,128]{1,0:T(8,128)(2,1)S(1)}, u32[]{:S(2)}, u32[]{:S(2)}) %collective-permute-start.2) | collective-permute-done | bytes 262176 | tf_op jit(solution)/shard_map/ppermute | solution.py:413
  7.0 0.1 combine_0_0_1.1
  7.1 0.4 collective-permute-start.3
  7.6 0.1 combine_0_0_0.1.refs_3_
  7.7 23.0 %collective-permute-start.15 = (bf16[1024,128]{1,0:T(8,128)(2,1)S(1)}, bf16[1024,128]{1,0:T(8,128)(2,1)S(1)}, u32[]{:S(2)}, u32[]{:S(2)}) collective-permute-start(bf16[1024,128]{1,0:T(8,128)(2,1)S(1)} %combine_0_0_0.1.refs_3_), channel_id=1, source_target_pairs={{0,16},{16,0},{1,17},{17,1},{2,18},{18,2},{3,19},{19,3},{4,20},{20... | collective-permute-start | bytes 786440 | tf_op jit(solution)/shard_map/ppermute | solution.py:419
  30.7 0.1 combine_0_1_0.1.refs_3_
  30.9 2.7 %collective-permute-start.8 = (bf16[1024,128]{1,0:T(8,128)(2,1)S(1)}, bf16[1024,128]{1,0:T(8,128)(2,1)S(1)}, u32[]{:S(2)}, u32[]{:S(2)}) collective-permute-start(bf16[1024,128]{1,0:T(8,128)(2,1)S(1)} %combine_0_1_0.1.refs_3_), channel_id=1, source_target_pairs={{0,16},{16,0},{1,17},{17,1},{2,18},{18,2},{3,19},{19,3},{4,20},{20... | collective-permute-start | bytes 786440 | tf_op jit(solution)/shard_map/ppermute | solution.py:419
  33.6 1.2 %prepare_1_0_0.1.refs_5_ = f32[3200,128]{1,0:T(8,128)S(1)} custom-call(bf16[1,2,2048,128]{3,2,1,0:T(8,128)(2,1)} %sources.7), custom_call_target="tpu_custom_call" | custom-call | flops 1000000 | bytes 1000000 | tf_op jit(solution)/shard_map/prepare_1_0_0/pallas_call | solution.py:269
  34.7 1.2 %prepare_1_1_0.1.refs_5_ = f32[3200,128]{1,0:T(8,128)S(1)} custom-call(bf16[1,2,2048,128]{3,2,1,0:T(8,128)(2,1)} %sources.7), custom_call_target="tpu_custom_call" | custom-call | flops 1000000 | bytes 1000000 | tf_op jit(solution)/shard_map/prepare_1_1_0/pallas_call | solution.py:269
  36.0 0.1 combine_0_1_1.1.refs_3_
  36.2 1.5 %collective-permute-start.4 = (bf16[1024,128]{1,0:T(8,128)(2,1)S(1)}, bf16[1024,128]{1,0:T(8,128)(2,1)S(1)}, u32[]{:S(2)}, u32[]{:S(2)}) collective-permute-start(bf16[1024,128]{1,0:T(8,128)(2,1)S(1)} %combine_0_1_1.1.refs_3_), channel_id=1, source_target_pairs={{0,16},{16,0},{1,17},{17,1},{2,18},{18,2},{3,19},{19,3},{4,20},{20... | collective-permute-start | bytes 786440 | tf_op jit(solution)/shard_map/ppermute | solution.py:419
  37.7 1.4 %chunk_1_0_0.1 = (bf16[1024,128]{1,0:T(8,128)(2,1)S(1)}, bf16[1024,128]{1,0:T(8,128)(2,1)S(1)}, f32[3200,128]{1,0:T(8,128)S(1)}) custom-call(s32[1,12]{1,0:T(1,128)S(4)} %get-tuple-element.33.refs_0_, s32[1,12]{1,0:T(1,128)S(4)} %get-tuple-element.34.refs_1_, s32[1,1]{1,0:T(1,128)S(6)} %copy.19.refs_2_, ...), custom_call_target="tpu_custom_call", output_to_operand_aliasing={{2}: (5, {})} | custom-call | flops 1000000000 | bytes 5000000 | tf_op jit(solution)/shard_map/chunk_1_0_0/pallas_call | solution.py:324
  39.2 2.4 %collective-permute-start.17 = (bf16[1024,128]{1,0:T(8,128)(2,1)S(1)}, bf16[1024,128]{1,0:T(8,128)(2,1)S(1)}, u32[]{:S(2)}, u32[]{:S(2)}) collective-permute-start(bf16[1024,128]{1,0:T(8,128)(2,1)S(1)} %get-tuple-element.60), channel_id=1, source_target_pairs={{0,1},{1,0},{2,3},{3,2},{4,5},{5,4},{6,7},{7,6},{8,9},{9,8},{10,11... | collective-permute-start | bytes 786440 | tf_op jit(solution)/shard_map/ppermute | solution.py:413
  41.5 1.4 %collective-permute-done.8.refs_3_ = bf16[1024,128]{1,0:T(8,128)(2,1)S(1)} collective-permute-done((bf16[1024,128]{1,0:T(8,128)(2,1)S(1)}, bf16[1024,128]{1,0:T(8,128)(2,1)S(1)}, u32[]{:S(2)}, u32[]{:S(2)}) %collective-permute-start.8) | collective-permute-done | bytes 262176 | tf_op jit(solution)/shard_map/ppermute | solution.py:419
  42.9 1.4 %chunk_1_1_0.1 = (bf16[1024,128]{1,0:T(8,128)(2,1)S(1)}, bf16[1024,128]{1,0:T(8,128)(2,1)S(1)}, f32[3200,128]{1,0:T(8,128)S(1)}) custom-call(s32[1,12]{1,0:T(1,128)S(4)} %get-tuple-element.33.refs_0_, s32[1,12]{1,0:T(1,128)S(4)} %get-tuple-element.34.refs_1_, s32[1,1]{1,0:T(1,128)S(6)} %copy.19.refs_2_, ...), custom_call_target="tpu_custom_call", output_to_operand_aliasing={{2}: (5, {})} | custom-call | flops 1000000000 | bytes 5000000 | tf_op jit(solution)/shard_map/chunk_1_1_0/pallas_call | solution.py:324
  44.4 1.2 %prepare_1_0_1.1.refs_5_ = f32[3200,128]{1,0:T(8,128)S(1)} custom-call(bf16[1,2,2048,128]{3,2,1,0:T(8,128)(2,1)} %sources.7), custom_call_target="tpu_custom_call" | custom-call | flops 1000000 | bytes 1000000 | tf_op jit(solution)/shard_map/prepare_1_0_1/pallas_call | solution.py:269
  45.7 1.2 %prepare_1_1_1.1.refs_5_ = f32[3200,128]{1,0:T(8,128)S(1)} custom-call(bf16[1,2,2048,128]{3,2,1,0:T(8,128)(2,1)} %sources.7), custom_call_target="tpu_custom_call" | custom-call | flops 1000000 | bytes 1000000 | tf_op jit(solution)/shard_map/prepare_1_1_1/pallas_call | solution.py:269
  46.9 1.5 %chunk_1_0_1.1 = (bf16[1024,128]{1,0:T(8,128)(2,1)S(1)}, bf16[1024,128]{1,0:T(8,128)(2,1)S(1)}, f32[3200,128]{1,0:T(8,128)S(1)}) custom-call(s32[1,12]{1,0:T(1,128)S(4)} %get-tuple-element.33.refs_0_, s32[1,12]{1,0:T(1,128)S(4)} %get-tuple-element.34.refs_1_, s32[1,1]{1,0:T(1,128)S(6)} %copy.19.refs_2_, ...), custom_call_target="tpu_custom_call", output_to_operand_aliasing={{2}: (5, {})} | custom-call | flops 1000000000 | bytes 5000000 | tf_op jit(solution)/shard_map/chunk_1_0_1/pallas_call | solution.py:324
  48.3 1.7 %collective-permute-start.12 = (bf16[1024,128]{1,0:T(8,128)(2,1)S(1)}, bf16[1024,128]{1,0:T(8,128)(2,1)S(1)}, u32[]{:S(2)}, u32[]{:S(2)}) collective-permute-start(bf16[1024,128]{1,0:T(8,128)(2,1)S(1)} %get-tuple-element.54), channel_id=1, source_target_pairs={{0,1},{1,0},{2,3},{3,2},{4,5},{5,4},{6,7},{7,6},{8,9},{9,8},{10,11... | collective-permute-start | bytes 786440 | tf_op jit(solution)/shard_map/ppermute | solution.py:416
  50.1 1.5 %chunk_1_1_1.1 = (bf16[1024,128]{1,0:T(8,128)(2,1)S(1)}, bf16[1024,128]{1,0:T(8,128)(2,1)S(1)}, f32[3200,128]{1,0:T(8,128)S(1)}) custom-call(s32[1,12]{1,0:T(1,128)S(4)} %get-tuple-element.33.refs_0_, s32[1,12]{1,0:T(1,128)S(4)} %get-tuple-element.34.refs_1_, s32[1,1]{1,0:T(1,128)S(6)} %copy.19.refs_2_, ...), custom_call_target="tpu_custom_call", output_to_operand_aliasing={{2}: (5, {})} | custom-call | flops 1000000000 | bytes 5000000 | tf_op jit(solution)/shard_map/chunk_1_1_1/pallas_call | solution.py:324
  51.7 0.5 collective-permute-start.13
  52.2 4.3 %collective-permute-start.5 = (bf16[1024,128]{1,0:T(8,128)(2,1)S(1)}, bf16[1024,128]{1,0:T(8,128)(2,1)S(1)}, u32[]{:S(2)}, u32[]{:S(2)}) collective-permute-start(bf16[1024,128]{1,0:T(8,128)(2,1)S(1)} %get-tuple-element.45), channel_id=1, source_target_pairs={{0,1},{1,0},{2,3},{3,2},{4,5},{5,4},{6,7},{7,6},{8,9},{9,8},{10,11... | collective-permute-start | bytes 786440 | tf_op jit(solution)/shard_map/ppermute | solution.py:416
  56.5 0.1 combine_1_0_0.1.refs_4_
  56.6 0.1 combine_1_1_0.1.refs_4_
  56.8 4.9 %collective-permute-done.13.refs_2_ = bf16[1024,128]{1,0:T(8,128)(2,1)S(1)} collective-permute-done((bf16[1024,128]{1,0:T(8,128)(2,1)S(1)}, bf16[1024,128]{1,0:T(8,128)(2,1)S(1)}, u32[]{:S(2)}, u32[]{:S(2)}) %collective-permute-start.13) | collective-permute-done | bytes 262176 | tf_op jit(solution)/shard_map/ppermute | solution.py:413
  61.7 1.0 %combine_1_0_1.1.refs_5_ = bf16[1,2,2048,128]{3,2,1,0:T(8,128)(2,1)} custom-call(f32[3200,128]{1,0:T(8,128)S(1)} %get-tuple-element.53.refs_0_, bf16[1024,128]{1,0:T(8,128)(2,1)S(1)} %collective-permute-done.12.refs_1_, bf16[1024,128]{1,0:T(8,128)(2,1)S(1)} %collective-permute-done.13.refs_2_, bf16[1024,128]{1,0:T(8,128)(2,1)S(1)} %get-tuple-element.52.refs_3_, ...), custom_call_target="tpu_custom_call" | custom-call | flops 1000000 | bytes 1000000 | tf_op jit(solution)/shard_map/combine_1_0_1/pallas_call | solution.py:392
  62.7 3.2 %collective-permute-done.6.refs_2_ = bf16[1024,128]{1,0:T(8,128)(2,1)S(1)} collective-permute-done((bf16[1024,128]{1,0:T(8,128)(2,1)S(1)}, bf16[1024,128]{1,0:T(8,128)(2,1)S(1)}, u32[]{:S(2)}, u32[]{:S(2)}) %collective-permute-start.6) | collective-permute-done | bytes 262176 | tf_op jit(solution)/shard_map/ppermute | solution.py:413
  66.0 1.0 %combine_1_1_1.1 = bf16[1,2,2048,128]{3,2,1,0:T(8,128)(2,1)} custom-call(f32[3200,128]{1,0:T(8,128)S(1)} %get-tuple-element.44.refs_0_, bf16[1024,128]{1,0:T(8,128)(2,1)S(1)} %collective-permute-done.5.refs_1_, bf16[1024,128]{1,0:T(8,128)(2,1)S(1)} %collective-permute-done.6.refs_2_, ...), custom_call_target="tpu_custom_call", output_to_operand_aliasing={{}: (5, {})} | custom-call | flops 1000000 | bytes 1000000 | tf_op jit(solution)/shard_map/combine_1_1_1/pallas_call | solution.py:392
  (23 shorter events, 0.6 us)
Async XLA Ops:
  3.6 3.4 %collective-permute-start.1 = (bf16[2048,128]{1,0:T(8,128)(2,1)S(1)}, bf16[2048,128]{1,0:T(8,128)(2,1)S(1)}, u32[]{:S(2)}, u32[]{:S(2)}) collective-permute-start(bf16[2048,128]{1,0:T(8,128)(2,1)S(1)} %get-tuple-element.40), channel_id=1, source_target_pairs={{0,1},{1,0},{2,3},{3,2},{4,5},{5,4},{6,7},{7,6},{8,9},{9,8},{10,11... | collective-permute-start | bytes 1572872 | tf_op jit(solution)/shard_map/ppermute | solution.py:416
  4.4 26.3 %collective-permute-start = (bf16[2048,128]{1,0:T(8,128)(2,1)S(1)}, bf16[2048,128]{1,0:T(8,128)(2,1)S(1)}, u32[]{:S(2)}, u32[]{:S(2)}) collective-permute-start(bf16[2048,128]{1,0:T(8,128)(2,1)S(1)} %get-tuple-element.37), channel_id=1, source_target_pairs={{0,1},{1,0},{2,3},{3,2},{4,5},{5,4},{6,7},{7,6},{8,9},{9,8},{10,11... | collective-permute-start | bytes 1572872 | tf_op jit(solution)/shard_map/ppermute | solution.py:416
  4.5 2.5 %collective-permute-start.2 = (bf16[1024,128]{1,0:T(8,128)(2,1)S(1)}, bf16[1024,128]{1,0:T(8,128)(2,1)S(1)}, u32[]{:S(2)}, u32[]{:S(2)}) collective-permute-start(bf16[1024,128]{1,0:T(8,128)(2,1)S(1)} %get-tuple-element.41), channel_id=1, source_target_pairs={{0,15},{1,2},{2,1},{3,4},{4,3},{5,6},{6,5},{7,8},{8,7},{9,10},{10,... | collective-permute-start | bytes 786440 | tf_op jit(solution)/shard_map/ppermute | solution.py:413
  5.0 2.6 %collective-permute-start.14 = (bf16[1024,128]{1,0:T(8,128)(2,1)S(1)}, bf16[1024,128]{1,0:T(8,128)(2,1)S(1)}, u32[]{:S(2)}, u32[]{:S(2)}) collective-permute-start(bf16[1024,128]{1,0:T(8,128)(2,1)S(1)} %get-tuple-element.57), channel_id=1, source_target_pairs={{0,15},{1,2},{2,1},{3,4},{4,3},{5,6},{6,5},{7,8},{8,7},{9,10},{10,... | collective-permute-start | bytes 786440 | tf_op jit(solution)/shard_map/ppermute | solution.py:413
  5.1 25.7 %collective-permute-start.7 = (bf16[1024,128]{1,0:T(8,128)(2,1)S(1)}, bf16[1024,128]{1,0:T(8,128)(2,1)S(1)}, u32[]{:S(2)}, u32[]{:S(2)}) collective-permute-start(bf16[1024,128]{1,0:T(8,128)(2,1)S(1)} %get-tuple-element.48), channel_id=1, source_target_pairs={{0,15},{1,2},{2,1},{3,4},{4,3},{5,6},{6,5},{7,8},{8,7},{9,10},{10,... | collective-permute-start | bytes 786440 | tf_op jit(solution)/shard_map/ppermute | solution.py:413
  7.1 28.9 %collective-permute-start.3 = (bf16[1024,128]{1,0:T(8,128)(2,1)S(1)}, bf16[1024,128]{1,0:T(8,128)(2,1)S(1)}, u32[]{:S(2)}, u32[]{:S(2)}) collective-permute-start(bf16[1024,128]{1,0:T(8,128)(2,1)S(1)} %get-tuple-element.43), channel_id=1, source_target_pairs={{0,15},{1,2},{2,1},{3,4},{4,3},{5,6},{6,5},{7,8},{8,7},{9,10},{10,... | collective-permute-start | bytes 786440 | tf_op jit(solution)/shard_map/ppermute | solution.py:413
  7.7 30.0 %collective-permute-start.15 = (bf16[1024,128]{1,0:T(8,128)(2,1)S(1)}, bf16[1024,128]{1,0:T(8,128)(2,1)S(1)}, u32[]{:S(2)}, u32[]{:S(2)}) collective-permute-start(bf16[1024,128]{1,0:T(8,128)(2,1)S(1)} %combine_0_0_0.1.refs_3_), channel_id=1, source_target_pairs={{0,16},{16,0},{1,17},{17,1},{2,18},{18,2},{3,19},{19,3},{4,20},{20... | collective-permute-start | bytes 786440 | tf_op jit(solution)/shard_map/ppermute | solution.py:419
  30.9 12.1 %collective-permute-start.8 = (bf16[1024,128]{1,0:T(8,128)(2,1)S(1)}, bf16[1024,128]{1,0:T(8,128)(2,1)S(1)}, u32[]{:S(2)}, u32[]{:S(2)}) collective-permute-start(bf16[1024,128]{1,0:T(8,128)(2,1)S(1)} %combine_0_1_0.1.refs_3_), channel_id=1, source_target_pairs={{0,16},{16,0},{1,17},{17,1},{2,18},{18,2},{3,19},{19,3},{4,20},{20... | collective-permute-start | bytes 786440 | tf_op jit(solution)/shard_map/ppermute | solution.py:419
  36.0 10.9 %collective-permute-start.11 = (bf16[1024,128]{1,0:T(8,128)(2,1)S(1)}, bf16[1024,128]{1,0:T(8,128)(2,1)S(1)}, u32[]{:S(2)}, u32[]{:S(2)}) collective-permute-start(bf16[1024,128]{1,0:T(8,128)(2,1)S(1)} %get-tuple-element.52.refs_3_), channel_id=1, source_target_pairs={{0,16},{16,0},{1,17},{17,1},{2,18},{18,2},{3,19},{19,3},{4,20},{20... | collective-permute-start | bytes 786440 | tf_op jit(solution)/shard_map/ppermute | solution.py:419
  36.2 13.9 %collective-permute-start.4 = (bf16[1024,128]{1,0:T(8,128)(2,1)S(1)}, bf16[1024,128]{1,0:T(8,128)(2,1)S(1)}, u32[]{:S(2)}, u32[]{:S(2)}) collective-permute-start(bf16[1024,128]{1,0:T(8,128)(2,1)S(1)} %combine_0_1_1.1.refs_3_), channel_id=1, source_target_pairs={{0,16},{16,0},{1,17},{17,1},{2,18},{18,2},{3,19},{19,3},{4,20},{20... | collective-permute-start | bytes 786440 | tf_op jit(solution)/shard_map/ppermute | solution.py:419
  39.1 12.5 %collective-permute-start.16 = (bf16[1024,128]{1,0:T(8,128)(2,1)S(1)}, bf16[1024,128]{1,0:T(8,128)(2,1)S(1)}, u32[]{:S(2)}, u32[]{:S(2)}) collective-permute-start(bf16[1024,128]{1,0:T(8,128)(2,1)S(1)} %get-tuple-element.59), channel_id=1, source_target_pairs={{0,1},{1,0},{2,3},{3,2},{4,5},{5,4},{6,7},{7,6},{8,9},{9,8},{10,11... | collective-permute-start | bytes 786440 | tf_op jit(solution)/shard_map/ppermute | solution.py:416
  39.2 13.0 %collective-permute-start.17 = (bf16[1024,128]{1,0:T(8,128)(2,1)S(1)}, bf16[1024,128]{1,0:T(8,128)(2,1)S(1)}, u32[]{:S(2)}, u32[]{:S(2)}) collective-permute-start(bf16[1024,128]{1,0:T(8,128)(2,1)S(1)} %get-tuple-element.60), channel_id=1, source_target_pairs={{0,1},{1,0},{2,3},{3,2},{4,5},{5,4},{6,7},{7,6},{8,9},{9,8},{10,11... | collective-permute-start | bytes 786440 | tf_op jit(solution)/shard_map/ppermute | solution.py:413
  44.4 12.1 %collective-permute-start.10 = (bf16[1024,128]{1,0:T(8,128)(2,1)S(1)}, bf16[1024,128]{1,0:T(8,128)(2,1)S(1)}, u32[]{:S(2)}, u32[]{:S(2)}) collective-permute-start(bf16[1024,128]{1,0:T(8,128)(2,1)S(1)} %get-tuple-element.51), channel_id=1, source_target_pairs={{0,1},{1,0},{2,3},{3,2},{4,5},{5,4},{6,7},{7,6},{8,9},{9,8},{10,11... | collective-permute-start | bytes 786440 | tf_op jit(solution)/shard_map/ppermute | solution.py:413
  48.3 8.5 %collective-permute-start.12 = (bf16[1024,128]{1,0:T(8,128)(2,1)S(1)}, bf16[1024,128]{1,0:T(8,128)(2,1)S(1)}, u32[]{:S(2)}, u32[]{:S(2)}) collective-permute-start(bf16[1024,128]{1,0:T(8,128)(2,1)S(1)} %get-tuple-element.54), channel_id=1, source_target_pairs={{0,1},{1,0},{2,3},{3,2},{4,5},{5,4},{6,7},{7,6},{8,9},{9,8},{10,11... | collective-permute-start | bytes 786440 | tf_op jit(solution)/shard_map/ppermute | solution.py:416
  50.0 6.6 %collective-permute-start.9 = (bf16[1024,128]{1,0:T(8,128)(2,1)S(1)}, bf16[1024,128]{1,0:T(8,128)(2,1)S(1)}, u32[]{:S(2)}, u32[]{:S(2)}) collective-permute-start(bf16[1024,128]{1,0:T(8,128)(2,1)S(1)} %get-tuple-element.50), channel_id=1, source_target_pairs={{0,1},{1,0},{2,3},{3,2},{4,5},{5,4},{6,7},{7,6},{8,9},{9,8},{10,11... | collective-permute-start | bytes 786440 | tf_op jit(solution)/shard_map/ppermute | solution.py:416
  51.7 10.0 %collective-permute-start.13 = (bf16[1024,128]{1,0:T(8,128)(2,1)S(1)}, bf16[1024,128]{1,0:T(8,128)(2,1)S(1)}, u32[]{:S(2)}, u32[]{:S(2)}) collective-permute-start(bf16[1024,128]{1,0:T(8,128)(2,1)S(1)} %get-tuple-element.55), channel_id=1, source_target_pairs={{0,1},{1,0},{2,3},{3,2},{4,5},{5,4},{6,7},{7,6},{8,9},{9,8},{10,11... | collective-permute-start | bytes 786440 | tf_op jit(solution)/shard_map/ppermute | solution.py:413
  52.2 10.6 %collective-permute-start.5 = (bf16[1024,128]{1,0:T(8,128)(2,1)S(1)}, bf16[1024,128]{1,0:T(8,128)(2,1)S(1)}, u32[]{:S(2)}, u32[]{:S(2)}) collective-permute-start(bf16[1024,128]{1,0:T(8,128)(2,1)S(1)} %get-tuple-element.45), channel_id=1, source_target_pairs={{0,1},{1,0},{2,3},{3,2},{4,5},{5,4},{6,7},{7,6},{8,9},{9,8},{10,11... | collective-permute-start | bytes 786440 | tf_op jit(solution)/shard_map/ppermute | solution.py:416
  56.5 9.5 %collective-permute-start.6 = (bf16[1024,128]{1,0:T(8,128)(2,1)S(1)}, bf16[1024,128]{1,0:T(8,128)(2,1)S(1)}, u32[]{:S(2)}, u32[]{:S(2)}) collective-permute-start(bf16[1024,128]{1,0:T(8,128)(2,1)S(1)} %get-tuple-element.46), channel_id=1, source_target_pairs={{0,1},{1,0},{2,3},{3,2},{4,5},{5,4},{6,7},{7,6},{8,9},{9,8},{10,11... | collective-permute-start | bytes 786440 | tf_op jit(solution)/shard_map/ppermute | solution.py:413

commit v8 on v5

--- a/solution.py
+++ b/solution.py
@@ -89,6 +89,11 @@
     return 2 * lax.rem(lax.axis_index("tile"), 2)
 
 
+def fetched_first(i, active, count_s, rows_s, blocks):
+    window = rows_s[0, i] - (lax.axis_index("tile") - 1) * blocks
+    return active & (i < count_s[0, 0]) & (lax.div(window, blocks) == outer_window())
+
+
 def open_kernel(blocks, *refs):
     index_refs, (incident, stored, *outer_refs), (pair, tiles) = refs[:3], refs[3:7], refs[7:9]
     rows_s, cols_s, sums, sems, tile_sems = refs[9:]
@@ -106,18 +111,19 @@
 
     for copy in copies:
         copy.start()
-    early = slots // 4
-    for i in range(early):
-        tile_copy(i).start()
+    copies[0].wait()
+    copies[1].wait()
+    first = (lax.axis_index("tile") - 1) * blocks
+
+    @pl.loop(0, slots)
+    def _(i):
+        pl.when(fetched_first(i, active, index_refs[2], rows_s, blocks))(lambda: tile_copy(i).start())
 
     @pl.when(active)
     def _():
         sums[...] = jnp.zeros(sums.shape, jnp.float32)
 
-    for copy in copies:
-        copy.wait()
-    for i in range(early, slots):
-        tile_copy(i).start()
+    copies[2].wait()
 
     @pl.when(active)
     def _():
@@ -125,18 +131,14 @@
             rows = pl.ds(r * tile_size, tile_size)
             pair[1, rows, :] = turn(pair[0, rows, :].astype(jnp.float32)).astype(jnp.bfloat16)
 
-    count = index_refs[2][0, 0]
-    first = (lax.axis_index("tile") - 1) * blocks
-
     @pl.loop(0, slots)
     def _(i):
-        tile_copy(i).wait()
-        window = rows_s[0, i] - first
-
-        @pl.when(active & (i < count) & (lax.div(window, blocks) == outer_window()))
+        @pl.when(fetched_first(i, active, index_refs[2], rows_s, blocks))
         def _():
+            tile_copy(i).wait()
             rows = pl.ds(pl.multiple_of(cols_s[0, i] * tile_size, tile_size), tile_size)
-            target = pl.ds(pl.multiple_of(lax.rem(window, blocks) * tile_size, tile_size), tile_size)
+            place = lax.rem(rows_s[0, i] - first, blocks)
+            target = pl.ds(pl.multiple_of(place * tile_size, tile_size), tile_size)
             term = jnp.dot(tiles[i, 0], pair[0, rows, :], preferred_element_type=jnp.float32)
             term += jnp.dot(tiles[i, 1], pair[1, rows, :], preferred_element_type=jnp.float32)
             sums[target, :] += term
@@ -176,22 +178,42 @@
 
 def front_kernel(front, blocks, *refs):
     index_refs, sources, tiles, operand = refs[:3], refs[3], refs[4], refs[5]
-    own = 3 if front == 0 else 4
-    outs, (source_v, sums, sems, *rest) = refs[6:-own], refs[-own:]
+    outs, (source_v, sums, sems, *rest) = refs[6 if front else 7 : -4], refs[-4:]
     inner_ref, own_refs, outer_refs = outs[0], outs[1:3], outs[3:]
+    active = lax.axis_index("layer") == 0
+    if front == 0:
+        stored, tiles = refs[6], outs[3]
+
+        @pl.loop(0, tiles.shape[0])
+        def _(i):
+            done = fetched_first(i, active, index_refs[2], index_refs[0], blocks)
+            copy = pltpu.make_async_copy(stored.at[0, i], tiles.at[i], rest[0].at[i])
+            pl.when(jnp.logical_not(done))(copy.start)
+
     pair = operand if front == 0 else rest[0]
     tile_size = tiles.shape[-1]
     rows_dev = pair.shape[1]
     packed = rows_dev // 2
-
-    @pl.when(lax.axis_index("layer") == 0)
-    def _():
-        copies = [pltpu.make_async_copy(sources.at[0, front], source_v, sems.at[0])]
-        if front > 0:
-            copies.insert(0, pltpu.make_async_copy(operand.at[front], pair.at[0], sems.at[1]))
+    copies = [pltpu.make_async_copy(sources.at[0, front], source_v, sems.at[0])]
+    if front > 0:
+        copies.insert(0, pltpu.make_async_copy(operand.at[front], pair.at[0], sems.at[1]))
+
+    @pl.when(active)
+    def _():
         for copy in copies:
             copy.start()
         sums[...] = jnp.zeros(sums.shape, jnp.float32)
+
+    if front == 0:
+
+        @pl.loop(0, tiles.shape[0])
+        def _(i):
+            done = fetched_first(i, active, index_refs[2], index_refs[0], blocks)
+            copy = pltpu.make_async_copy(stored.at[0, i], tiles.at[i], rest[0].at[i])
+            pl.when(jnp.logical_not(done))(copy.wait)
+
+    @pl.when(active)
+    def _():
         if front > 0:
             copies[0].wait()
             for r in range(blocks):
@@ -223,7 +245,7 @@
     )
 
 
-def front_products(front, operand, sources, tiles, index, blocks):
+def front_products(front, operand, sources, tiles, index, blocks, stored=None):
     rows_dev, width = sources.shape[-2:]
     tile_size = tiles.shape[-1]
     outer = pltpu.VMEM((rows_dev // 2, width), jnp.bfloat16)
@@ -234,16 +256,25 @@
         pltpu.VMEM((3 * rows_dev + tile_size, width), jnp.float32),
         pltpu.SemaphoreType.DMA((2,)),
     ]
+    args, specs, aliases = [*index, sources, tiles, operand], [SMEM, SMEM, SMEM, HBM, VMEM], {}
+    specs.append(HBM if front else VMEM)
     if front:
         scratch.append(pltpu.VMEM((2, rows_dev, width), jnp.bfloat16))
+    else:
+        scratch.append(pltpu.SemaphoreType.DMA((tiles.shape[0],)))
+        outs.append(pltpu.VMEM(tiles.shape, tiles.dtype))
+        args.append(stored)
+        specs.append(HBM)
+        aliases = {4: 3}
     return pl.pallas_call(
         functools.partial(front_kernel, front, blocks),
         out_shape=outs,
-        in_specs=[SMEM, SMEM, SMEM, HBM, VMEM, HBM if front else VMEM],
+        in_specs=specs,
+        input_output_aliases=aliases,
         out_specs=[VMEM] * len(outs),
         scratch_shapes=scratch,
         **kernel_options(f"front_{front}", 10**9, 5 * 10**6, 6),
-    )(*index, sources, tiles, operand)
+    )(*args)
 
 
 def prepare_kernel(wave, front, part, blocks, sources, sums, source_v, sem):
@@ -424,7 +455,10 @@
     index = (*first[4:], tile_count)
     chunks = []
     for front in range(fronts):
-        made = front_products(front, incident if front else first[2], sources, held, index, blocks)
+        operand = incident if front else first[2]
+        made = front_products(front, operand, sources, held, index, blocks, green_tiles)
+        if front == 0:
+            held, made = made[3], made[:3]
         inner = beside(made[0])
         payloads += made[3:]
         chunks += [[made[1 + part], inner, None] for part in range(PARTS)]

time: 67.4 us -> 67.7 us (level)
    pallas_call x2, Pallas kernels: 0.05 us -> 2.02 us  [front_products(): pl.pallas_call(functools.partial(front_kernel, front, blocks), out_shape=...]
    pallas_call x1, Pallas kernels: 2.93 us -> 1.18 us  [open_products(): pl.pallas_call(functools.partial(open_kernel, blocks), out_shape=[outer,...]
where the time goes in v8:
time: 67.7 us; the launch traced here: 67.4 us
  starting transfers between devices  38.8 us (57%)
  Pallas kernels  16.4 us (24%)
  waiting for transfers between devices  11.2 us (17%)
  between operations  1.02 us (2%)
    ppermute x4, starting transfers between devices, down(): return lax.ppermute(payload, 'layer', layer_route)  27.5 us
    ppermute x8, waiting for transfers between devices, across(): lax.ppermute(payload, ('layer', 'tile'), outer_route(wave, depth, devices))  9.78 us
    ppermute x6, starting transfers between devices, beside(): return lax.ppermute(payload, 'tile', inner_route(devices))  6.85 us
    pallas_call x4, Pallas kernels, chunk_products(): pl.pallas_call(functools.partial(chunk_kernel, wave, blocks), out_shape=[...  5.89 us
    pallas_call x4, Pallas kernels, prepare(): pl.pallas_call(functools.partial(prepare_kernel, wave, front, part, rows_...  4.78 us
    ppermute x8, starting transfers between devices, across(): lax.ppermute(payload, ('layer', 'tile'), outer_route(wave, depth, devices))  4.42 us
    pallas_call x8, Pallas kernels, combine(): pl.pallas_call(functools.partial(combine_kernel, wave, part, through is n...  2.5 us
    pallas_call x2, Pallas kernels, front_products(): pl.pallas_call(functools.partial(front_kernel, front, blocks), out_shape=...  2.02 us
  transfers between devices with their start and end apart: 18, of which 4 were waited for; matrix products, arithmetic and copies ran while one was open for 0% of the time, Pallas kernels for 18%

profile of v8, /device:TPU:3, one launch (start us, length us, event | category | flops | bytes accessed | tf_op | source)
XLA Modules:
  0.0 67.4 jit_solution(10489238572189849570)
XLA Ops:
  0.7 1.2 %open.1 = (bf16[1024,128]{1,0:T(8,128)(2,1)S(1)}, bf16[1024,128]{1,0:T(8,128)(2,1)S(1)}, bf16[2,2048,128]{2,1,0:T(8,128)(2,1)S(1)}, bf16[12,2,256,256]{3,2,1,0:T...) custom-call(s32[1,12]{1,0:T(1,128)} %refs_0_.1, s32[1,12]{1,0:T(1,128)} %refs_1_.1, s32[1,1]{1,0:T(1,128)S(6)} %copy.21.refs_2_, ...), custom_call_target="tpu_custom_call" | custom-call | flops 500000000 | bytes 4000000 | tf_op jit(solution)/shard_map/open/pallas_call | solution.py:158
  1.8 2.0 %front_0.1 = (bf16[2048,128]{1,0:T(8,128)(2,1)S(1)}, f32[1024,128]{1,0:T(8,128)S(1)}, f32[1024,128]{1,0:T(8,128)S(1)}, bf16[12,2,256,256]{3,2,1,0:T(8,128)(2,1)S(1)}) custom-call(s32[1,12]{1,0:T(1,128)S(4)} %get-tuple-element.34.refs_0_, s32[1,12]{1,0:T(1,128)S(4)} %get-tuple-element.35.refs_1_, ...), custom_call_target="tpu_custom_call", output_to_operand_aliasing={{3}: (4, {})} | custom-call | flops 1000000000 | bytes 5000000 | tf_op jit(solution)/shard_map/front_0/pallas_call | solution.py:269
  3.8 0.7 %collective-permute-start.1 = (bf16[2048,128]{1,0:T(8,128)(2,1)S(1)}, bf16[2048,128]{1,0:T(8,128)(2,1)S(1)}, u32[]{:S(2)}, u32[]{:S(2)}) collective-permute-start(bf16[2048,128]{1,0:T(8,128)(2,1)S(1)} %get-tuple-element.42), channel_id=1, source_target_pairs={{0,1},{1,0},{2,3},{3,2},{4,5},{5,4},{6,7},{7,6},{8,9},{9,8},{10,11... | collective-permute-start | bytes 1572872 | tf_op jit(solution)/shard_map/ppermute | solution.py:445
  4.6 0.1 collective-permute-start
  4.7 0.5 collective-permute-start.2
  5.3 0.4 collective-permute-start.7
  5.7 1.5 %collective-permute-done.2.refs_2_ = bf16[1024,128]{1,0:T(8,128)(2,1)S(1)} collective-permute-done((bf16[1024,128]{1,0:T(8,128)(2,1)S(1)}, bf16[1024,128]{1,0:T(8,128)(2,1)S(1)}, u32[]{:S(2)}, u32[]{:S(2)}) %collective-permute-start.2) | collective-permute-done | bytes 262176 | tf_op jit(solution)/shard_map/ppermute | solution.py:442
  7.3 0.4 collective-permute-start.3
  7.9 23.2 %collective-permute-start.15 = (bf16[1024,128]{1,0:T(8,128)(2,1)S(1)}, bf16[1024,128]{1,0:T(8,128)(2,1)S(1)}, u32[]{:S(2)}, u32[]{:S(2)}) collective-permute-start(bf16[1024,128]{1,0:T(8,128)(2,1)S(1)} %combine_0_0_0.1.refs_3_), channel_id=1, source_target_pairs={{0,16},{16,0},{1,17},{17,1},{2,18},{18,2},{3,19},{19,3},{4,20},{20... | collective-permute-start | bytes 786440 | tf_op jit(solution)/shard_map/ppermute | solution.py:448
  31.2 2.7 %collective-permute-start.8 = (bf16[1024,128]{1,0:T(8,128)(2,1)S(1)}, bf16[1024,128]{1,0:T(8,128)(2,1)S(1)}, u32[]{:S(2)}, u32[]{:S(2)}) collective-permute-start(bf16[1024,128]{1,0:T(8,128)(2,1)S(1)} %combine_0_1_0.1.refs_3_), channel_id=1, source_target_pairs={{0,16},{16,0},{1,17},{17,1},{2,18},{18,2},{3,19},{19,3},{4,20},{20... | collective-permute-start | bytes 786440 | tf_op jit(solution)/shard_map/ppermute | solution.py:448
  33.9 1.2 %prepare_1_0_0.1.refs_5_ = f32[3200,128]{1,0:T(8,128)S(1)} custom-call(bf16[1,2,2048,128]{3,2,1,0:T(8,128)(2,1)} %sources.7), custom_call_target="tpu_custom_call" | custom-call | flops 1000000 | bytes 1000000 | tf_op jit(solution)/shard_map/prepare_1_0_0/pallas_call | solution.py:300
  35.1 1.2 %prepare_1_1_0.1.refs_5_ = f32[3200,128]{1,0:T(8,128)S(1)} custom-call(bf16[1,2,2048,128]{3,2,1,0:T(8,128)(2,1)} %sources.7), custom_call_target="tpu_custom_call" | custom-call | flops 1000000 | bytes 1000000 | tf_op jit(solution)/shard_map/prepare_1_1_0/pallas_call | solution.py:300
  36.4 0.1 combine_0_1_1.1.refs_3_
  36.5 1.5 %collective-permute-start.4 = (bf16[1024,128]{1,0:T(8,128)(2,1)S(1)}, bf16[1024,128]{1,0:T(8,128)(2,1)S(1)}, u32[]{:S(2)}, u32[]{:S(2)}) collective-permute-start(bf16[1024,128]{1,0:T(8,128)(2,1)S(1)} %combine_0_1_1.1.refs_3_), channel_id=1, source_target_pairs={{0,16},{16,0},{1,17},{17,1},{2,18},{18,2},{3,19},{19,3},{4,20},{20... | collective-permute-start | bytes 786440 | tf_op jit(solution)/shard_map/ppermute | solution.py:448
  38.0 1.4 %chunk_1_0_0.1 = (bf16[1024,128]{1,0:T(8,128)(2,1)S(1)}, bf16[1024,128]{1,0:T(8,128)(2,1)S(1)}, f32[3200,128]{1,0:T(8,128)S(1)}) custom-call(s32[1,12]{1,0:T(1,128)S(4)} %get-tuple-element.34.refs_0_, s32[1,12]{1,0:T(1,128)S(4)} %get-tuple-element.35.refs_1_, s32[1,1]{1,0:T(1,128)S(6)} %copy.21.refs_2_, ...), custom_call_target="tpu_custom_call", output_to_operand_aliasing={{2}: (5, {})} | custom-call | flops 1000000000 | bytes 5000000 | tf_op jit(solution)/shard_map/chunk_1_0_0/pallas_call | solution.py:355
  39.5 2.4 %collective-permute-start.17 = (bf16[1024,128]{1,0:T(8,128)(2,1)S(1)}, bf16[1024,128]{1,0:T(8,128)(2,1)S(1)}, u32[]{:S(2)}, u32[]{:S(2)}) collective-permute-start(bf16[1024,128]{1,0:T(8,128)(2,1)S(1)} %get-tuple-element.62), channel_id=1, source_target_pairs={{0,1},{1,0},{2,3},{3,2},{4,5},{5,4},{6,7},{7,6},{8,9},{9,8},{10,11... | collective-permute-start | bytes 786440 | tf_op jit(solution)/shard_map/ppermute | solution.py:442
  41.9 1.4 %collective-permute-done.8.refs_3_ = bf16[1024,128]{1,0:T(8,128)(2,1)S(1)} collective-permute-done((bf16[1024,128]{1,0:T(8,128)(2,1)S(1)}, bf16[1024,128]{1,0:T(8,128)(2,1)S(1)}, u32[]{:S(2)}, u32[]{:S(2)}) %collective-permute-start.8) | collective-permute-done | bytes 262176 | tf_op jit(solution)/shard_map/ppermute | solution.py:448
  43.3 1.4 %chunk_1_1_0.1 = (bf16[1024,128]{1,0:T(8,128)(2,1)S(1)}, bf16[1024,128]{1,0:T(8,128)(2,1)S(1)}, f32[3200,128]{1,0:T(8,128)S(1)}) custom-call(s32[1,12]{1,0:T(1,128)S(4)} %get-tuple-element.34.refs_0_, s32[1,12]{1,0:T(1,128)S(4)} %get-tuple-element.35.refs_1_, s32[1,1]{1,0:T(1,128)S(6)} %copy.21.refs_2_, ...), custom_call_target="tpu_custom_call", output_to_operand_aliasing={{2}: (5, {})} | custom-call | flops 1000000000 | bytes 5000000 | tf_op jit(solution)/shard_map/chunk_1_1_0/pallas_call | solution.py:355
  44.8 1.2 %prepare_1_0_1.1.refs_5_ = f32[3200,128]{1,0:T(8,128)S(1)} custom-call(bf16[1,2,2048,128]{3,2,1,0:T(8,128)(2,1)} %sources.7), custom_call_target="tpu_custom_call" | custom-call | flops 1000000 | bytes 1000000 | tf_op jit(solution)/shard_map/prepare_1_0_1/pallas_call | solution.py:300
  46.0 1.2 %prepare_1_1_1.1.refs_5_ = f32[3200,128]{1,0:T(8,128)S(1)} custom-call(bf16[1,2,2048,128]{3,2,1,0:T(8,128)(2,1)} %sources.7), custom_call_target="tpu_custom_call" | custom-call | flops 1000000 | bytes 1000000 | tf_op jit(solution)/shard_map/prepare_1_1_1/pallas_call | solution.py:300
  47.2 1.5 %chunk_1_0_1.1 = (bf16[1024,128]{1,0:T(8,128)(2,1)S(1)}, bf16[1024,128]{1,0:T(8,128)(2,1)S(1)}, f32[3200,128]{1,0:T(8,128)S(1)}) custom-call(s32[1,12]{1,0:T(1,128)S(4)} %get-tuple-element.34.refs_0_, s32[1,12]{1,0:T(1,128)S(4)} %get-tuple-element.35.refs_1_, s32[1,1]{1,0:T(1,128)S(6)} %copy.21.refs_2_, ...), custom_call_target="tpu_custom_call", output_to_operand_aliasing={{2}: (5, {})} | custom-call | flops 1000000000 | bytes 5000000 | tf_op jit(solution)/shard_map/chunk_1_0_1/pallas_call | solution.py:355
  48.7 1.6 %collective-permute-start.12 = (bf16[1024,128]{1,0:T(8,128)(2,1)S(1)}, bf16[1024,128]{1,0:T(8,128)(2,1)S(1)}, u32[]{:S(2)}, u32[]{:S(2)}) collective-permute-start(bf16[1024,128]{1,0:T(8,128)(2,1)S(1)} %get-tuple-element.56), channel_id=1, source_target_pairs={{0,1},{1,0},{2,3},{3,2},{4,5},{5,4},{6,7},{7,6},{8,9},{9,8},{10,11... | collective-permute-start | bytes 786440 | tf_op jit(solution)/shard_map/ppermute | solution.py:445
  50.3 0.1 collective-permute-start.9
  50.4 1.5 %chunk_1_1_1.1 = (bf16[1024,128]{1,0:T(8,128)(2,1)S(1)}, bf16[1024,128]{1,0:T(8,128)(2,1)S(1)}, f32[3200,128]{1,0:T(8,128)S(1)}) custom-call(s32[1,12]{1,0:T(1,128)S(4)} %get-tuple-element.34.refs_0_, s32[1,12]{1,0:T(1,128)S(4)} %get-tuple-element.35.refs_1_, s32[1,1]{1,0:T(1,128)S(6)} %copy.21.refs_2_, ...), custom_call_target="tpu_custom_call", output_to_operand_aliasing={{2}: (5, {})} | custom-call | flops 1000000000 | bytes 5000000 | tf_op jit(solution)/shard_map/chunk_1_1_1/pallas_call | solution.py:355
  52.0 0.6 collective-permute-start.13
  52.5 4.2 %collective-permute-start.5 = (bf16[1024,128]{1,0:T(8,128)(2,1)S(1)}, bf16[1024,128]{1,0:T(8,128)(2,1)S(1)}, u32[]{:S(2)}, u32[]{:S(2)}) collective-permute-start(bf16[1024,128]{1,0:T(8,128)(2,1)S(1)} %get-tuple-element.47), channel_id=1, source_target_pairs={{0,1},{1,0},{2,3},{3,2},{4,5},{5,4},{6,7},{7,6},{8,9},{9,8},{10,11... | collective-permute-start | bytes 786440 | tf_op jit(solution)/shard_map/ppermute | solution.py:445
  56.8 0.1 combine_1_0_0.1.refs_4_
  56.9 0.1 combine_1_1_0.1.refs_4_
  57.0 5.0 %collective-permute-done.13.refs_2_ = bf16[1024,128]{1,0:T(8,128)(2,1)S(1)} collective-permute-done((bf16[1024,128]{1,0:T(8,128)(2,1)S(1)}, bf16[1024,128]{1,0:T(8,128)(2,1)S(1)}, u32[]{:S(2)}, u32[]{:S(2)}) %collective-permute-start.13) | collective-permute-done | bytes 262176 | tf_op jit(solution)/shard_map/ppermute | solution.py:442
  62.0 1.0 %combine_1_0_1.1.refs_5_ = bf16[1,2,2048,128]{3,2,1,0:T(8,128)(2,1)} custom-call(f32[3200,128]{1,0:T(8,128)S(1)} %get-tuple-element.55.refs_0_, bf16[1024,128]{1,0:T(8,128)(2,1)S(1)} %collective-permute-done.12.refs_1_, bf16[1024,128]{1,0:T(8,128)(2,1)S(1)} %collective-permute-done.13.refs_2_, bf16[1024,128]{1,0:T(8,128)(2,1)S(1)} %get-tuple-element.54.refs_3_, ...), custom_call_target="tpu_custom_call" | custom-call | flops 1000000 | bytes 1000000 | tf_op jit(solution)/shard_map/combine_1_0_1/pallas_call | solution.py:421
  63.0 3.2 %collective-permute-done.6.refs_2_ = bf16[1024,128]{1,0:T(8,128)(2,1)S(1)} collective-permute-done((bf16[1024,128]{1,0:T(8,128)(2,1)S(1)}, bf16[1024,128]{1,0:T(8,128)(2,1)S(1)}, u32[]{:S(2)}, u32[]{:S(2)}) %collective-permute-start.6) | collective-permute-done | bytes 262176 | tf_op jit(solution)/shard_map/ppermute | solution.py:442
  66.3 1.0 %combine_1_1_1.1 = bf16[1,2,2048,128]{3,2,1,0:T(8,128)(2,1)} custom-call(f32[3200,128]{1,0:T(8,128)S(1)} %get-tuple-element.46.refs_0_, bf16[1024,128]{1,0:T(8,128)(2,1)S(1)} %collective-permute-done.5.refs_1_, bf16[1024,128]{1,0:T(8,128)(2,1)S(1)} %collective-permute-done.6.refs_2_, ...), custom_call_target="tpu_custom_call", output_to_operand_aliasing={{}: (5, {})} | custom-call | flops 1000000 | bytes 1000000 | tf_op jit(solution)/shard_map/combine_1_1_1/pallas_call | solution.py:421
  (23 shorter events, 0.6 us)
Async XLA Ops:
  3.8 3.4 %collective-permute-start.1 = (bf16[2048,128]{1,0:T(8,128)(2,1)S(1)}, bf16[2048,128]{1,0:T(8,128)(2,1)S(1)}, u32[]{:S(2)}, u32[]{:S(2)}) collective-permute-start(bf16[2048,128]{1,0:T(8,128)(2,1)S(1)} %get-tuple-element.42), channel_id=1, source_target_pairs={{0,1},{1,0},{2,3},{3,2},{4,5},{5,4},{6,7},{7,6},{8,9},{9,8},{10,11... | collective-permute-start | bytes 1572872 | tf_op jit(solution)/shard_map/ppermute | solution.py:445
  4.6 26.5 %collective-permute-start = (bf16[2048,128]{1,0:T(8,128)(2,1)S(1)}, bf16[2048,128]{1,0:T(8,128)(2,1)S(1)}, u32[]{:S(2)}, u32[]{:S(2)}) collective-permute-start(bf16[2048,128]{1,0:T(8,128)(2,1)S(1)} %get-tuple-element.40), channel_id=1, source_target_pairs={{0,1},{1,0},{2,3},{3,2},{4,5},{5,4},{6,7},{7,6},{8,9},{9,8},{10,11... | collective-permute-start | bytes 1572872 | tf_op jit(solution)/shard_map/ppermute | solution.py:445
  4.7 2.5 %collective-permute-start.2 = (bf16[1024,128]{1,0:T(8,128)(2,1)S(1)}, bf16[1024,128]{1,0:T(8,128)(2,1)S(1)}, u32[]{:S(2)}, u32[]{:S(2)}) collective-permute-start(bf16[1024,128]{1,0:T(8,128)(2,1)S(1)} %get-tuple-element.43), channel_id=1, source_target_pairs={{0,15},{1,2},{2,1},{3,4},{4,3},{5,6},{6,5},{7,8},{8,7},{9,10},{10,... | collective-permute-start | bytes 786440 | tf_op jit(solution)/shard_map/ppermute | solution.py:442
  5.2 2.6 %collective-permute-start.14 = (bf16[1024,128]{1,0:T(8,128)(2,1)S(1)}, bf16[1024,128]{1,0:T(8,128)(2,1)S(1)}, u32[]{:S(2)}, u32[]{:S(2)}) collective-permute-start(bf16[1024,128]{1,0:T(8,128)(2,1)S(1)} %get-tuple-element.59), channel_id=1, source_target_pairs={{0,15},{1,2},{2,1},{3,4},{4,3},{5,6},{6,5},{7,8},{8,7},{9,10},{10,... | collective-permute-start | bytes 786440 | tf_op jit(solution)/shard_map/ppermute | solution.py:442
  5.3 25.8 %collective-permute-start.7 = (bf16[1024,128]{1,0:T(8,128)(2,1)S(1)}, bf16[1024,128]{1,0:T(8,128)(2,1)S(1)}, u32[]{:S(2)}, u32[]{:S(2)}) collective-permute-start(bf16[1024,128]{1,0:T(8,128)(2,1)S(1)} %get-tuple-element.50), channel_id=1, source_target_pairs={{0,15},{1,2},{2,1},{3,4},{4,3},{5,6},{6,5},{7,8},{8,7},{9,10},{10,... | collective-permute-start | bytes 786440 | tf_op jit(solution)/shard_map/ppermute | solution.py:442
  7.3 29.0 %collective-permute-start.3 = (bf16[1024,128]{1,0:T(8,128)(2,1)S(1)}, bf16[1024,128]{1,0:T(8,128)(2,1)S(1)}, u32[]{:S(2)}, u32[]{:S(2)}) collective-permute-start(bf16[1024,128]{1,0:T(8,128)(2,1)S(1)} %get-tuple-element.45), channel_id=1, source_target_pairs={{0,15},{1,2},{2,1},{3,4},{4,3},{5,6},{6,5},{7,8},{8,7},{9,10},{10,... | collective-permute-start | bytes 786440 | tf_op jit(solution)/shard_map/ppermute | solution.py:442
  7.9 30.1 %collective-permute-start.15 = (bf16[1024,128]{1,0:T(8,128)(2,1)S(1)}, bf16[1024,128]{1,0:T(8,128)(2,1)S(1)}, u32[]{:S(2)}, u32[]{:S(2)}) collective-permute-start(bf16[1024,128]{1,0:T(8,128)(2,1)S(1)} %combine_0_0_0.1.refs_3_), channel_id=1, source_target_pairs={{0,16},{16,0},{1,17},{17,1},{2,18},{18,2},{3,19},{19,3},{4,20},{20... | collective-permute-start | bytes 786440 | tf_op jit(solution)/shard_map/ppermute | solution.py:448
  31.2 12.1 %collective-permute-start.8 = (bf16[1024,128]{1,0:T(8,128)(2,1)S(1)}, bf16[1024,128]{1,0:T(8,128)(2,1)S(1)}, u32[]{:S(2)}, u32[]{:S(2)}) collective-permute-start(bf16[1024,128]{1,0:T(8,128)(2,1)S(1)} %combine_0_1_0.1.refs_3_), channel_id=1, source_target_pairs={{0,16},{16,0},{1,17},{17,1},{2,18},{18,2},{3,19},{19,3},{4,20},{20... | collective-permute-start | bytes 786440 | tf_op jit(solution)/shard_map/ppermute | solution.py:448
  36.3 10.9 %collective-permute-start.11 = (bf16[1024,128]{1,0:T(8,128)(2,1)S(1)}, bf16[1024,128]{1,0:T(8,128)(2,1)S(1)}, u32[]{:S(2)}, u32[]{:S(2)}) collective-permute-start(bf16[1024,128]{1,0:T(8,128)(2,1)S(1)} %get-tuple-element.54.refs_3_), channel_id=1, source_target_pairs={{0,16},{16,0},{1,17},{17,1},{2,18},{18,2},{3,19},{19,3},{4,20},{20... | collective-permute-start | bytes 786440 | tf_op jit(solution)/shard_map/ppermute | solution.py:448
  36.5 13.8 %collective-permute-start.4 = (bf16[1024,128]{1,0:T(8,128)(2,1)S(1)}, bf16[1024,128]{1,0:T(8,128)(2,1)S(1)}, u32[]{:S(2)}, u32[]{:S(2)}) collective-permute-start(bf16[1024,128]{1,0:T(8,128)(2,1)S(1)} %combine_0_1_1.1.refs_3_), channel_id=1, source_target_pairs={{0,16},{16,0},{1,17},{17,1},{2,18},{18,2},{3,19},{19,3},{4,20},{20... | collective-permute-start | bytes 786440 | tf_op jit(solution)/shard_map/ppermute | solution.py:448
  39.4 12.5 %collective-permute-start.16 = (bf16[1024,128]{1,0:T(8,128)(2,1)S(1)}, bf16[1024,128]{1,0:T(8,128)(2,1)S(1)}, u32[]{:S(2)}, u32[]{:S(2)}) collective-permute-start(bf16[1024,128]{1,0:T(8,128)(2,1)S(1)} %get-tuple-element.61), channel_id=1, source_target_pairs={{0,1},{1,0},{2,3},{3,2},{4,5},{5,4},{6,7},{7,6},{8,9},{9,8},{10,11... | collective-permute-start | bytes 786440 | tf_op jit(solution)/shard_map/ppermute | solution.py:445
  39.5 13.0 %collective-permute-start.17 = (bf16[1024,128]{1,0:T(8,128)(2,1)S(1)}, bf16[1024,128]{1,0:T(8,128)(2,1)S(1)}, u32[]{:S(2)}, u32[]{:S(2)}) collective-permute-start(bf16[1024,128]{1,0:T(8,128)(2,1)S(1)} %get-tuple-element.62), channel_id=1, source_target_pairs={{0,1},{1,0},{2,3},{3,2},{4,5},{5,4},{6,7},{7,6},{8,9},{9,8},{10,11... | collective-permute-start | bytes 786440 | tf_op jit(solution)/shard_map/ppermute | solution.py:442
  44.7 12.1 %collective-permute-start.10 = (bf16[1024,128]{1,0:T(8,128)(2,1)S(1)}, bf16[1024,128]{1,0:T(8,128)(2,1)S(1)}, u32[]{:S(2)}, u32[]{:S(2)}) collective-permute-start(bf16[1024,128]{1,0:T(8,128)(2,1)S(1)} %get-tuple-element.53), channel_id=1, source_target_pairs={{0,1},{1,0},{2,3},{3,2},{4,5},{5,4},{6,7},{7,6},{8,9},{9,8},{10,11... | collective-permute-start | bytes 786440 | tf_op jit(solution)/shard_map/ppermute | solution.py:442
  48.7 8.3 %collective-permute-start.12 = (bf16[1024,128]{1,0:T(8,128)(2,1)S(1)}, bf16[1024,128]{1,0:T(8,128)(2,1)S(1)}, u32[]{:S(2)}, u32[]{:S(2)}) collective-permute-start(bf16[1024,128]{1,0:T(8,128)(2,1)S(1)} %get-tuple-element.56), channel_id=1, source_target_pairs={{0,1},{1,0},{2,3},{3,2},{4,5},{5,4},{6,7},{7,6},{8,9},{9,8},{10,11... | collective-permute-start | bytes 786440 | tf_op jit(solution)/shard_map/ppermute | solution.py:445
  50.3 6.6 %collective-permute-start.9 = (bf16[1024,128]{1,0:T(8,128)(2,1)S(1)}, bf16[1024,128]{1,0:T(8,128)(2,1)S(1)}, u32[]{:S(2)}, u32[]{:S(2)}) collective-permute-start(bf16[1024,128]{1,0:T(8,128)(2,1)S(1)} %get-tuple-element.52), channel_id=1, source_target_pairs={{0,1},{1,0},{2,3},{3,2},{4,5},{5,4},{6,7},{7,6},{8,9},{9,8},{10,11... | collective-permute-start | bytes 786440 | tf_op jit(solution)/shard_map/ppermute | solution.py:445
  52.0 10.1 %collective-permute-start.13 = (bf16[1024,128]{1,0:T(8,128)(2,1)S(1)}, bf16[1024,128]{1,0:T(8,128)(2,1)S(1)}, u32[]{:S(2)}, u32[]{:S(2)}) collective-permute-start(bf16[1024,128]{1,0:T(8,128)(2,1)S(1)} %get-tuple-element.57), channel_id=1, source_target_pairs={{0,1},{1,0},{2,3},{3,2},{4,5},{5,4},{6,7},{7,6},{8,9},{9,8},{10,11... | collective-permute-start | bytes 786440 | tf_op jit(solution)/shard_map/ppermute | solution.py:442
  52.5 10.5 %collective-permute-start.5 = (bf16[1024,128]{1,0:T(8,128)(2,1)S(1)}, bf16[1024,128]{1,0:T(8,128)(2,1)S(1)}, u32[]{:S(2)}, u32[]{:S(2)}) collective-permute-start(bf16[1024,128]{1,0:T(8,128)(2,1)S(1)} %get-tuple-element.47), channel_id=1, source_target_pairs={{0,1},{1,0},{2,3},{3,2},{4,5},{5,4},{6,7},{7,6},{8,9},{9,8},{10,11... | collective-permute-start | bytes 786440 | tf_op jit(solution)/shard_map/ppermute | solution.py:445
  56.8 9.5 %collective-permute-start.6 = (bf16[1024,128]{1,0:T(8,128)(2,1)S(1)}, bf16[1024,128]{1,0:T(8,128)(2,1)S(1)}, u32[]{:S(2)}, u32[]{:S(2)}) collective-permute-start(bf16[1024,128]{1,0:T(8,128)(2,1)S(1)} %get-tuple-element.48), channel_id=1, source_target_pairs={{0,1},{1,0},{2,3},{3,2},{4,5},{5,4},{6,7},{7,6},{8,9},{9,8},{10,11... | collective-permute-start | bytes 786440 | tf_op jit(solution)/shard_map/ppermute | solution.py:442
